TPU v7x, 32 devices: a whole 2x2x4 slice. The times are simulated.
32 devices in a mesh: rep: 1, seq: 16 (over z, y, core), head: 2 (over x).
Axes of the slice: x: 2, y: 2, z: 4, core: 2. Of those that a mesh axis runs over, the one named last changes fastest.
Arguments:
- states: bfloat16 [256, 8192], P('rep', 'seq'), may hold values from -6 to 6
- w_query: bfloat16 [8192, 8192], P('seq', 'head'), may hold values from -0.0625 to 0.0625
- w_key: bfloat16 [8192, 1024], P('seq', 'head'), may hold values from -0.3125 to 0.3125
- w_value: bfloat16 [8192, 1024], P('seq', 'head'), may hold values from -0.25 to 0.25
- w_out: bfloat16 [8192, 8192], P('head', 'seq'), may hold values from -0.09375 to 0.09375
- key_cache: bfloat16 [2, 8192, 1024], P('rep', 'seq', 'head'), may hold values from -480 to 480
- value_cache: bfloat16 [2, 8192, 1024], P('rep', 'seq', 'head'), may hold values from -24 to 24
- parents: int32 [2, 128], P('rep'), may hold values from 0 to 126, as said below
- cache_lengths: int32 [2], P('rep'), may hold values from 2048 to 8192, as said below
Outputs:
- attended: bfloat16 [256, 8192], P('rep', ('seq', 'head'))
Inputs may be any that keep to these rules, and one draw needn't show every extreme that they name: parents[t, 0] = 0, parents[t, i] < i for i >= 1, and the last node's parent is node 126. `cache_lengths`: at least one sequence fills all 8192 positions.
All inputs are finite; a program needn't handle non-finite values.
Results may differ from a plain program's by a relative error of at most 0.014.
The roundings to bfloat16 on the way count: a program that leaves them out, or rounds other values in their place, can miss the bound.
Values may be sent and summed in bfloat16 or wider, within the bound.
No kernel may reach another device: no remote copies, remote signals or barrier semaphores. Data moves between devices by JAX's collectives and lax.ppermute only.
A program may use at most 320 MiB of HBM per device.

v0:
```python
import jax
import jax.numpy as jnp
from jax import lax
from jax.sharding import PartitionSpec as P

HEAD_DIM = 128


rope_base = 500000.0
neg_big = -1e30


def ancestry(parents):
    count = parents.shape[1]
    ident = jnp.eye(count, dtype=jnp.float32)
    onehot = (parents[:, :, None] == jnp.arange(count, dtype=jnp.int32)[None, None, :]).astype(
        jnp.float32
    )
    reach = jnp.minimum(ident[None] + onehot, 1.0)
    for level in range(max(1, (count - 1).bit_length())):
        reach = jnp.minimum(
            jnp.einsum("tij,tjk->tik", reach, reach, precision=lax.Precision.HIGHEST), 1.0
        )
    return reach


def rotate(values, position):
    count = values.shape[0]
    half = HEAD_DIM // 2
    shaped = values.reshape(count, -1, HEAD_DIM)
    freq = rope_base ** (-(jnp.arange(half, dtype=jnp.float32) * 2.0 / HEAD_DIM))
    angle = position[:, None] * freq[None, :]
    cosine = jnp.cos(angle)[:, None, :]
    sine = jnp.sin(angle)[:, None, :]
    first = shaped[..., :half]
    second = shaped[..., half:]
    turned = jnp.concatenate([first * cosine - second * sine, second * cosine + first * sine], -1)
    return turned.reshape(count, -1)


def combine(left, right):
    top = jnp.maximum(left[0], right[0])
    scale_left = jnp.exp(left[0] - top)
    scale_right = jnp.exp(right[0] - top)
    return (
        top,
        left[1] * scale_left + right[1] * scale_right,
        left[2] * scale_left[..., None] + right[2] * scale_right[..., None],
    )


def cache_state(query, keys, values, length, offset):
    total = keys.shape[0]
    block = min(total, 2048)
    count = total // block
    rows_here, kv_local, group, width = query.shape
    scale = width ** (-0.5)
    keys = keys.reshape(count, block, kv_local, width)
    values = values.reshape(count, block, kv_local, width)

    def step(carry, inputs):
        key_block, value_block, first = inputs
        valid = offset + first + jnp.arange(block, dtype=jnp.int32) < length
        scores = (
            jnp.einsum("rkgd,nkd->rkgn", query, key_block, preferred_element_type=jnp.float32)
            * scale
        )
        scores = jnp.where(valid, scores, neg_big)
        top = jnp.maximum(carry[0], jnp.max(scores, -1))
        weights = jnp.where(valid, jnp.exp(scores - top[..., None]), 0.0)
        shrink = jnp.exp(carry[0] - top)
        mass = carry[1] * shrink + jnp.sum(weights, -1)
        acc = carry[2] * shrink[..., None] + jnp.einsum(
            "rkgn,nkd->rkgd",
            weights.astype(jnp.bfloat16),
            value_block,
            preferred_element_type=jnp.float32,
        )
        return ((top, mass, acc), None)

    init = (
        jnp.full((rows_here, kv_local, group), neg_big, jnp.float32),
        jnp.zeros((rows_here, kv_local, group), jnp.float32),
        jnp.zeros((rows_here, kv_local, group, width), jnp.float32),
    )
    firsts = jnp.arange(count, dtype=jnp.int32) * block
    state, _ = lax.scan(step, init, (keys, values, firsts))
    return state


def tree_state(query, new_keys, new_values, allowed):
    rows_here, kv_local, group, width = query.shape
    scale = width ** (-0.5)
    keys = new_keys.reshape(-1, kv_local, width)
    values = new_values.reshape(-1, kv_local, width)
    mask = allowed[:, None, None, :]
    scores = jnp.einsum("rkgd,nkd->rkgn", query, keys, preferred_element_type=jnp.float32) * scale
    scores = jnp.where(mask, scores, neg_big)
    top = jnp.max(scores, -1)
    weights = jnp.where(mask, jnp.exp(scores - top[..., None]), 0.0)
    acc = jnp.einsum(
        "rkgn,nkd->rkgd", weights.astype(jnp.bfloat16), values, preferred_element_type=jnp.float32
    )
    return (top, jnp.sum(weights, -1), acc)


def local(states, w_query, w_key, w_value, w_out, key_cache, value_cache, parents, cache_lengths):
    trees, tree_rows = parents.shape
    rows = trees * tree_rows
    kv_local = key_cache.shape[2] // HEAD_DIM
    heads_local = w_query.shape[1] // HEAD_DIM
    group = heads_local // kv_local
    reach = ancestry(parents)
    position = (cache_lengths.astype(jnp.float32)[:, None] + jnp.sum(reach, -1) - 1.0).reshape(-1)
    allowed = (jnp.eye(trees, dtype=jnp.float32)[:, None, :, None] * reach[:, :, None, :]).reshape(
        rows, rows
    ) > 0.5
    q_part = jnp.dot(states, w_query, preferred_element_type=jnp.float32)
    k_part = jnp.dot(states, w_key, preferred_element_type=jnp.float32)
    v_part = jnp.dot(states, w_value, preferred_element_type=jnp.float32)
    q_raw, k_raw, v_raw = lax.psum((q_part, k_part, v_part), "seq")
    queries = rotate(q_raw, position).astype(jnp.bfloat16)
    new_keys = rotate(k_raw, position).astype(jnp.bfloat16)
    new_values = v_raw.astype(jnp.bfloat16)
    query_heads = queries.reshape(rows, kv_local, group, HEAD_DIM)
    offset = lax.axis_index("seq") * key_cache.shape[1]
    parts_list = []
    for tree in range(trees):
        parts_list.append(
            cache_state(
                query_heads[tree * tree_rows : (tree + 1) * tree_rows],
                key_cache[tree],
                value_cache[tree],
                cache_lengths[tree],
                offset,
            )
        )
    peak = jnp.concatenate([item[0] for item in parts_list], 0)
    mass = jnp.concatenate([item[1] for item in parts_list], 0)
    acc = jnp.concatenate([item[2] for item in parts_list], 0)
    summit = lax.pmax(peak, "seq")
    factor = jnp.exp(peak - summit)
    mass_share, acc_share = (
        lax.psum_scatter(mass * factor, "seq", scatter_dimension=0, tiled=True),
        lax.psum_scatter(acc * factor[..., None], "seq", scatter_dimension=0, tiled=True),
    )
    share = mass_share.shape[0]
    first_row = lax.axis_index("seq") * share
    summit_share = lax.dynamic_slice_in_dim(summit, first_row, share)
    query_share = lax.dynamic_slice_in_dim(query_heads, first_row, share)
    allowed_share = lax.dynamic_slice_in_dim(allowed, first_row, share)
    total = combine(
        (summit_share, mass_share, acc_share),
        tree_state(query_share, new_keys, new_values, allowed_share),
    )
    attention_share = (total[2] / total[1][..., None]).reshape(share, -1).astype(jnp.bfloat16)
    attention = lax.all_gather(attention_share, "seq", axis=0, tiled=True)
    partial_value = jnp.dot(attention, w_out, preferred_element_type=jnp.float32)
    return lax.psum_scatter(partial_value, "head", scatter_dimension=1, tiled=True).astype(
        jnp.bfloat16
    )


def solution(mesh):
    placed = (
        P("rep", "seq"),
        P("seq", "head"),
        P("seq", "head"),
        P("seq", "head"),
        P("head", "seq"),
        P("rep", "seq", "head"),
        P("rep", "seq", "head"),
        P("rep", None),
        P("rep"),
    )
    return jax.shard_map(
        local, mesh=mesh, in_specs=placed, out_specs=P("rep", ("seq", "head")), check_vma=False
    )
```

profile of v0, /device:TPU:0, one launch (start us, length us, event | category | flops | bytes accessed | tf_op | source)
XLA Modules:
  0.0 412.9 jit_solution(16273453118756324011)
XLA Ops:
  6.5 1.0 copy-done
  7.6 1.2 convolution_bitcast_fusion.1
  8.8 0.9 copy.84
  9.7 3.5 convolution_bitcast_fusion
  13.2 2.7 copy.76
  16.0 1.1 copy-done.6
  18.0 1.0 copy.74
  19.2 1.0 copy.72
  20.4 1.8 fusion.47
  25.0 110.8 %all-reduce.4.cloned.1.call-done = (f32[256,4,128]{2,0,1:T(8,128)}, f32[256,32,128]{2,1,0:T(8,128)}) async-done(((f32[256,4,128]{2,0,1:T(8,128)}, f32[256,32,128]{2,1,0:T(8,128)}), (f32[256,4,128]{2,0,1:T(8,128)}, f32[256,32,128]{2,1,0:T(8,128)})) %all-reduce.4.cloned.1.call-update) | async-done | bytes 4718608 | tf_op jit(solution)/shard_map/psum | solution.py:121
  135.7 4.8 %multiply_subtract_fusion = (bf16[256,32,64]{2,1,0:T(8,128)(2,1)S(1)}, bf16[256,32,64]{2,1,0:T(8,128)(2,1)S(1)}) fusion(f32[256,32,128]{2,1,0:T(8,128)} %get-tuple-element.40, f32[256,64]{1,0:T(8,128)S(1)} %get-tuple-element.81, f32[256,64]{1,0:T(8,128)S(1)} %get-tuple-element.80), kind=kLoop, calls=%fused_computation.17 | loop fusion | flops 4194304 | bytes 6422528 | tf_op jit(solution)/shard_map/sub | solution.py:37
  140.6 1.2 maximum_convert_fusion
  142.5 1.3 bitcast_reduce_fusion
  143.9 3.1 fusion.6
  148.1 1.3 bitcast_reduce_fusion.1
  149.5 2.4 fusion.4
  151.9 0.8 copy-done.3
  153.3 60.0 %pmax.7 = f32[256,4,8]{0,2,1:T(8,128)S(1)} all-reduce(f32[256,4,8]{0,2,1:T(8,128)S(1)} %pad_maximum_fusion), channel_id=1, replica_groups=mesh['rep'=1,'seq'=16,'head'=2] {'seq'}, use_global_device_ids=true, to_apply=%region_4.5 | all-reduce | flops 8192 | bytes 65536 | tf_op jit(solution)/shard_map/pmax | solution.py:141
  215.0 5.7 %bitcast_add_fusion = f32[128,4,8,128]{3,0,2,1:T(8,128)S(1)} fusion(bf16[512,4,128,1]{0,2,3,1:T(8,128)(2,1)S(1)} %bitcast.140, f32[4,128,8,512]{3,1,2,0:T(8,128)} %copy-done.2, f32[128,4,8]{0,2,1:T(8,128)S(1)} %broadcast_maximum_fusion, pred[512]{0:T(512)(128)(4,1)} %copy-done.19, f32[128,4,8]{0,2,1:T(8,128)} %get-tuple-element.79), kind=kOutput, calls=%fused_computation.25 | convolution fusion | flops 547880960 | bytes 11043328 | tf_op jit(solution)/shard_map/while/body/eval_jaxpr/rkgn,nkd->rkgd/dot_general | solution.py:73
  220.7 5.5 %bitcast_add_fusion.1 = f32[128,4,8,128]{3,0,2,1:T(8,128)S(1)} fusion(bf16[512,4,128,1]{0,2,3,1:T(8,128)(2,1)S(1)} %bitcast.139, f32[4,128,8,512]{3,1,2,0:T(8,128)} %copy-done.3, f32[128,4,8]{0,2,1:T(8,128)S(1)} %copy-done.11, pred[512]{0:T(512)(128)(4,1)S(1)} %copy-done.18, f32[128,4,8]{0,2,1:T(8,128)S(1)} %copy-done.16), kind=kOutput, calls=%fused_computation.26 | convolution fusion | flops 547880960 | bytes 11043328 | tf_op jit(solution)/shard_map/while/body/eval_jaxpr/rkgn,nkd->rkgd/dot_general | solution.py:73
  226.2 2.6 maximum_multiply_fusion
  229.8 2.1 fusion.69
  231.9 63.7 %all-reduce.5 = bf16[256,512]{1,0:T(8,128)(2,1)S(1)} all-reduce(f32[256,512]{1,0:T(8,128)} %fusion.69), channel_id=1, replica_groups=mesh['rep'=1,'seq'=16,'head'=2] {'seq'}, use_global_device_ids=true, to_apply=%region_8.9 | all-reduce | flops 131072 | bytes 786432 | tf_op jit(solution)/shard_map/psum | solution.py:121
  295.6 0.8 reshape.143
  296.4 0.8 copy.46
  298.2 0.8 copy.70
  299.1 44.5 %reduce-scatter.6.cloned.1.call-done = f32[16,4,8,128]{3,0,2,1:T(8,128)} async-done(((f32[256,4,8,128]{3,0,2,1:T(8,128)}), f32[16,4,8,128]{3,0,2,1:T(8,128)}) %reduce-scatter.6.cloned.1.call-update) | async-done | bytes 262160 | tf_op jit(solution)/shard_map/reduce_scatter | solution.py:145
  343.5 1.4 fusion.25
  345.7 40.6 %all-gather.2.cloned.1.call-done = bf16[256,4096]{1,0:T(8,128)(2,1)} async-done(((bf16[16,4096]{1,0:T(8,128)(2,1)}), bf16[256,4096]{1,0:T(8,128)(2,1)}) %all-gather.2.cloned.1.call-update) | async-done | bytes 2097168 | tf_op jit(solution)/shard_map/all_gather | solution.py:157
  386.4 4.9 %fusion.70 = f32[256,512]{1,0:T(8,128)} fusion(bf16[256,4096]{1,0:T(8,128)(2,1)} %all-gather.2.cloned.1.call-done, bf16[4096,512]{1,0:T(8,128)(2,1)} %param.13), kind=kOutput, calls=%fused_computation.111 | convolution fusion | flops 1073741824 | bytes 6815744 | tf_op jit(solution)/shard_map/dot_general | solution.py:158
  391.3 13.5 %reduce-scatter.8.cloned.1.call-done = f32[256,256]{1,0:T(8,128)} async-done(((f32[256,512]{1,0:T(8,128)}), f32[256,256]{1,0:T(8,128)}) %reduce-scatter.8.cloned.1.call-update) | async-done | bytes 262160 | tf_op jit(solution)/shard_map/reduce_scatter | solution.py:159
  404.8 1.6 convert_element_type.65
  (89 shorter events, 10.9 us)
Async XLA Ops:
  6.5 1.0 copy-start
  6.5 129.2 %all-reduce.4.cloned.1.call-start = ((), (), s32[]{:S(2)}) async-start(), calls=%async_computation.7 | async-start | bytes 9437184 | tf_op jit(solution)/shard_map/psum | solution.py:121
  16.0 1.2 copy-start.6
  16.0 1.3 copy-start.20
  16.0 1.9 copy-start.7
  16.0 6.2 %copy-start.21 = (s32[2,128]{1,0:T(2,128)S(1)}, s32[2,128]{1,0:T(2,128)}, u32[]{:S(2)}) copy-start(s32[2,128]{1,0:T(2,128)} %param.16) | copy-start | bytes 3076
  16.0 282.2 %reduce-scatter.10.cloned.1.call-start = ((), (), s32[]{:S(2)}) async-start(), calls=%async_computation.6 | async-start | bytes 139264
  22.2 120.3 %copy-start.19 = (pred[512]{0:T(512)(128)(4,1)}, pred[512]{0:T(512)(128)(4,1)S(1)}, u32[]{:S(2)}) copy-start(pred[512]{0:T(512)(128)(4,1)S(1)} %get-tuple-element.92) | copy-start | bytes 1540
  143.9 3.2 copy-start.2
  143.9 4.3 %copy-start.17 = (pred[512]{0:T(512)(128)(4,1)S(1)}, pred[512]{0:T(512)(128)(4,1)}, u32[]{:S(2)}) copy-start(pred[512]{0:T(512)(128)(4,1)} %get-tuple-element.93) | copy-start | bytes 1540
  149.5 3.2 copy-start.3
  149.5 63.8 %copy-start.10 = (f32[128,4,8]{0,2,1:T(8,128)}, f32[128,4,8]{0,2,1:T(8,128)S(1)}, u32[]{:S(2)}) copy-start(f32[128,4,8]{0,2,1:T(8,128)S(1)} %broadcast_maximum_fusion.1) | copy-start | bytes 49156
  149.5 63.8 %copy-start.15 = (f32[128,4,8]{0,2,1:T(8,128)S(1)}, f32[128,4,8]{0,2,1:T(8,128)}, u32[]{:S(2)}) copy-start(f32[128,4,8]{0,2,1:T(8,128)} %get-tuple-element.78) | copy-start | bytes 49156
  149.5 65.4 %copy-start.9 = (bf16[1,512,512]{1,2,0:T(8,128)(2,1)S(1)}, bf16[1,512,512]{1,2,0:T(8,128)(2,1)}, u32[]{:S(2)}) copy-start(bf16[1,512,512]{1,2,0:T(8,128)(2,1)} %copy.74) | copy-start | bytes 1572868
  213.3 1.6 copy-start.12
  214.7 128.8 %reduce-scatter.6.cloned.1.call-start = ((), (), s32[]{:S(2)}) async-start(), calls=%async_computation.3 | async-start | bytes 4456448 | tf_op jit(solution)/shard_map/reduce_scatter | solution.py:145
  214.9 5.7 %copy-start.8 = (bf16[1,512,512]{1,2,0:T(8,128)(2,1)S(1)}, bf16[1,512,512]{1,2,0:T(8,128)(2,1)}, u32[]{:S(2)}) copy-start(bf16[1,512,512]{1,2,0:T(8,128)(2,1)} %copy.72) | copy-start | bytes 1572868
  215.0 5.7 %copy-start.11 = (f32[128,4,8]{0,2,1:T(8,128)S(1)}, f32[128,4,8]{0,2,1:T(8,128)}, u32[]{:S(2)}) copy-start(f32[128,4,8]{0,2,1:T(8,128)} %copy-done.10) | copy-start | bytes 49156
  215.0 5.7 %copy-start.16 = (f32[128,4,8]{0,2,1:T(8,128)S(1)}, f32[128,4,8]{0,2,1:T(8,128)}, u32[]{:S(2)}) copy-start(f32[128,4,8]{0,2,1:T(8,128)} %get-tuple-element.77) | copy-start | bytes 49156
  215.0 5.7 %copy-start.18 = (pred[512]{0:T(512)(128)(4,1)S(1)}, pred[512]{0:T(512)(128)(4,1)}, u32[]{:S(2)}) copy-start(pred[512]{0:T(512)(128)(4,1)} %get-tuple-element.93) | copy-start | bytes 1540
  220.7 5.5 %copy-start.14 = (f32[256,4,8]{0,2,1:T(8,128)S(1)}, f32[256,4,8]{0,2,1:T(8,128)}, u32[]{:S(2)}) copy-start(f32[256,4,8]{0,2,1:T(8,128)} %get-tuple-element.54) | copy-start | bytes 98308
  228.8 1.0 copy-start.4
  228.8 68.4 %copy-start.5 = (f32[256,4,128]{2,0,1:T(8,128)S(1)}, f32[256,4,128]{2,0,1:T(8,128)}, u32[]{:S(2)}) copy-start(f32[256,4,128]{2,0,1:T(8,128)} %get-tuple-element.39) | copy-start | bytes 1572868
  228.8 157.5 %all-gather.2.cloned.1.call-start = ((), (), s32[]{:S(2)}) async-start(), calls=%async_computation.4 | async-start | bytes 2228224 | tf_op jit(solution)/shard_map/all_gather | solution.py:157
  295.6 3.3 copy-start.13
  345.7 60.7 %copy-start.1 = (bf16[512,512]{1,0:T(8,128)(2,1)S(1)}, bf16[512,512]{1,0:T(8,128)(2,1)}, u32[]{:S(2)}) copy-start(bf16[512,512]{1,0:T(8,128)(2,1)} %param.11) | copy-start | bytes 1572868
  345.7 59.1 %reduce-scatter.8.cloned.1.call-start = ((), (), s32[]{:S(2)}) async-start(), calls=%async_computation.5 | async-start | bytes 786432 | tf_op jit(solution)/shard_map/reduce_scatter | solution.py:159
Sparse Core Ops, SparseCore 0:
  16.1 119.5 all-reduce.3
  214.8 52.9 reduce-scatter.9
  271.7 71.8 reduce-scatter.5
  345.8 40.5 all-gather.1
  391.4 13.3 reduce-scatter.7
where the time goes:
time: 414 us; the launch traced here: 413 us
  waiting for transfers between devices  209 us (50%)
  blocking collectives  124 us (30%)
  matrix products  29.4 us (7%)
  other arithmetic  20.9 us (5%)
  local copies, waits for them, and re-layouts  15.5 us (4%)
  between operations  13.6 us (3%)
    psum x1, waiting for transfers between devices, local(): q_raw, k_raw, v_raw = lax.psum((q_part, k_part, v_part), 'seq')  111 us
    psum x1, blocking collectives, local(): q_raw, k_raw, v_raw = lax.psum((q_part, k_part, v_part), 'seq')  63.7 us
    pmax x1, blocking collectives, local(): summit = lax.pmax(peak, 'seq')  60 us
    reduce_scatter x1, waiting for transfers between devices, local(): lax.psum_scatter(acc * factor[..., None], 'seq', scatter_dimension=0, til...  44.5 us
    all_gather x1, waiting for transfers between devices, local(): attention = lax.all_gather(attention_share, 'seq', axis=0, tiled=True)  40.6 us
    reduce_scatter x1, waiting for transfers between devices, local(): lax.psum_scatter(partial_value, 'head', scatter_dimension=1, tiled=True)  13.5 us
    unnamed x53, local copies, waits for them, and re-layouts  11.1 us
    dot_general x2, matrix products, step(): jnp.einsum('rkgn,nkd->rkgd', weights.astype(jnp.bfloat16), value_block, p...  11.1 us
  transfers between devices with their start and end apart: 5, of which 4 were waited for; matrix products, arithmetic and copies ran while one was open for 7% of the time, Pallas kernels for 0%

commit v1 on v0

v1 whole, which is shorter than its diff:
```python
import functools

import jax
import jax.numpy as jnp
from jax import lax
from jax.experimental import pallas as pl
from jax.experimental.pallas import tpu as pltpu
from jax.sharding import PartitionSpec as P


HEAD_DIM = 128
rope_base = 500000.0
neg_big = -1e30
log2_e = 1.4426950408889634

VMEM = pl.BlockSpec(memory_space=pltpu.VMEM)
SMEM = pl.BlockSpec(memory_space=pltpu.SMEM)


def room(mib):
    return pltpu.CompilerParams(vmem_limit_bytes=mib * 1024 * 1024)


def bits_of(count):
    return max(0, (count - 1).bit_length())


def reverse_bits(value, width):
    out = 0
    for bit in range(width):
        out = out | (((value >> bit) & 1) << (width - 1 - bit))
    return out


def swap(value, mask, size):
    return lax.ppermute(value, "seq", [(i, i ^ mask) for i in range(size)])


def dot_t(left, right):
    return lax.dot_general(left, right, (((1,), (1,)), ((), ())), preferred_element_type=jnp.float32)


def place_of(splits, trees):
    me = lax.axis_index("seq").astype(jnp.int32)
    split_bits = bits_of(splits)
    return me & (splits - 1), (me >> split_bits) & (trees - 1), me >> (split_bits + bits_of(trees))


def pack_kernel(splits, trees, key_ref, value_ref, *outs):
    _, tree, head = place_of(splits, trees)
    for unit, out in enumerate(outs):
        source = (unit & (trees - 1)) ^ tree
        lanes = pl.ds(pl.multiple_of(((unit >> bits_of(trees)) ^ head) * HEAD_DIM, HEAD_DIM), HEAD_DIM)
        out[0] = key_ref[source, :, lanes]
        out[1] = value_ref[source, :, lanes]


def project_kernel(splits, trees, states, wq, wk, wv, keep, low_send, high_send):
    my_part, my_tree, my_head = place_of(splits, trees)
    heads, share = keep.shape[1:3]
    width = bits_of(splits)
    rows = []
    for part in range(splits):
        for tree in range(trees):
            row = ((tree ^ my_tree) * splits + (reverse_bits(part, width) ^ my_part)) * share
            rows.append(states[pl.ds(pl.multiple_of(row, share), share), :])
    left = jnp.concatenate(rows, 0)
    for head in range(heads):
        source = reverse_bits(head, bits_of(heads)) ^ my_head
        low = 0
        for weight in (wq, wk, wv):
            size = weight.shape[1] // heads
            lanes = pl.ds(pl.multiple_of(source * size, size), size)
            out = jnp.dot(left, weight[:, lanes], preferred_element_type=jnp.float32)
            row = 0
            for target in (keep, low_send, high_send):
                count = target.shape[0]
                piece = out[row : row + count * share].reshape(count, share, size)
                target[:, head, :, low : low + size] = piece
                row += count * share
            low += size


def lane_blocks(value):
    return [value[:, low : low + HEAD_DIM] for low in range(0, value.shape[1], HEAD_DIM)]


def scores_of(query, keys, scores, meta, offset, top):
    span = keys.shape[1]
    length = meta[4]

    def body(i, top):
        piece = dot_t(query[...], keys[i])
        place = meta[offset + i] + lax.broadcasted_iota(jnp.int32, (1, span), 1)
        piece = piece + jnp.where(place < length, 0.0, neg_big)
        scores[i] = piece
        return functools.reduce(jnp.maximum, lane_blocks(piece), top)

    return lax.fori_loop(0, keys.shape[0], body, top)


def weigh(scores, values, top, mass, acc):
    rate = HEAD_DIM**-0.5 * log2_e

    def body(i, _):
        weight = jnp.exp2((scores[i] - top) * rate)
        mass[...] += functools.reduce(jnp.add, lane_blocks(weight))
        acc[...] += jnp.dot(weight.astype(jnp.bfloat16), values[i], preferred_element_type=jnp.float32)
        return 0

    lax.fori_loop(0, values.shape[0], body, 0)


def cache_kernel(count, group, offset, meta, raw, cosine, sine, *refs):
    chunks = refs[:count]
    query, top_out, mass, acc, keys, values, scores = refs[count:]
    share = raw.shape[0]
    for head in range(group):
        value = raw[:, head * HEAD_DIM : (head + 1) * HEAD_DIM]
        value = value * cosine[...] + pltpu.roll(value, HEAD_DIM // 2, 1) * sine[...]
        query[head * share : (head + 1) * share, :] = value.astype(query.dtype)
    for i, chunk in enumerate(chunks):
        keys[i] = chunk[0]
        values[i] = chunk[1]
    top = jnp.full(top_out.shape, neg_big, jnp.float32)
    top = scores_of(query, keys, scores, meta, offset, top)
    top = jnp.max(top, 1, keepdims=True)
    mass[...] = jnp.zeros(mass.shape, jnp.float32)
    acc[...] = jnp.zeros(acc.shape, jnp.float32)
    weigh(scores, values, top, mass, acc)
    top_out[...] = jnp.broadcast_to(top, top_out.shape)


def last_kernel(count, pieces, group, offset, meta, query, *refs):
    chunks = refs[:count]
    fresh = refs[count : count + pieces]
    bias, top_in, mass_in, acc_in, out, keys, values, scores, nodes, mass, acc = refs[count + pieces :]
    rate = HEAD_DIM**-0.5 * log2_e
    rows = query.shape[0]
    share = rows // group
    for i, chunk in enumerate(chunks):
        keys[i] = chunk[0]
        values[i] = chunk[1]
    for i, piece in enumerate(fresh):
        place = pl.ds(pl.multiple_of((meta[0] ^ i) * share, share), share)
        nodes[0, place, :] = piece[0]
        nodes[1, place, :] = piece[1]
    tree = dot_t(query[...], nodes[0])
    tree = (tree.reshape(group, share, -1) + bias[...][None]).reshape(rows, -1)
    top = functools.reduce(jnp.maximum, lane_blocks(tree), top_in[...])
    top = scores_of(query, keys, scores, meta, offset, top)
    top = jnp.max(top, 1, keepdims=True)
    shrink = jnp.exp2((top_in[...] - top) * rate)
    weight = jnp.exp2((tree - top) * rate)
    mass[...] = mass_in[...] * shrink + functools.reduce(jnp.add, lane_blocks(weight))
    acc[...] = acc_in[...] * shrink + jnp.dot(
        weight.astype(jnp.bfloat16), nodes[1], preferred_element_type=jnp.float32
    )
    weigh(scores, values, top, mass, acc)
    total = jnp.sum(mass[...], 1, keepdims=True)
    result = (acc[...] / total).astype(out.dtype)
    for head in range(group):
        out[:, head * HEAD_DIM : (head + 1) * HEAD_DIM] = result[head * share : (head + 1) * share]


def out_kernel(splits, trees, heads, step, meta, *refs):
    blocks = refs[: splits * trees * heads]
    weight, out = refs[splits * trees * heads :]
    share, depth = blocks[0].shape
    width = out.shape[1]
    if weight.shape[1] == width:
        column = slice(None)
    else:
        column = pl.ds(pl.multiple_of((meta[3] ^ step) * width, width), width)
    total = None
    for head in range(heads):
        left = jnp.concatenate(
            [blocks[(head * trees + tree) * splits + part][...] for tree in range(trees) for part in range(splits)], 0
        )
        deep = pl.ds(pl.multiple_of((head ^ meta[2]) * depth, depth), depth)
        term = jnp.dot(left, weight[deep, column], preferred_element_type=jnp.float32)
        total = term if total is None else total + term
    for tree in range(trees):
        for part in range(splits):
            row = ((tree ^ meta[1]) * splits + (part ^ meta[0])) * share
            low = (tree * splits + part) * share
            out[pl.ds(pl.multiple_of(row, share), share), :] = total[low : low + share].astype(out.dtype)


def reach_of(parent):
    count = parent.shape[0]
    spots = jnp.arange(count, dtype=jnp.int32)
    reach = ((parent[:, None] == spots[None, :]) | (spots[:, None] == spots[None, :])).astype(jnp.bfloat16)
    for _ in range(max(1, (count - 1).bit_length())):
        reach = jnp.minimum(jnp.dot(reach, reach, preferred_element_type=jnp.float32), 1.0).astype(jnp.bfloat16)
    return reach.astype(jnp.float32)


def local(size, sides, states, w_query, w_key, w_value, w_out, key_cache, value_cache, parents, cache_lengths):
    trees, tree_rows = parents.shape
    rows = trees * tree_rows
    span = key_cache.shape[1]
    heads = key_cache.shape[2] // HEAD_DIM
    group = w_query.shape[1] // HEAD_DIM // heads
    units = trees * heads
    splits = size // units
    share = tree_rows // splits
    split_bits, tree_bits = bits_of(splits), bits_of(trees)
    width = (group + 2) * HEAD_DIM
    f32, bf16 = jnp.float32, jnp.bfloat16
    shape = jax.ShapeDtypeStruct

    me = lax.axis_index("seq").astype(jnp.int32)
    side = lax.axis_index("head").astype(jnp.int32)
    my_part = me & (splits - 1)
    my_tree = (me >> split_bits) & (trees - 1)
    my_head = me >> (split_bits + tree_bits)

    order = sorted(
        range(1, units), key=lambda u: (-(u & (trees - 1)), -bits_of((u >> tree_bits) + 1), u)
    )
    masks = [unit * splits + part for unit in [0] + order for part in range(splits)]
    length = lax.dynamic_index_in_dim(cache_lengths, my_tree, 0, False)
    meta = jnp.stack(
        [my_part, my_tree, my_head, side, length, me] + [(me ^ mask) * span for mask in masks]
    )
    near = len(masks) // 2

    packed = pl.pallas_call(
        functools.partial(pack_kernel, splits, trees),
        out_shape=[shape((2, span, HEAD_DIM), bf16)] * units,
        in_specs=[VMEM, VMEM],
        out_specs=[VMEM] * units,
        name="pack",
    )(key_cache, value_cache)
    held = {0: packed[0]}
    for unit in order:
        held[unit] = swap(packed[unit], unit * splits, size)

    groups = splits * trees
    project = pl.pallas_call(
        functools.partial(project_kernel, splits, trees),
        out_shape=[shape((part, heads, share, width), f32) for part in (groups // 2, groups // 4, groups // 4)],
        in_specs=[VMEM] * 4,
        out_specs=[VMEM] * 3,
        name="project",
        compiler_params=room(12),
    )
    keep, low_send, high_send = project(states, w_query, w_key, w_value)
    keep, low_send, high_send = [item.reshape(-1, share, width) for item in (keep, low_send, high_send)]
    steps = bits_of(size)
    rest = jnp.zeros((), f32)
    for bit in range(steps - 1):
        high = swap(high_send, 1 << bit, size)
        low = swap(low_send, 1 << bit, size)
        half = keep.shape[0] // 2
        if bit:
            high, rest = lax.optimization_barrier((high, rest))
            keep = keep + rest.astype(f32)
        send = (keep[half:] + high.astype(f32)).astype(jnp.float16)
        keep, rest = keep[:half], low
        low_send, high_send = send[: half // 2], send[half // 2 :]
    high = swap(send, 1 << (steps - 1), size)
    high, rest = lax.optimization_barrier((high, rest))
    raw = (keep + rest.astype(f32) + high.astype(f32))[0]
    w_out, raw = lax.optimization_barrier((w_out, raw))

    reach = reach_of(lax.dynamic_index_in_dim(parents, my_tree, 0, False))
    reach_rows = lax.dynamic_slice_in_dim(reach, my_part * share, share, 0)
    position = length.astype(f32) + jnp.sum(reach_rows, -1) - 1.0
    half_dim = HEAD_DIM // 2
    freq = rope_base ** (-(jnp.arange(half_dim, dtype=f32) * 2.0 / HEAD_DIM))
    angle = position[:, None] * freq[None, :]
    cosine = jnp.cos(angle)
    sine = jnp.sin(angle)
    cosine = jnp.concatenate([cosine, cosine], -1)
    sine = jnp.concatenate([-sine, sine], -1)
    bias = jnp.where(reach_rows > 0.5, 0.0, neg_big)

    raw_key = raw[:, group * HEAD_DIM : (group + 1) * HEAD_DIM]
    new_key = raw_key * cosine + jnp.roll(raw_key, half_dim, 1) * sine
    fresh = [jnp.stack([new_key.astype(bf16), raw[:, (group + 1) * HEAD_DIM :].astype(bf16)])]
    chunks = {unit: [held[unit]] for unit in held}
    for bit in range(split_bits):
        fresh = fresh + [swap(item, 1 << bit, size) for item in fresh]
        for unit in chunks:
            chunks[unit] = chunks[unit] + [swap(item, 1 << bit, size) for item in chunks[unit]]
    chunks = [item for unit in [0] + order for item in chunks[unit]]

    count = group * share
    query, top, mass, acc = pl.pallas_call(
        functools.partial(cache_kernel, near, group, 6),
        out_shape=[shape((count, HEAD_DIM), bf16)] + [shape((count, HEAD_DIM), f32)] * 3,
        in_specs=[SMEM] + [VMEM] * (3 + near),
        out_specs=[VMEM] * 4,
        scratch_shapes=[
            pltpu.VMEM((near, span, HEAD_DIM), bf16),
            pltpu.VMEM((near, span, HEAD_DIM), bf16),
            pltpu.VMEM((near, count, span), f32),
        ],
        name="cache",
        compiler_params=room(20),
    )(meta, raw, cosine, sine, *chunks[:near])

    far = len(masks) - near
    block = pl.pallas_call(
        functools.partial(last_kernel, far, splits, group, 6 + near),
        out_shape=shape((share, group * HEAD_DIM), bf16),
        in_specs=[SMEM] + [VMEM] * (1 + far + splits + 4),
        out_specs=VMEM,
        scratch_shapes=[
            pltpu.VMEM((far, span, HEAD_DIM), bf16),
            pltpu.VMEM((far, span, HEAD_DIM), bf16),
            pltpu.VMEM((far, count, span), f32),
            pltpu.VMEM((2, tree_rows, HEAD_DIM), bf16),
            pltpu.VMEM((count, HEAD_DIM), f32),
            pltpu.VMEM((count, HEAD_DIM), f32),
        ],
        name="last",
        compiler_params=room(20),
    )(meta, query, *chunks[near:], *fresh, bias, top, mass, acc)

    blocks = [block] + [swap(block, i * splits * trees, size) for i in range(1, heads)]
    blocks = [
        item if i == 0 else swap(item, i * splits, size) for item in blocks for i in range(trees)
    ]
    blocks = [[item] for item in blocks]
    for bit in range(split_bits):
        blocks = [item + [swap(piece, 1 << bit, size) for piece in item] for item in blocks]
    blocks = [piece for item in blocks for piece in item]

    out_width = w_out.shape[1] // sides
    if sides == 2:
        order = [1, 0]
    else:
        order = list(range(1, sides)) + [0]

    def product(step, dtype):
        weight = w_out
        if out_width % HEAD_DIM:
            weight = lax.dynamic_slice_in_dim(w_out, (side ^ step) * out_width, out_width, 1)
        return pl.pallas_call(
            functools.partial(out_kernel, splits, trees, heads, step),
            out_shape=shape((rows, out_width), dtype),
            in_specs=[SMEM] + [VMEM] * (len(blocks) + 1),
            out_specs=VMEM,
            name="output",
            compiler_params=room(12),
        )(meta, *blocks, weight)

    total = None
    arrived = []
    for step in order:
        if step:
            arrived.append(
                lax.ppermute(product(step, bf16), "head", [(i, i ^ step) for i in range(sides)])
            )
        else:
            total = product(step, f32)
    for item in arrived:
        total = total + item.astype(f32)
    return total.astype(bf16)


def solution(mesh):
    placed = (
        P("rep", "seq"),
        P("seq", "head"),
        P("seq", "head"),
        P("seq", "head"),
        P("head", "seq"),
        P("rep", "seq", "head"),
        P("rep", "seq", "head"),
        P("rep", None),
        P("rep"),
    )
    return jax.shard_map(
        functools.partial(local, mesh.shape["seq"], mesh.shape["head"]),
        mesh=mesh,
        in_specs=placed,
        out_specs=P("rep", ("seq", "head")),
        check_vma=False,
    )
```

time: 414 us -> 133 us (0.32)
  waiting for transfers between devices: 209 us -> 60.8 us
  blocking collectives: 124 us -> 0 us
  starting transfers between devices: 0.35 us -> 33.7 us
  matrix products: 29.4 us -> 1.04 us
  Pallas kernels: 0 us -> 22 us
  other arithmetic: 20.9 us -> 4.49 us
  between operations: 13.6 us -> 0.89 us
  local copies, waits for them, and re-layouts: 15.5 us -> 9.61 us
    psum x1 -> x0, waiting for transfers between devices: 111 us -> none  [local(): q_raw, k_raw, v_raw = lax.psum((q_part, k_part, v_part), 'seq')]
    psum x1 -> x0, blocking collectives: 63.7 us -> none  [local(): q_raw, k_raw, v_raw = lax.psum((q_part, k_part, v_part), 'seq')]
    ppermute x0 -> x39, waiting for transfers between devices: none -> 60.8 us  [the longest x38 58 us: swap(): return lax.ppermute(value, 'seq', [(i, i ^ mask) for i in range(size)])]
    pmax x1 -> x0, blocking collectives: 60 us -> none  [local(): summit = lax.pmax(peak, 'seq')]
    reduce_scatter x2 -> x0, waiting for transfers between devices: 58 us -> none  [the longest x1 44.5 us: local(): lax.psum_scatter(acc * factor[..., None], 'seq', scatter_dimension=0, til...]
    all_gather x1 -> x0, waiting for transfers between devices: 40.6 us -> none  [local(): attention = lax.all_gather(attention_share, 'seq', axis=0, tiled=True)]
    ppermute x0 -> x39, starting transfers between devices: none -> 33.7 us  [the longest x38 32.2 us: swap(): return lax.ppermute(value, 'seq', [(i, i ^ mask) for i in range(size)])]
    dot_general x17 -> x4, matrix products: 29.4 us -> 1.04 us  [reach_of(): jnp.dot(reach, reach, preferred_element_type=jnp.float32)]
  transfers between devices with their start and end apart: 5 -> 39, of which waited for: 4 -> 13; matrix products, arithmetic and copies ran while one was open for 7% -> 5% of each run, Pallas kernels for 0% -> 8%
where the time goes in v1:
time: 133 us
  waiting for transfers between devices  60.8 us (46%)
  starting transfers between devices  33.7 us (25%)
  Pallas kernels  22 us (17%)
  local copies, waits for them, and re-layouts  9.61 us (7%)
  other arithmetic  4.49 us (3%)
    ppermute x38, waiting for transfers between devices, swap(): return lax.ppermute(value, 'seq', [(i, i ^ mask) for i in range(size)])  58 us
    ppermute x38, starting transfers between devices, swap(): return lax.ppermute(value, 'seq', [(i, i ^ mask) for i in range(size)])  32.2 us
    unnamed x34, local copies, waits for them, and re-layouts  8.1 us
    pallas_call x1, Pallas kernels, local(): pl.pallas_call(functools.partial(last_kernel, far, splits, group, 6 + nea...  7.06 us
    pallas_call x1, Pallas kernels, local(): pl.pallas_call(functools.partial(cache_kernel, near, group, 6), out_shape...  5.92 us
    pallas_call x1, Pallas kernels, local(): keep, low_send, high_send = project(states, w_query, w_key, w_value)  3.26 us
    pallas_call x1, Pallas kernels, local(): pl.pallas_call(functools.partial(pack_kernel, splits, trees), out_shape=[...  3.22 us
    ppermute x1, waiting for transfers between devices, local(): lax.ppermute(product(step, bf16), 'head', [(i, i ^ step) for i in range(s...  2.82 us
  transfers between devices with their start and end apart: 39, of which 13 were waited for; matrix products, arithmetic and copies ran while one was open for 5% of the time, Pallas kernels for 8%

profile of v1, /device:TPU:0, one launch (start us, length us, event | category | flops | bytes accessed | tf_op | source)
XLA Modules:
  0.0 132.6 jit_solution(6378260321877805552)
XLA Ops:
  0.0 2.2 %copy-done.2 = bf16[512,4096]{1,0:T(8,128)(2,1)S(1)} copy-done((bf16[512,4096]{1,0:T(8,128)(2,1)S(1)}, bf16[512,4096]{1,0:T(8,128)(2,1)}, u32[]{:S(2)}) %copy-start.2) | copy-done | bytes 4194328
  5.2 3.3 %project.1 = (f32[2,4,64,1280]{3,2,1,0:T(8,128)S(1)}, f32[1,4,64,1280]{3,2,1,0:T(8,128)}, f32[1,4,64,1280]{3,2,1,0:T(8,128)}) custom-call(bf16[256,512]{1,0:T(8,128)(2,1)S(1)} %copy-done.10, bf16[512,4096]{1,0:T(8,128)(2,1)S(1)} %copy-done.2, bf16[512,512]{1,0:T(8,128)(2,1)S(1)} %copy-done.3, bf16[512,512]{1,0:T(8,128)(2,1)S(1)} %copy-done.4), custom_call_target="tpu_custom_call" | custom-call | tf_op jit(solution)/shard_map/project/pallas_call | solution.py:249
  9.0 3.2 %pack.1 = (bf16[2,512,128]{2,1,0:T(8,128)(2,1)}, bf16[2,512,128]{2,1,0:T(8,128)(2,1)}, bf16[2,512,128]{2,1,0:T(8,128)(2,1)}, bf16[2,512,128]{2,1,0:T(8,128)(2,1)...) custom-call(bf16[2,512,512]{2,1,0:T(8,128)(2,1)} %key_ref.1, ...), custom_call_target="tpu_custom_call" | custom-call | tf_op jit(solution)/shard_map/pack/pallas_call | solution.py:229
  12.7 4.5 %collective-permute-start.8 = (bf16[2,512,128]{2,1,0:T(8,128)(2,1)}, bf16[2,512,128]{2,1,0:T(8,128)(2,1)S(1)}, u32[]{:S(2)}, u32[]{:S(2)}) collective-permute-start(bf16[2,512,128]{2,1,0:T(8,128)(2,1)} %get-tuple-element.39), channel_id=1, source_target_pairs={{0,20},{2,22},{4,16},{6,18},{8,28},{10,30},{12,24},{14,26},{16,4},... | collective-permute-start | bytes 786440 | tf_op jit(solution)/shard_map/ppermute | solution.py:36
  17.3 1.3 collective-permute-start.10
  20.7 1.6 %fusion = f16[4,64,1280]{2,1,0:T(8,128)(2,1)S(1)} fusion(f32[4,64,1280]{2,1,0:T(8,128)} %collective-permute-done, f32[2,4,64,1280]{3,2,1,0:T(8,128)S(1)} %get-tuple-element.28), kind=kLoop, calls=%fused_computation.1 | loop fusion | flops 655360 | bytes 3276800 | tf_op jit(solution)/shard_map/convert_element_type | solution.py:260
  22.4 1.6 %collective-permute-start.1 = (f16[2,64,1280]{2,1,0:T(8,128)(2,1)S(1)}, f16[2,64,1280]{2,1,0:T(8,128)(2,1)S(1)}, u32[]{:S(2)}, u32[]{:S(2)}) collective-permute-start(f16[2,64,1280]{2,1,0:T(8,128)(2,1)S(1)} %get-tuple-element.54), channel_id=1, source_target_pairs={{0,4},{2,6},{4,0},{6,2},{8,12},{10,14},{12,8},{14,10},{16,20},{18,... | collective-permute-start | bytes 983048 | tf_op jit(solution)/shard_map/ppermute | solution.py:36
  24.8 17.9 %collective-permute-done.1 = f16[2,64,1280]{2,1,0:T(8,128)(2,1)S(1)} collective-permute-done((f16[2,64,1280]{2,1,0:T(8,128)(2,1)S(1)}, f16[2,64,1280]{2,1,0:T(8,128)(2,1)S(1)}, u32[]{:S(2)}, u32[]{:S(2)}) %collective-permute-start.1) | collective-permute-done | bytes 327712 | tf_op jit(solution)/shard_map/ppermute | solution.py:36
  42.7 1.5 %bitcast_add_fusion.1 = f32[4,64,1280]{2,1,0:T(8,128)S(1)} fusion(f32[4,64,1280]{2,1,0:T(8,128)} %collective-permute-done.2, f32[2,4,64,1280]{3,2,1,0:T(8,128)S(1)} %get-tuple-element.28), kind=kLoop, calls=%fused_computation.2 | loop fusion | flops 327680 | bytes 3932160 | tf_op jit(solution)/shard_map/add | solution.py:259
  44.5 4.6 %collective-permute-done.4 = f16[2,64,1280]{2,1,0:T(8,128)(2,1)S(1)} collective-permute-done((f16[2,64,1280]{2,1,0:T(8,128)(2,1)S(1)}, f16[2,64,1280]{2,1,0:T(8,128)(2,1)S(1)}, u32[]{:S(2)}, u32[]{:S(2)}) %collective-permute-start.4) | collective-permute-done | bytes 327712 | tf_op jit(solution)/shard_map/ppermute | solution.py:36
  50.0 3.5 %collective-permute-start.5 = (f16[1,64,1280]{2,1,0:T(8,128)(2,1)S(1)}, f16[1,64,1280]{2,1,0:T(8,128)(2,1)S(1)}, u32[]{:S(2)}, u32[]{:S(2)}) collective-permute-start(f16[1,64,1280]{2,1,0:T(8,128)(2,1)S(1)} %fusion.8), channel_id=1, source_target_pairs={{0,16},{2,18},{4,20},{6,22},{8,24},{10,26},{12,28},{14,30},{16,0},... | collective-permute-start | bytes 491528 | tf_op jit(solution)/shard_map/ppermute | solution.py:36
  53.6 4.7 %collective-permute-done.6 = f16[1,64,1280]{2,1,0:T(8,128)(2,1)S(1)} collective-permute-done((f16[1,64,1280]{2,1,0:T(8,128)(2,1)S(1)}, f16[1,64,1280]{2,1,0:T(8,128)(2,1)S(1)}, u32[]{:S(2)}, u32[]{:S(2)}) %collective-permute-start.6) | collective-permute-done | bytes 163872 | tf_op jit(solution)/shard_map/ppermute | solution.py:36
  60.4 1.3 collective-permute-start.14
  61.8 1.2 collective-permute-start.16
  63.0 2.5 %collective-permute-start.18 = (bf16[2,512,128]{2,1,0:T(8,128)(2,1)S(1)}, bf16[2,512,128]{2,1,0:T(8,128)(2,1)S(1)}, u32[]{:S(2)}, u32[]{:S(2)}) collective-permute-start(bf16[2,512,128]{2,1,0:T(8,128)(2,1)S(1)} %copy-done.12), channel_id=1, source_target_pairs={{0,24},{2,26},{4,28},{6,30},{8,16},{10,18},{12,20},{14,22},{16,8},... | collective-permute-start | bytes 786440 | tf_op jit(solution)/shard_map/ppermute | solution.py:36
  65.5 4.8 %collective-permute-done.12.refs_6_ = bf16[2,512,128]{2,1,0:T(8,128)(2,1)S(1)} collective-permute-done((bf16[2,512,128]{2,1,0:T(8,128)(2,1)S(1)}, bf16[2,512,128]{2,1,0:T(8,128)(2,1)S(1)}, u32[]{:S(2)}, u32[]{:S(2)}) %collective-permute-start.12) | collective-permute-done | bytes 262176 | tf_op jit(solution)/shard_map/ppermute | solution.py:36
  70.9 10.5 %collective-permute-done.16.refs_2_ = bf16[2,512,128]{2,1,0:T(8,128)(2,1)S(1)} collective-permute-done((bf16[2,512,128]{2,1,0:T(8,128)(2,1)S(1)}, bf16[2,512,128]{2,1,0:T(8,128)(2,1)S(1)}, u32[]{:S(2)}, u32[]{:S(2)}) %collective-permute-start.16) | collective-permute-done | bytes 262176 | tf_op jit(solution)/shard_map/ppermute | solution.py:36
  86.5 5.9 %cache.1 = (bf16[512,128]{1,0:T(8,128)(2,1)S(1)}, f32[512,128]{1,0:T(8,128)S(1)}, f32[512,128]{1,0:T(8,128)S(1)}, f32[512,128]{1,0:T(8,128)S(1)}) custom-call(s32[22]{0:T(128)S(1)} %stack.97.meta, f32[64,1280]{1,0:T(8,128)S(1)} %fusion.10.raw, f32[64,128]{1,0:T(8,128)S(1)} %get-tuple-element.61.cosine, f32[64,128]{1,0:T(8,128)S(1)} %get-tuple-element.52.sine, ...), custom_call_target="tpu_custom_call" | custom-call | tf_op jit(solution)/shard_map/cache/pallas_call | solution.py:291
  92.5 7.1 %last.1.refs_0_ = bf16[64,1024]{1,0:T(8,128)(2,1)S(1)} custom-call(s32[22]{0:T(128)S(1)} %stack.97.meta, bf16[512,128]{1,0:T(8,128)(2,1)S(1)} %get-tuple-element.42.query, bf16[2,512,128]{2,1,0:T(8,128)(2,1)S(1)} %collective-permute-done.14.refs_0_, bf16[2,512,128]{2,1,0:T(8,128)(2,1)S(1)} %collective-permute-done.15.refs_1_, ...), custom_call_target="tpu_custom_call" | custom-call | tf_op jit(solution)/shard_map/last/pallas_call | solution.py:306
  99.6 1.5 %collective-permute-start.24 = (bf16[64,1024]{1,0:T(8,128)(2,1)S(1)}, bf16[64,1024]{1,0:T(8,128)(2,1)S(1)}, u32[]{:S(2)}, u32[]{:S(2)}) collective-permute-start(bf16[64,1024]{1,0:T(8,128)(2,1)S(1)} %last.1.refs_0_), channel_id=1, source_target_pairs={{0,4},{2,6},{4,0},{6,2},{8,12},{10,14},{12,8},{14,10},{16,20},{18,... | collective-permute-start | bytes 393224 | tf_op jit(solution)/shard_map/ppermute | solution.py:36
  101.1 3.3 %collective-permute-start.26 = (bf16[64,1024]{1,0:T(8,128)(2,1)S(1)}, bf16[64,1024]{1,0:T(8,128)(2,1)S(1)}, u32[]{:S(2)}, u32[]{:S(2)}) collective-permute-start(bf16[64,1024]{1,0:T(8,128)(2,1)S(1)} %last.1.refs_0_), channel_id=1, source_target_pairs={{0,8},{2,10},{4,12},{6,14},{8,0},{10,2},{12,4},{14,6},{16,24},{18,... | collective-permute-start | bytes 393224 | tf_op jit(solution)/shard_map/ppermute | solution.py:36
  104.4 1.9 %collective-permute-start.30 = (bf16[64,1024]{1,0:T(8,128)(2,1)S(1)}, bf16[64,1024]{1,0:T(8,128)(2,1)S(1)}, u32[]{:S(2)}, u32[]{:S(2)}) collective-permute-start(bf16[64,1024]{1,0:T(8,128)(2,1)S(1)} %last.1.refs_0_), channel_id=1, source_target_pairs={{0,16},{2,18},{4,20},{6,22},{8,24},{10,26},{12,28},{14,30},{16,0},... | collective-permute-start | bytes 393224 | tf_op jit(solution)/shard_map/ppermute | solution.py:36
  106.3 1.5 %collective-permute-start.34 = (bf16[64,1024]{1,0:T(8,128)(2,1)S(1)}, bf16[64,1024]{1,0:T(8,128)(2,1)S(1)}, u32[]{:S(2)}, u32[]{:S(2)}) collective-permute-start(bf16[64,1024]{1,0:T(8,128)(2,1)S(1)} %last.1.refs_0_), channel_id=1, source_target_pairs={{0,24},{2,26},{4,28},{6,30},{8,16},{10,18},{12,20},{14,22},{16,8},... | collective-permute-start | bytes 393224 | tf_op jit(solution)/shard_map/ppermute | solution.py:36
  108.9 8.3 %collective-permute-done.30.refs_8_ = bf16[64,1024]{1,0:T(8,128)(2,1)S(1)} collective-permute-done((bf16[64,1024]{1,0:T(8,128)(2,1)S(1)}, bf16[64,1024]{1,0:T(8,128)(2,1)S(1)}, u32[]{:S(2)}, u32[]{:S(2)}) %collective-permute-start.30) | collective-permute-done | bytes 131104 | tf_op jit(solution)/shard_map/ppermute | solution.py:36
  117.9 1.4 %collective-permute-start.36 = (bf16[64,1024]{1,0:T(8,128)(2,1)S(1)}, bf16[64,1024]{1,0:T(8,128)(2,1)S(1)}, u32[]{:S(2)}, u32[]{:S(2)}) collective-permute-start(bf16[64,1024]{1,0:T(8,128)(2,1)S(1)} %collective-permute-done.34.refs_12_), channel_id=1, source_target_pairs={{0,4},{2,6},{4,0},{6,2},{8,12},{10,14},{12,8},{14,10},{16,20},{18,... | collective-permute-start | bytes 393224 | tf_op jit(solution)/shard_map/ppermute | solution.py:36
  119.9 2.3 %collective-permute-done.32.refs_10_ = bf16[64,1024]{1,0:T(8,128)(2,1)S(1)} collective-permute-done((bf16[64,1024]{1,0:T(8,128)(2,1)S(1)}, bf16[64,1024]{1,0:T(8,128)(2,1)S(1)}, u32[]{:S(2)}, u32[]{:S(2)}) %collective-permute-start.32) | collective-permute-done | bytes 131104 | tf_op jit(solution)/shard_map/ppermute | solution.py:36
  122.2 1.4 %collective-permute-done.36.refs_14_ = bf16[64,1024]{1,0:T(8,128)(2,1)S(1)} collective-permute-done((bf16[64,1024]{1,0:T(8,128)(2,1)S(1)}, bf16[64,1024]{1,0:T(8,128)(2,1)S(1)}, u32[]{:S(2)}, u32[]{:S(2)}) %collective-permute-start.36) | collective-permute-done | bytes 131104 | tf_op jit(solution)/shard_map/ppermute | solution.py:36
  123.7 1.3 collective-permute-done.37.refs_15_
  125.0 1.3 output.3
  126.3 1.5 %collective-permute-start.38 = (bf16[256,256]{1,0:T(8,128)(2,1)S(1)}, bf16[256,256]{1,0:T(8,128)(2,1)S(1)}, u32[]{:S(2)}, u32[]{:S(2)}) collective-permute-start(bf16[256,256]{1,0:T(8,128)(2,1)S(1)} %output.3), channel_id=1, source_target_pairs={{0,1},{1,0},{2,3},{3,2},{4,5},{5,4},{6,7},{7,6},{8,9},{9,8},{10,11... | collective-permute-start | bytes 393224 | tf_op jit(solution)/shard_map/ppermute | solution.py:356
  127.8 1.2 output.2
  129.1 2.8 %collective-permute-done.38 = bf16[256,256]{1,0:T(8,128)(2,1)S(1)} collective-permute-done((bf16[256,256]{1,0:T(8,128)(2,1)S(1)}, bf16[256,256]{1,0:T(8,128)(2,1)S(1)}, u32[]{:S(2)}, u32[]{:S(2)}) %collective-permute-start.38) | collective-permute-done | bytes 131104 | tf_op jit(solution)/shard_map/ppermute | solution.py:356
  (109 shorter events, 18.8 us)
Async XLA Ops:
  8.5 12.2 %collective-permute-start = (f32[4,64,1280]{2,1,0:T(8,128)}, f32[4,64,1280]{2,1,0:T(8,128)}, u32[]{:S(2)}, u32[]{:S(2)}) collective-permute-start(f32[4,64,1280]{2,1,0:T(8,128)} %bitcast.23), channel_id=1, source_target_pairs={{0,2},{2,0},{4,6},{6,4},{8,10},{10,8},{12,14},{14,12},{16,18},{18,... | collective-permute-start | bytes 3932168 | tf_op jit(solution)/shard_map/ppermute | solution.py:36
  9.0 15.2 %collective-permute-start.2 = (f32[4,64,1280]{2,1,0:T(8,128)}, f32[4,64,1280]{2,1,0:T(8,128)}, u32[]{:S(2)}, u32[]{:S(2)}) collective-permute-start(f32[4,64,1280]{2,1,0:T(8,128)} %bitcast.24), channel_id=1, source_target_pairs={{0,2},{2,0},{4,6},{6,4},{8,10},{10,8},{12,14},{14,12},{16,18},{18,... | collective-permute-start | bytes 3932168 | tf_op jit(solution)/shard_map/ppermute | solution.py:36
  12.2 49.6 %collective-permute-start.7 = (bf16[2,512,128]{2,1,0:T(8,128)(2,1)}, bf16[2,512,128]{2,1,0:T(8,128)(2,1)S(1)}, u32[]{:S(2)}, u32[]{:S(2)}) collective-permute-start(bf16[2,512,128]{2,1,0:T(8,128)(2,1)} %get-tuple-element.38.refs_0_), channel_id=1, source_target_pairs={{0,2},{2,0},{4,6},{6,4},{8,10},{10,8},{12,14},{14,12},{16,18},{18,... | collective-permute-start | bytes 786440 | tf_op jit(solution)/shard_map/ppermute | solution.py:36
  12.7 50.3 %collective-permute-start.8 = (bf16[2,512,128]{2,1,0:T(8,128)(2,1)}, bf16[2,512,128]{2,1,0:T(8,128)(2,1)S(1)}, u32[]{:S(2)}, u32[]{:S(2)}) collective-permute-start(bf16[2,512,128]{2,1,0:T(8,128)(2,1)} %get-tuple-element.39), channel_id=1, source_target_pairs={{0,20},{2,22},{4,16},{6,18},{8,28},{10,30},{12,24},{14,26},{16,4},... | collective-permute-start | bytes 786440 | tf_op jit(solution)/shard_map/ppermute | solution.py:36
  17.3 48.3 %collective-permute-start.10 = (bf16[2,512,128]{2,1,0:T(8,128)(2,1)}, bf16[2,512,128]{2,1,0:T(8,128)(2,1)S(1)}, u32[]{:S(2)}, u32[]{:S(2)}) collective-permute-start(bf16[2,512,128]{2,1,0:T(8,128)(2,1)} %get-tuple-element.40), channel_id=1, source_target_pairs={{0,28},{2,30},{4,24},{6,26},{8,20},{10,22},{12,16},{14,18},{16,12}... | collective-permute-start | bytes 786440 | tf_op jit(solution)/shard_map/ppermute | solution.py:36
  22.4 20.3 %collective-permute-start.1 = (f16[2,64,1280]{2,1,0:T(8,128)(2,1)S(1)}, f16[2,64,1280]{2,1,0:T(8,128)(2,1)S(1)}, u32[]{:S(2)}, u32[]{:S(2)}) collective-permute-start(f16[2,64,1280]{2,1,0:T(8,128)(2,1)S(1)} %get-tuple-element.54), channel_id=1, source_target_pairs={{0,4},{2,6},{4,0},{6,2},{8,12},{10,14},{12,8},{14,10},{16,20},{18,... | collective-permute-start | bytes 983048 | tf_op jit(solution)/shard_map/ppermute | solution.py:36
  24.2 24.9 %collective-permute-start.4 = (f16[2,64,1280]{2,1,0:T(8,128)(2,1)S(1)}, f16[2,64,1280]{2,1,0:T(8,128)(2,1)S(1)}, u32[]{:S(2)}, u32[]{:S(2)}) collective-permute-start(f16[2,64,1280]{2,1,0:T(8,128)(2,1)S(1)} %get-tuple-element.53), channel_id=1, source_target_pairs={{0,4},{2,6},{4,0},{6,2},{8,12},{10,14},{12,8},{14,10},{16,20},{18,... | collective-permute-start | bytes 983048 | tf_op jit(solution)/shard_map/ppermute | solution.py:36
  44.4 5.4 %collective-permute-start.3 = (f16[1,64,1280]{2,1,0:T(8,128)(2,1)S(1)}, f16[1,64,1280]{2,1,0:T(8,128)(2,1)S(1)}, u32[]{:S(2)}, u32[]{:S(2)}) collective-permute-start(f16[1,64,1280]{2,1,0:T(8,128)(2,1)S(1)} %get-tuple-element.58), channel_id=1, source_target_pairs={{0,8},{2,10},{4,12},{6,14},{8,0},{10,2},{12,4},{14,6},{16,24},{18,... | collective-permute-start | bytes 491528 | tf_op jit(solution)/shard_map/ppermute | solution.py:36
  49.1 9.1 %collective-permute-start.6 = (f16[1,64,1280]{2,1,0:T(8,128)(2,1)S(1)}, f16[1,64,1280]{2,1,0:T(8,128)(2,1)S(1)}, u32[]{:S(2)}, u32[]{:S(2)}) collective-permute-start(f16[1,64,1280]{2,1,0:T(8,128)(2,1)S(1)} %get-tuple-element.57), channel_id=1, source_target_pairs={{0,8},{2,10},{4,12},{6,14},{8,0},{10,2},{12,4},{14,6},{16,24},{18,... | collective-permute-start | bytes 491528 | tf_op jit(solution)/shard_map/ppermute | solution.py:36
  50.0 10.5 %collective-permute-start.5 = (f16[1,64,1280]{2,1,0:T(8,128)(2,1)S(1)}, f16[1,64,1280]{2,1,0:T(8,128)(2,1)S(1)}, u32[]{:S(2)}, u32[]{:S(2)}) collective-permute-start(f16[1,64,1280]{2,1,0:T(8,128)(2,1)S(1)} %fusion.8), channel_id=1, source_target_pairs={{0,16},{2,18},{4,20},{6,22},{8,24},{10,26},{12,28},{14,30},{16,0},... | collective-permute-start | bytes 491528 | tf_op jit(solution)/shard_map/ppermute | solution.py:36
  58.3 12.0 %collective-permute-start.12 = (bf16[2,512,128]{2,1,0:T(8,128)(2,1)S(1)}, bf16[2,512,128]{2,1,0:T(8,128)(2,1)S(1)}, u32[]{:S(2)}, u32[]{:S(2)}) collective-permute-start(bf16[2,512,128]{2,1,0:T(8,128)(2,1)S(1)} %copy-done.15), channel_id=1, source_target_pairs={{0,12},{2,14},{4,8},{6,10},{8,4},{10,6},{12,0},{14,2},{16,28},{18,... | collective-permute-start | bytes 786440 | tf_op jit(solution)/shard_map/ppermute | solution.py:36
  60.4 9.9 %collective-permute-start.14 = (bf16[2,512,128]{2,1,0:T(8,128)(2,1)S(1)}, bf16[2,512,128]{2,1,0:T(8,128)(2,1)S(1)}, u32[]{:S(2)}, u32[]{:S(2)}) collective-permute-start(bf16[2,512,128]{2,1,0:T(8,128)(2,1)S(1)} %copy-done.14), channel_id=1, source_target_pairs={{0,4},{2,6},{4,0},{6,2},{8,12},{10,14},{12,8},{14,10},{16,20},{18,... | collective-permute-start | bytes 786440 | tf_op jit(solution)/shard_map/ppermute | solution.py:36
  61.8 19.5 %collective-permute-start.16 = (bf16[2,512,128]{2,1,0:T(8,128)(2,1)S(1)}, bf16[2,512,128]{2,1,0:T(8,128)(2,1)S(1)}, u32[]{:S(2)}, u32[]{:S(2)}) collective-permute-start(bf16[2,512,128]{2,1,0:T(8,128)(2,1)S(1)} %copy-done.13), channel_id=1, source_target_pairs={{0,16},{2,18},{4,20},{6,22},{8,24},{10,26},{12,28},{14,30},{16,0},... | collective-permute-start | bytes 786440 | tf_op jit(solution)/shard_map/ppermute | solution.py:36
  63.0 18.3 %collective-permute-start.18 = (bf16[2,512,128]{2,1,0:T(8,128)(2,1)S(1)}, bf16[2,512,128]{2,1,0:T(8,128)(2,1)S(1)}, u32[]{:S(2)}, u32[]{:S(2)}) collective-permute-start(bf16[2,512,128]{2,1,0:T(8,128)(2,1)S(1)} %copy-done.12), channel_id=1, source_target_pairs={{0,24},{2,26},{4,28},{6,30},{8,16},{10,18},{12,20},{14,22},{16,8},... | collective-permute-start | bytes 786440 | tf_op jit(solution)/shard_map/ppermute | solution.py:36
  65.5 16.4 %collective-permute-start.20 = (bf16[2,512,128]{2,1,0:T(8,128)(2,1)S(1)}, bf16[2,512,128]{2,1,0:T(8,128)(2,1)S(1)}, u32[]{:S(2)}, u32[]{:S(2)}) collective-permute-start(bf16[2,512,128]{2,1,0:T(8,128)(2,1)S(1)} %copy-done.11), channel_id=1, source_target_pairs={{0,8},{2,10},{4,12},{6,14},{8,0},{10,2},{12,4},{14,6},{16,24},{18,... | collective-permute-start | bytes 786440 | tf_op jit(solution)/shard_map/ppermute | solution.py:36
  70.3 11.7 %collective-permute-start.9 = (bf16[2,512,128]{2,1,0:T(8,128)(2,1)S(1)}, bf16[2,512,128]{2,1,0:T(8,128)(2,1)S(1)}, u32[]{:S(2)}, u32[]{:S(2)}) collective-permute-start(bf16[2,512,128]{2,1,0:T(8,128)(2,1)S(1)} %collective-permute-done.8.refs_2_), channel_id=1, source_target_pairs={{0,2},{2,0},{4,6},{6,4},{8,10},{10,8},{12,14},{14,12},{16,18},{18,... | collective-permute-start | bytes 786440 | tf_op jit(solution)/shard_map/ppermute | solution.py:36
  70.3 12.1 %collective-permute-start.11 = (bf16[2,512,128]{2,1,0:T(8,128)(2,1)S(1)}, bf16[2,512,128]{2,1,0:T(8,128)(2,1)S(1)}, u32[]{:S(2)}, u32[]{:S(2)}) collective-permute-start(bf16[2,512,128]{2,1,0:T(8,128)(2,1)S(1)} %collective-permute-done.10.refs_4_), channel_id=1, source_target_pairs={{0,2},{2,0},{4,6},{6,4},{8,10},{10,8},{12,14},{14,12},{16,18},{18,... | collective-permute-start | bytes 786440 | tf_op jit(solution)/shard_map/ppermute | solution.py:36
  81.4 11.1 %collective-permute-start.15 = (bf16[2,512,128]{2,1,0:T(8,128)(2,1)S(1)}, bf16[2,512,128]{2,1,0:T(8,128)(2,1)S(1)}, u32[]{:S(2)}, u32[]{:S(2)}) collective-permute-start(bf16[2,512,128]{2,1,0:T(8,128)(2,1)S(1)} %collective-permute-done.14.refs_0_), channel_id=1, source_target_pairs={{0,2},{2,0},{4,6},{6,4},{8,10},{10,8},{12,14},{14,12},{16,18},{18,... | collective-permute-start | bytes 786440 | tf_op jit(solution)/shard_map/ppermute | solution.py:36
  81.9 10.6 %collective-permute-start.17 = (bf16[2,512,128]{2,1,0:T(8,128)(2,1)S(1)}, bf16[2,512,128]{2,1,0:T(8,128)(2,1)}, u32[]{:S(2)}, u32[]{:S(2)}) collective-permute-start(bf16[2,512,128]{2,1,0:T(8,128)(2,1)S(1)} %collective-permute-done.16.refs_2_), channel_id=1, source_target_pairs={{0,2},{2,0},{4,6},{6,4},{8,10},{10,8},{12,14},{14,12},{16,18},{18,... | collective-permute-start | bytes 786440 | tf_op jit(solution)/shard_map/ppermute | solution.py:36
  82.0 10.5 %collective-permute-start.19 = (bf16[2,512,128]{2,1,0:T(8,128)(2,1)S(1)}, bf16[2,512,128]{2,1,0:T(8,128)(2,1)}, u32[]{:S(2)}, u32[]{:S(2)}) collective-permute-start(bf16[2,512,128]{2,1,0:T(8,128)(2,1)S(1)} %collective-permute-done.18.refs_4_), channel_id=1, source_target_pairs={{0,2},{2,0},{4,6},{6,4},{8,10},{10,8},{12,14},{14,12},{16,18},{18,... | collective-permute-start | bytes 786440 | tf_op jit(solution)/shard_map/ppermute | solution.py:36
  82.4 10.1 %collective-permute-start.21 = (bf16[2,512,128]{2,1,0:T(8,128)(2,1)S(1)}, bf16[2,512,128]{2,1,0:T(8,128)(2,1)}, u32[]{:S(2)}, u32[]{:S(2)}) collective-permute-start(bf16[2,512,128]{2,1,0:T(8,128)(2,1)S(1)} %collective-permute-done.20.refs_6_), channel_id=1, source_target_pairs={{0,2},{2,0},{4,6},{6,4},{8,10},{10,8},{12,14},{14,12},{16,18},{18,... | collective-permute-start | bytes 786440 | tf_op jit(solution)/shard_map/ppermute | solution.py:36
  83.8 8.6 %collective-permute-start.22 = (bf16[2,64,128]{2,1,0:T(8,128)(2,1)S(1)}, bf16[2,64,128]{2,1,0:T(8,128)(2,1)S(1)}, u32[]{:S(2)}, u32[]{:S(2)}) collective-permute-start(bf16[2,64,128]{2,1,0:T(8,128)(2,1)S(1)} %pad_maximum_fusion.2.refs_8_), channel_id=1, source_target_pairs={{0,2},{2,0},{4,6},{6,4},{8,10},{10,8},{12,14},{14,12},{16,18},{18,... | collective-permute-start | bytes 98312 | tf_op jit(solution)/shard_map/ppermute | solution.py:36
  99.6 8.2 %collective-permute-start.24 = (bf16[64,1024]{1,0:T(8,128)(2,1)S(1)}, bf16[64,1024]{1,0:T(8,128)(2,1)S(1)}, u32[]{:S(2)}, u32[]{:S(2)}) collective-permute-start(bf16[64,1024]{1,0:T(8,128)(2,1)S(1)} %last.1.refs_0_), channel_id=1, source_target_pairs={{0,4},{2,6},{4,0},{6,2},{8,12},{10,14},{12,8},{14,10},{16,20},{18,... | collective-permute-start | bytes 393224 | tf_op jit(solution)/shard_map/ppermute | solution.py:36
  101.1 6.9 %collective-permute-start.26 = (bf16[64,1024]{1,0:T(8,128)(2,1)S(1)}, bf16[64,1024]{1,0:T(8,128)(2,1)S(1)}, u32[]{:S(2)}, u32[]{:S(2)}) collective-permute-start(bf16[64,1024]{1,0:T(8,128)(2,1)S(1)} %last.1.refs_0_), channel_id=1, source_target_pairs={{0,8},{2,10},{4,12},{6,14},{8,0},{10,2},{12,4},{14,6},{16,24},{18,... | collective-permute-start | bytes 393224 | tf_op jit(solution)/shard_map/ppermute | solution.py:36
  104.4 12.9 %collective-permute-start.30 = (bf16[64,1024]{1,0:T(8,128)(2,1)S(1)}, bf16[64,1024]{1,0:T(8,128)(2,1)S(1)}, u32[]{:S(2)}, u32[]{:S(2)}) collective-permute-start(bf16[64,1024]{1,0:T(8,128)(2,1)S(1)} %last.1.refs_0_), channel_id=1, source_target_pairs={{0,16},{2,18},{4,20},{6,22},{8,24},{10,26},{12,28},{14,30},{16,0},... | collective-permute-start | bytes 393224 | tf_op jit(solution)/shard_map/ppermute | solution.py:36
  106.3 11.6 %collective-permute-start.34 = (bf16[64,1024]{1,0:T(8,128)(2,1)S(1)}, bf16[64,1024]{1,0:T(8,128)(2,1)S(1)}, u32[]{:S(2)}, u32[]{:S(2)}) collective-permute-start(bf16[64,1024]{1,0:T(8,128)(2,1)S(1)} %last.1.refs_0_), channel_id=1, source_target_pairs={{0,24},{2,26},{4,28},{6,30},{8,16},{10,18},{12,20},{14,22},{16,8},... | collective-permute-start | bytes 393224 | tf_op jit(solution)/shard_map/ppermute | solution.py:36
  107.7 11.5 %collective-permute-start.25 = (bf16[64,1024]{1,0:T(8,128)(2,1)S(1)}, bf16[64,1024]{1,0:T(8,128)(2,1)S(1)}, u32[]{:S(2)}, u32[]{:S(2)}) collective-permute-start(bf16[64,1024]{1,0:T(8,128)(2,1)S(1)} %collective-permute-done.24.refs_2_), channel_id=1, source_target_pairs={{0,2},{2,0},{4,6},{6,4},{8,10},{10,8},{12,14},{14,12},{16,18},{18,... | collective-permute-start | bytes 393224 | tf_op jit(solution)/shard_map/ppermute | solution.py:36
  108.0 11.3 %collective-permute-start.27 = (bf16[64,1024]{1,0:T(8,128)(2,1)S(1)}, bf16[64,1024]{1,0:T(8,128)(2,1)S(1)}, u32[]{:S(2)}, u32[]{:S(2)}) collective-permute-start(bf16[64,1024]{1,0:T(8,128)(2,1)S(1)} %collective-permute-done.26.refs_4_), channel_id=1, source_target_pairs={{0,2},{2,0},{4,6},{6,4},{8,10},{10,8},{12,14},{14,12},{16,18},{18,... | collective-permute-start | bytes 393224 | tf_op jit(solution)/shard_map/ppermute | solution.py:36
  108.3 11.5 %collective-permute-start.28 = (bf16[64,1024]{1,0:T(8,128)(2,1)S(1)}, bf16[64,1024]{1,0:T(8,128)(2,1)S(1)}, u32[]{:S(2)}, u32[]{:S(2)}) collective-permute-start(bf16[64,1024]{1,0:T(8,128)(2,1)S(1)} %collective-permute-done.26.refs_4_), channel_id=1, source_target_pairs={{0,4},{2,6},{4,0},{6,2},{8,12},{10,14},{12,8},{14,10},{16,20},{18,... | collective-permute-start | bytes 393224 | tf_op jit(solution)/shard_map/ppermute | solution.py:36
  117.3 5.0 %collective-permute-start.32 = (bf16[64,1024]{1,0:T(8,128)(2,1)S(1)}, bf16[64,1024]{1,0:T(8,128)(2,1)S(1)}, u32[]{:S(2)}, u32[]{:S(2)}) collective-permute-start(bf16[64,1024]{1,0:T(8,128)(2,1)S(1)} %collective-permute-done.30.refs_8_), channel_id=1, source_target_pairs={{0,4},{2,6},{4,0},{6,2},{8,12},{10,14},{12,8},{14,10},{16,20},{18,... | collective-permute-start | bytes 393224 | tf_op jit(solution)/shard_map/ppermute | solution.py:36
  117.9 5.7 %collective-permute-start.36 = (bf16[64,1024]{1,0:T(8,128)(2,1)S(1)}, bf16[64,1024]{1,0:T(8,128)(2,1)S(1)}, u32[]{:S(2)}, u32[]{:S(2)}) collective-permute-start(bf16[64,1024]{1,0:T(8,128)(2,1)S(1)} %collective-permute-done.34.refs_12_), channel_id=1, source_target_pairs={{0,4},{2,6},{4,0},{6,2},{8,12},{10,14},{12,8},{14,10},{16,20},{18,... | collective-permute-start | bytes 393224 | tf_op jit(solution)/shard_map/ppermute | solution.py:36
  126.3 5.6 %collective-permute-start.38 = (bf16[256,256]{1,0:T(8,128)(2,1)S(1)}, bf16[256,256]{1,0:T(8,128)(2,1)S(1)}, u32[]{:S(2)}, u32[]{:S(2)}) collective-permute-start(bf16[256,256]{1,0:T(8,128)(2,1)S(1)} %output.3), channel_id=1, source_target_pairs={{0,1},{1,0},{2,3},{3,2},{4,5},{5,4},{6,7},{7,6},{8,9},{9,8},{10,11... | collective-permute-start | bytes 393224 | tf_op jit(solution)/shard_map/ppermute | solution.py:356
  (24 other events, 205.1 us)

commit v2 on v1

--- a/solution.py
+++ b/solution.py
@@ -13,8 +13,8 @@
 neg_big = -1e30
 log2_e = 1.4426950408889634
 
+HBM = pl.BlockSpec(memory_space=pltpu.HBM)
 VMEM = pl.BlockSpec(memory_space=pltpu.VMEM)
-SMEM = pl.BlockSpec(memory_space=pltpu.SMEM)
 
 
 def room(mib):
@@ -46,18 +46,24 @@
     return me & (splits - 1), (me >> split_bits) & (trees - 1), me >> (split_bits + bits_of(trees))
 
 
-def pack_kernel(splits, trees, key_ref, value_ref, *outs):
+def pack_kernel(splits, trees, units, key_ref, value_ref, *refs):
+    outs, sems = refs[:-1], refs[-1]
     _, tree, head = place_of(splits, trees)
-    for unit, out in enumerate(outs):
+    copies = []
+    for unit, out in zip(units, outs):
         source = (unit & (trees - 1)) ^ tree
         lanes = pl.ds(pl.multiple_of(((unit >> bits_of(trees)) ^ head) * HEAD_DIM, HEAD_DIM), HEAD_DIM)
-        out[0] = key_ref[source, :, lanes]
-        out[1] = value_ref[source, :, lanes]
-
-
-def project_kernel(splits, trees, states, wq, wk, wv, keep, low_send, high_send):
+        for i, ref in enumerate((key_ref, value_ref)):
+            copies.append(pltpu.make_async_copy(ref.at[source, :, lanes], out.at[i], sems.at[len(copies)]))
+    for copy in copies:
+        copy.start()
+    for copy in copies:
+        copy.wait()
+
+
+def project_kernel(splits, trees, heads, states, wq, wk, wv, *targets):
     my_part, my_tree, my_head = place_of(splits, trees)
-    heads, share = keep.shape[1:3]
+    share = targets[0].shape[1]
     width = bits_of(splits)
     rows = []
     for part in range(splits):
@@ -72,12 +78,13 @@
             size = weight.shape[1] // heads
             lanes = pl.ds(pl.multiple_of(source * size, size), size)
             out = jnp.dot(left, weight[:, lanes], preferred_element_type=jnp.float32)
-            row = 0
-            for target in (keep, low_send, high_send):
-                count = target.shape[0]
-                piece = out[row : row + count * share].reshape(count, share, size)
-                target[:, head, :, low : low + size] = piece
-                row += count * share
+            for group in range(splits * trees):
+                spot = group * heads + head
+                for target in targets:
+                    if spot < target.shape[0]:
+                        target[spot, :, low : low + size] = out[group * share : (group + 1) * share]
+                        break
+                    spot -= target.shape[0]
             low += size
 
 
@@ -85,14 +92,10 @@
     return [value[:, low : low + HEAD_DIM] for low in range(0, value.shape[1], HEAD_DIM)]
 
 
-def scores_of(query, keys, scores, meta, offset, top):
-    span = keys.shape[1]
-    length = meta[4]
-
+def scores_of(query, keys, scores, filled, top):
     def body(i, top):
         piece = dot_t(query[...], keys[i])
-        place = meta[offset + i] + lax.broadcasted_iota(jnp.int32, (1, span), 1)
-        piece = piece + jnp.where(place < length, 0.0, neg_big)
+        piece = piece + filled[pl.ds(i, 1), :]
         scores[i] = piece
         return functools.reduce(jnp.maximum, lane_blocks(piece), top)
 
@@ -111,7 +114,7 @@
     lax.fori_loop(0, values.shape[0], body, 0)
 
 
-def cache_kernel(count, group, offset, meta, raw, cosine, sine, *refs):
+def cache_kernel(count, group, filled, raw, cosine, sine, *refs):
     chunks = refs[:count]
     query, top_out, mass, acc, keys, values, scores = refs[count:]
     share = raw.shape[0]
@@ -123,7 +126,7 @@
         keys[i] = chunk[0]
         values[i] = chunk[1]
     top = jnp.full(top_out.shape, neg_big, jnp.float32)
-    top = scores_of(query, keys, scores, meta, offset, top)
+    top = scores_of(query, keys, scores, filled, top)
     top = jnp.max(top, 1, keepdims=True)
     mass[...] = jnp.zeros(mass.shape, jnp.float32)
     acc[...] = jnp.zeros(acc.shape, jnp.float32)
@@ -131,7 +134,7 @@
     top_out[...] = jnp.broadcast_to(top, top_out.shape)
 
 
-def last_kernel(count, pieces, group, offset, meta, query, *refs):
+def last_kernel(count, pieces, group, filled, query, *refs):
     chunks = refs[:count]
     fresh = refs[count : count + pieces]
     bias, top_in, mass_in, acc_in, out, keys, values, scores, nodes, mass, acc = refs[count + pieces :]
@@ -141,14 +144,15 @@
     for i, chunk in enumerate(chunks):
         keys[i] = chunk[0]
         values[i] = chunk[1]
+    mine = lax.axis_index("seq").astype(jnp.int32) & (pieces - 1)
     for i, piece in enumerate(fresh):
-        place = pl.ds(pl.multiple_of((meta[0] ^ i) * share, share), share)
+        place = pl.ds(pl.multiple_of((mine ^ i) * share, share), share)
         nodes[0, place, :] = piece[0]
         nodes[1, place, :] = piece[1]
     tree = dot_t(query[...], nodes[0])
     tree = (tree.reshape(group, share, -1) + bias[...][None]).reshape(rows, -1)
     top = functools.reduce(jnp.maximum, lane_blocks(tree), top_in[...])
-    top = scores_of(query, keys, scores, meta, offset, top)
+    top = scores_of(query, keys, scores, filled, top)
     top = jnp.max(top, 1, keepdims=True)
     shrink = jnp.exp2((top_in[...] - top) * rate)
     weight = jnp.exp2((tree - top) * rate)
@@ -163,7 +167,8 @@
         out[:, head * HEAD_DIM : (head + 1) * HEAD_DIM] = result[head * share : (head + 1) * share]
 
 
-def out_kernel(splits, trees, heads, step, meta, *refs):
+def out_kernel(splits, trees, heads, step, *refs):
+    my_part, my_tree, my_head = place_of(splits, trees)
     blocks = refs[: splits * trees * heads]
     weight, out = refs[splits * trees * heads :]
     share, depth = blocks[0].shape
@@ -171,18 +176,18 @@
     if weight.shape[1] == width:
         column = slice(None)
     else:
-        column = pl.ds(pl.multiple_of((meta[3] ^ step) * width, width), width)
+        column = pl.ds(pl.multiple_of((lax.axis_index("head").astype(jnp.int32) ^ step) * width, width), width)
     total = None
     for head in range(heads):
         left = jnp.concatenate(
             [blocks[(head * trees + tree) * splits + part][...] for tree in range(trees) for part in range(splits)], 0
         )
-        deep = pl.ds(pl.multiple_of((head ^ meta[2]) * depth, depth), depth)
+        deep = pl.ds(pl.multiple_of((head ^ my_head) * depth, depth), depth)
         term = jnp.dot(left, weight[deep, column], preferred_element_type=jnp.float32)
         total = term if total is None else total + term
     for tree in range(trees):
         for part in range(splits):
-            row = ((tree ^ meta[1]) * splits + (part ^ meta[0])) * share
+            row = ((tree ^ my_tree) * splits + (part ^ my_part)) * share
             low = (tree * splits + part) * share
             out[pl.ds(pl.multiple_of(row, share), share), :] = total[low : low + share].astype(out.dtype)
 
@@ -205,7 +210,7 @@
     units = trees * heads
     splits = size // units
     share = tree_rows // splits
-    split_bits, tree_bits = bits_of(splits), bits_of(trees)
+    split_bits = bits_of(splits)
     width = (group + 2) * HEAD_DIM
     f32, bf16 = jnp.float32, jnp.bfloat16
     shape = jax.ShapeDtypeStruct
@@ -214,57 +219,60 @@
     side = lax.axis_index("head").astype(jnp.int32)
     my_part = me & (splits - 1)
     my_tree = (me >> split_bits) & (trees - 1)
-    my_head = me >> (split_bits + tree_bits)
-
-    order = sorted(
-        range(1, units), key=lambda u: (-(u & (trees - 1)), -bits_of((u >> tree_bits) + 1), u)
-    )
-    masks = [unit * splits + part for unit in [0] + order for part in range(splits)]
-    length = lax.dynamic_index_in_dim(cache_lengths, my_tree, 0, False)
-    meta = jnp.stack(
-        [my_part, my_tree, my_head, side, length, me] + [(me ^ mask) * span for mask in masks]
-    )
-    near = len(masks) // 2
-
-    packed = pl.pallas_call(
-        functools.partial(pack_kernel, splits, trees),
-        out_shape=[shape((2, span, HEAD_DIM), bf16)] * units,
-        in_specs=[VMEM, VMEM],
-        out_specs=[VMEM] * units,
-        name="pack",
-    )(key_cache, value_cache)
-    held = {0: packed[0]}
-    for unit in order:
-        held[unit] = swap(packed[unit], unit * splits, size)
-
-    groups = splits * trees
+
+    steps = bits_of(size)
+    pieces = [size // 2, size // 4, size // 4]
     project = pl.pallas_call(
-        functools.partial(project_kernel, splits, trees),
-        out_shape=[shape((part, heads, share, width), f32) for part in (groups // 2, groups // 4, groups // 4)],
+        functools.partial(project_kernel, splits, trees, heads),
+        out_shape=[shape((piece, share, width), f32) for piece in pieces],
         in_specs=[VMEM] * 4,
-        out_specs=[VMEM] * 3,
+        out_specs=[VMEM] * len(pieces),
         name="project",
         compiler_params=room(12),
     )
     keep, low_send, high_send = project(states, w_query, w_key, w_value)
-    keep, low_send, high_send = [item.reshape(-1, share, width) for item in (keep, low_send, high_send)]
-    steps = bits_of(size)
-    rest = jnp.zeros((), f32)
+    rest = None
     for bit in range(steps - 1):
         high = swap(high_send, 1 << bit, size)
         low = swap(low_send, 1 << bit, size)
-        half = keep.shape[0] // 2
-        if bit:
+        if rest is not None:
             high, rest = lax.optimization_barrier((high, rest))
             keep = keep + rest.astype(f32)
+        half = keep.shape[0] // 2
         send = (keep[half:] + high.astype(f32)).astype(jnp.float16)
         keep, rest = keep[:half], low
+        if bit == 0:
+            keep, rest = keep + low, None
         low_send, high_send = send[: half // 2], send[half // 2 :]
     high = swap(send, 1 << (steps - 1), size)
     high, rest = lax.optimization_barrier((high, rest))
     raw = (keep + rest.astype(f32) + high.astype(f32))[0]
+    away = sorted(range(1, heads), key=lambda h: (h.bit_count() > 1, -h))
+    order = [h * trees + t for h in away for t in range(1, trees)]
+    order += [h * trees for h in away[:-1]]
+    order += list(range(1, trees))
+    order += [h * trees for h in away[-1:]]
+    packed = pl.pallas_call(
+        functools.partial(pack_kernel, splits, trees, [0] + order),
+        out_shape=[shape((2, span, HEAD_DIM), bf16)] * units,
+        in_specs=[HBM, HBM],
+        out_specs=[VMEM] * units,
+        scratch_shapes=[pltpu.SemaphoreType.DMA((2 * units,))],
+        name="pack",
+        compiler_params=room(60),
+    )(key_cache, value_cache)
+    held = {0: packed[0]}
+    for spot, unit in enumerate(order):
+        held[unit] = swap(packed[1 + spot], unit * splits, size)
+
     w_out, raw = lax.optimization_barrier((w_out, raw))
 
+    length = lax.dynamic_index_in_dim(cache_lengths, my_tree, 0, False)
+    masks = [unit * splits + part for unit in [0] + order for part in range(splits)]
+    sources = jnp.stack([me ^ mask for mask in masks])
+    places = sources[:, None] * span + jnp.arange(span, dtype=jnp.int32)[None, :]
+    filled = jnp.where(places < length, 0.0, neg_big)
+    near = len(masks) - splits
     reach = reach_of(lax.dynamic_index_in_dim(parents, my_tree, 0, False))
     reach_rows = lax.dynamic_slice_in_dim(reach, my_part * share, share, 0)
     position = length.astype(f32) + jnp.sum(reach_rows, -1) - 1.0
@@ -280,18 +288,20 @@
     raw_key = raw[:, group * HEAD_DIM : (group + 1) * HEAD_DIM]
     new_key = raw_key * cosine + jnp.roll(raw_key, half_dim, 1) * sine
     fresh = [jnp.stack([new_key.astype(bf16), raw[:, (group + 1) * HEAD_DIM :].astype(bf16)])]
-    chunks = {unit: [held[unit]] for unit in held}
     for bit in range(split_bits):
         fresh = fresh + [swap(item, 1 << bit, size) for item in fresh]
-        for unit in chunks:
-            chunks[unit] = chunks[unit] + [swap(item, 1 << bit, size) for item in chunks[unit]]
-    chunks = [item for unit in [0] + order for item in chunks[unit]]
+    chunks = []
+    for unit in [0] + order:
+        pieces = [held[unit]]
+        for bit in range(split_bits):
+            pieces = pieces + [swap(item, 1 << bit, size) for item in pieces]
+        chunks += pieces
 
     count = group * share
-    query, top, mass, acc = pl.pallas_call(
-        functools.partial(cache_kernel, near, group, 6),
+    attend = pl.pallas_call(
+        functools.partial(cache_kernel, near, group),
         out_shape=[shape((count, HEAD_DIM), bf16)] + [shape((count, HEAD_DIM), f32)] * 3,
-        in_specs=[SMEM] + [VMEM] * (3 + near),
+        in_specs=[VMEM] * (4 + near),
         out_specs=[VMEM] * 4,
         scratch_shapes=[
             pltpu.VMEM((near, span, HEAD_DIM), bf16),
@@ -299,14 +309,15 @@
             pltpu.VMEM((near, count, span), f32),
         ],
         name="cache",
-        compiler_params=room(20),
-    )(meta, raw, cosine, sine, *chunks[:near])
+        compiler_params=room(30),
+    )
+    query, top, mass, acc = attend(filled[:near], raw, cosine, sine, *chunks[:near])
 
     far = len(masks) - near
     block = pl.pallas_call(
-        functools.partial(last_kernel, far, splits, group, 6 + near),
+        functools.partial(last_kernel, far, splits, group),
         out_shape=shape((share, group * HEAD_DIM), bf16),
-        in_specs=[SMEM] + [VMEM] * (1 + far + splits + 4),
+        in_specs=[VMEM] * (2 + far + splits + 4),
         out_specs=VMEM,
         scratch_shapes=[
             pltpu.VMEM((far, span, HEAD_DIM), bf16),
@@ -317,8 +328,8 @@
             pltpu.VMEM((count, HEAD_DIM), f32),
         ],
         name="last",
-        compiler_params=room(20),
-    )(meta, query, *chunks[near:], *fresh, bias, top, mass, acc)
+        compiler_params=room(14),
+    )(filled[near:], query, *chunks[near:], *fresh, bias, top, mass, acc)
 
     blocks = [block] + [swap(block, i * splits * trees, size) for i in range(1, heads)]
     blocks = [
@@ -342,11 +353,11 @@
         return pl.pallas_call(
             functools.partial(out_kernel, splits, trees, heads, step),
             out_shape=shape((rows, out_width), dtype),
-            in_specs=[SMEM] + [VMEM] * (len(blocks) + 1),
+            in_specs=[VMEM] * (len(blocks) + 1),
             out_specs=VMEM,
             name="output",
             compiler_params=room(12),
-        )(meta, *blocks, weight)
+        )(*blocks, weight)
 
     total = None
     arrived = []

time: 133 us -> 134 us (level)
  starting transfers between devices: 33.7 us -> 44.4 us
  local copies, waits for them, and re-layouts: 9.61 us -> 6.24 us
  Pallas kernels: 22 us -> 19 us
  waiting for transfers between devices: 60.8 us -> 58.2 us
    ppermute x38, starting transfers between devices: 32.2 us -> 42.8 us  [swap(): return lax.ppermute(value, 'seq', [(i, i ^ mask) for i in range(size)])]
    ppermute x38, waiting for transfers between devices: 58 us -> 54.9 us  [swap(): return lax.ppermute(value, 'seq', [(i, i ^ mask) for i in range(size)])]
    unnamed x34 -> x26, local copies, waits for them, and re-layouts: 8.1 us -> 5.27 us
    pallas_call x3, Pallas kernels: 16.2 us -> 14.3 us  [the longest x1 9.25 us: local(): attend(filled[:near], raw, cosine, sine, *chunks[:near])]
    add x2 -> x1, other arithmetic: 1.61 us -> 0.07 us  [local(): keep = keep + rest.astype(f32)]
  transfers between devices with their start and end apart: 39 -> 39, of which waited for: 13 -> 14; matrix products, arithmetic and copies ran while one was open for 5% -> 4% of each run, Pallas kernels for 8% -> 10%
where the time goes in v2:
time: 134 us
  waiting for transfers between devices  58.2 us (43%)
  starting transfers between devices  44.4 us (33%)
  Pallas kernels  19 us (14%)
  local copies, waits for them, and re-layouts  6.24 us (5%)
  other arithmetic  4.1 us (3%)
    ppermute x38, waiting for transfers between devices, swap(): return lax.ppermute(value, 'seq', [(i, i ^ mask) for i in range(size)])  54.9 us
    ppermute x38, starting transfers between devices, swap(): return lax.ppermute(value, 'seq', [(i, i ^ mask) for i in range(size)])  42.8 us
    pallas_call x1, Pallas kernels, local(): attend(filled[:near], raw, cosine, sine, *chunks[:near])  9.25 us
    unnamed x26, local copies, waits for them, and re-layouts  5.27 us
    ppermute x1, waiting for transfers between devices, local(): lax.ppermute(product(step, bf16), 'head', [(i, i ^ step) for i in range(s...  3.37 us
    pallas_call x1, Pallas kernels, local(): keep, low_send, high_send = project(states, w_query, w_key, w_value)  3.26 us
    pallas_call x1, Pallas kernels, local(): pl.pallas_call(functools.partial(pack_kernel, splits, trees, [0] + order)...  3.11 us
  transfers between devices with their start and end apart: 39, of which 14 were waited for; matrix products, arithmetic and copies ran while one was open for 4% of the time, Pallas kernels for 10%

profile of v2, /device:TPU:0, one launch (start us, length us, event | category | flops | bytes accessed | tf_op | source)
XLA Modules:
  0.0 133.9 jit_solution(11325361521096046143)
XLA Ops:
  0.0 2.2 %copy-done.2 = bf16[512,4096]{1,0:T(8,128)(2,1)S(1)} copy-done((bf16[512,4096]{1,0:T(8,128)(2,1)S(1)}, bf16[512,4096]{1,0:T(8,128)(2,1)}, u32[]{:S(2)}) %copy-start.2) | copy-done | bytes 4194328
  2.2 1.0 copy-done.3
  3.2 1.0 copy-done.4
  4.3 0.9 copy-done.6
  5.2 3.3 %project.1 = (f32[8,64,1280]{2,1,0:T(8,128)S(1)}, f32[4,64,1280]{2,1,0:T(8,128)}, f32[4,64,1280]{2,1,0:T(8,128)}) custom-call(bf16[256,512]{1,0:T(8,128)(2,1)S(1)} %copy-done.6, bf16[512,4096]{1,0:T(8,128)(2,1)S(1)} %copy-done.2, bf16[512,512]{1,0:T(8,128)(2,1)S(1)} %copy-done.3, bf16[512,512]{1,0:T(8,128)(2,1)S(1)} %copy-done.4), custom_call_target="tpu_custom_call" | custom-call | tf_op jit(solution)/shard_map/project/pallas_call | solution.py:233
  9.0 3.1 %pack.1 = (bf16[2,512,128]{2,1,0:T(8,128)(2,1)}, bf16[2,512,128]{2,1,0:T(8,128)(2,1)}, bf16[2,512,128]{2,1,0:T(8,128)(2,1)}, bf16[2,512,128]{2,1,0:T(8,128)(2,1)...) custom-call(bf16[2,512,512]{2,1,0:T(8,128)(2,1)} %key_ref.1, ...), custom_call_target="tpu_custom_call" | custom-call | tf_op jit(solution)/shard_map/pack/pallas_call | solution.py:255
  12.7 4.6 %collective-permute-start.8 = (bf16[2,512,128]{2,1,0:T(8,128)(2,1)}, bf16[2,512,128]{2,1,0:T(8,128)(2,1)S(1)}, u32[]{:S(2)}, u32[]{:S(2)}) collective-permute-start(bf16[2,512,128]{2,1,0:T(8,128)(2,1)} %get-tuple-element.35), channel_id=1, source_target_pairs={{0,20},{2,22},{4,16},{6,18},{8,28},{10,30},{12,24},{14,26},{16,4},... | collective-permute-start | bytes 786440 | tf_op jit(solution)/shard_map/ppermute | solution.py:36
  17.3 1.5 %collective-permute-start.10 = (bf16[2,512,128]{2,1,0:T(8,128)(2,1)}, bf16[2,512,128]{2,1,0:T(8,128)(2,1)S(1)}, u32[]{:S(2)}, u32[]{:S(2)}) collective-permute-start(bf16[2,512,128]{2,1,0:T(8,128)(2,1)} %get-tuple-element.36), channel_id=1, source_target_pairs={{0,12},{2,14},{4,8},{6,10},{8,4},{10,6},{12,0},{14,2},{16,28},{18,... | collective-permute-start | bytes 786440 | tf_op jit(solution)/shard_map/ppermute | solution.py:36
  21.3 2.1 %add_convert_fusion = (f16[4,64,1280]{2,1,0:T(8,128)(2,1)S(1)}, f32[4,64,1280]{2,1,0:T(8,128)S(1)}) fusion(f32[4,64,1280]{2,1,0:T(8,128)} %collective-permute-done.1, f32[8,64,1280]{2,1,0:T(8,128)S(1)} %get-tuple-element.26, f32[4,64,1280]{2,1,0:T(8,128)} %collective-permute-done), kind=kLoop, calls=%fused_computation | loop fusion | flops 983040 | bytes 7208960 | tf_op jit(solution)/shard_map/convert_element_type | solution.py:242
  23.5 1.6 %collective-permute-start.2 = (f16[2,64,1280]{2,1,0:T(8,128)(2,1)S(1)}, f16[2,64,1280]{2,1,0:T(8,128)(2,1)S(1)}, u32[]{:S(2)}, u32[]{:S(2)}) collective-permute-start(f16[2,64,1280]{2,1,0:T(8,128)(2,1)S(1)} %get-tuple-element.52), channel_id=1, source_target_pairs={{0,4},{2,6},{4,0},{6,2},{8,12},{10,14},{12,8},{14,10},{16,20},{18,... | collective-permute-start | bytes 983048 | tf_op jit(solution)/shard_map/ppermute | solution.py:36
  25.7 12.6 %collective-permute-done.2 = f16[2,64,1280]{2,1,0:T(8,128)(2,1)S(1)} collective-permute-done((f16[2,64,1280]{2,1,0:T(8,128)(2,1)S(1)}, f16[2,64,1280]{2,1,0:T(8,128)(2,1)S(1)}, u32[]{:S(2)}, u32[]{:S(2)}) %collective-permute-start.2) | collective-permute-done | bytes 327712 | tf_op jit(solution)/shard_map/ppermute | solution.py:36
  39.2 6.1 %collective-permute-done.4 = f16[2,64,1280]{2,1,0:T(8,128)(2,1)S(1)} collective-permute-done((f16[2,64,1280]{2,1,0:T(8,128)(2,1)S(1)}, f16[2,64,1280]{2,1,0:T(8,128)(2,1)S(1)}, u32[]{:S(2)}, u32[]{:S(2)}) %collective-permute-start.4) | collective-permute-done | bytes 327712 | tf_op jit(solution)/shard_map/ppermute | solution.py:36
  45.9 2.7 %collective-permute-start.5 = (f16[1,64,1280]{2,1,0:T(8,128)(2,1)S(1)}, f16[1,64,1280]{2,1,0:T(8,128)(2,1)S(1)}, u32[]{:S(2)}, u32[]{:S(2)}) collective-permute-start(f16[1,64,1280]{2,1,0:T(8,128)(2,1)S(1)} %fusion.7), channel_id=1, source_target_pairs={{0,16},{2,18},{4,20},{6,22},{8,24},{10,26},{12,28},{14,30},{16,0},... | collective-permute-start | bytes 491528 | tf_op jit(solution)/shard_map/ppermute | solution.py:36
  48.5 6.1 %collective-permute-done.6 = f16[1,64,1280]{2,1,0:T(8,128)(2,1)S(1)} collective-permute-done((f16[1,64,1280]{2,1,0:T(8,128)(2,1)S(1)}, f16[1,64,1280]{2,1,0:T(8,128)(2,1)S(1)}, u32[]{:S(2)}, u32[]{:S(2)}) %collective-permute-start.6) | collective-permute-done | bytes 163872 | tf_op jit(solution)/shard_map/ppermute | solution.py:36
  54.6 1.3 collective-permute-start.12
  56.7 13.7 %collective-permute-start.16 = (bf16[2,512,128]{2,1,0:T(8,128)(2,1)S(1)}, bf16[2,512,128]{2,1,0:T(8,128)(2,1)S(1)}, u32[]{:S(2)}, u32[]{:S(2)}) collective-permute-start(bf16[2,512,128]{2,1,0:T(8,128)(2,1)S(1)} %copy-done.9), channel_id=1, source_target_pairs={{0,8},{2,10},{4,12},{6,14},{8,0},{10,2},{12,4},{14,6},{16,24},{18,... | collective-permute-start | bytes 786440 | tf_op jit(solution)/shard_map/ppermute | solution.py:36
  70.4 1.6 %collective-permute-start.18 = (bf16[2,512,128]{2,1,0:T(8,128)(2,1)S(1)}, bf16[2,512,128]{2,1,0:T(8,128)(2,1)S(1)}, u32[]{:S(2)}, u32[]{:S(2)}) collective-permute-start(bf16[2,512,128]{2,1,0:T(8,128)(2,1)S(1)} %copy-done.8), channel_id=1, source_target_pairs={{0,4},{2,6},{4,0},{6,2},{8,12},{10,14},{12,8},{14,10},{16,20},{18,... | collective-permute-start | bytes 786440 | tf_op jit(solution)/shard_map/ppermute | solution.py:36
  72.1 13.1 %collective-permute-done.14.refs_8_ = bf16[2,512,128]{2,1,0:T(8,128)(2,1)S(1)} collective-permute-done((bf16[2,512,128]{2,1,0:T(8,128)(2,1)S(1)}, bf16[2,512,128]{2,1,0:T(8,128)(2,1)S(1)}, u32[]{:S(2)}, u32[]{:S(2)}) %collective-permute-start.14) | collective-permute-done | bytes 262176 | tf_op jit(solution)/shard_map/ppermute | solution.py:36
  88.3 9.2 %cache.1 = (bf16[512,128]{1,0:T(8,128)(2,1)S(1)}, f32[512,128]{1,0:T(8,128)S(1)}, f32[512,128]{1,0:T(8,128)S(1)}, f32[512,128]{1,0:T(8,128)S(1)}) custom-call(f32[14,512]{1,0:T(8,128)S(1)} %bitcast.32, f32[64,1280]{1,0:T(8,128)S(1)} %fusion.9.raw, f32[64,128]{1,0:T(8,128)S(1)} %get-tuple-element.59.cosine, f32[64,128]{1,0:T(8,128)S(1)} %get-tuple-element.48.sine, ...), custom_call_target="tpu_custom_call" | custom-call | tf_op jit(solution)/shard_map/cache/pallas_call | solution.py:314
  97.6 1.9 %last.1.refs_0_ = bf16[64,1024]{1,0:T(8,128)(2,1)S(1)} custom-call(f32[2,512]{1,0:T(2,128)S(1)} %slice.69.filled, bf16[512,128]{1,0:T(8,128)(2,1)S(1)} %get-tuple-element.41.query, bf16[2,512,128]{2,1,0:T(8,128)(2,1)S(1)} %collective-permute-done.20.refs_0_, bf16[2,512,128]{2,1,0:T(8,128)(2,1)S(1)} %collective-permute-done.21.refs_1_, ...), custom_call_target="tpu_custom_call" | custom-call | tf_op jit(solution)/shard_map/last/pallas_call | solution.py:317
  99.5 1.6 %collective-permute-start.24 = (bf16[64,1024]{1,0:T(8,128)(2,1)S(1)}, bf16[64,1024]{1,0:T(8,128)(2,1)S(1)}, u32[]{:S(2)}, u32[]{:S(2)}) collective-permute-start(bf16[64,1024]{1,0:T(8,128)(2,1)S(1)} %last.1.refs_0_), channel_id=1, source_target_pairs={{0,4},{2,6},{4,0},{6,2},{8,12},{10,14},{12,8},{14,10},{16,20},{18,... | collective-permute-start | bytes 393224 | tf_op jit(solution)/shard_map/ppermute | solution.py:36
  101.1 4.2 %collective-permute-start.26 = (bf16[64,1024]{1,0:T(8,128)(2,1)S(1)}, bf16[64,1024]{1,0:T(8,128)(2,1)S(1)}, u32[]{:S(2)}, u32[]{:S(2)}) collective-permute-start(bf16[64,1024]{1,0:T(8,128)(2,1)S(1)} %last.1.refs_0_), channel_id=1, source_target_pairs={{0,8},{2,10},{4,12},{6,14},{8,0},{10,2},{12,4},{14,6},{16,24},{18,... | collective-permute-start | bytes 393224 | tf_op jit(solution)/shard_map/ppermute | solution.py:36
  105.2 1.1 collective-permute-start.30
  106.3 1.5 %collective-permute-start.34 = (bf16[64,1024]{1,0:T(8,128)(2,1)S(1)}, bf16[64,1024]{1,0:T(8,128)(2,1)S(1)}, u32[]{:S(2)}, u32[]{:S(2)}) collective-permute-start(bf16[64,1024]{1,0:T(8,128)(2,1)S(1)} %last.1.refs_0_), channel_id=1, source_target_pairs={{0,24},{2,26},{4,28},{6,30},{8,16},{10,18},{12,20},{14,22},{16,8},... | collective-permute-start | bytes 393224 | tf_op jit(solution)/shard_map/ppermute | solution.py:36
  108.0 1.1 collective-permute-done.26.refs_4_
  109.6 8.5 %collective-permute-done.30.refs_8_ = bf16[64,1024]{1,0:T(8,128)(2,1)S(1)} collective-permute-done((bf16[64,1024]{1,0:T(8,128)(2,1)S(1)}, bf16[64,1024]{1,0:T(8,128)(2,1)S(1)}, u32[]{:S(2)}, u32[]{:S(2)}) %collective-permute-start.30) | collective-permute-done | bytes 131104 | tf_op jit(solution)/shard_map/ppermute | solution.py:36
  118.6 1.5 %collective-permute-start.36 = (bf16[64,1024]{1,0:T(8,128)(2,1)S(1)}, bf16[64,1024]{1,0:T(8,128)(2,1)S(1)}, u32[]{:S(2)}, u32[]{:S(2)}) collective-permute-start(bf16[64,1024]{1,0:T(8,128)(2,1)S(1)} %collective-permute-done.34.refs_12_), channel_id=1, source_target_pairs={{0,4},{2,6},{4,0},{6,2},{8,12},{10,14},{12,8},{14,10},{16,20},{18,... | collective-permute-start | bytes 393224 | tf_op jit(solution)/shard_map/ppermute | solution.py:36
  120.8 3.4 %collective-permute-done.32.refs_10_ = bf16[64,1024]{1,0:T(8,128)(2,1)S(1)} collective-permute-done((bf16[64,1024]{1,0:T(8,128)(2,1)S(1)}, bf16[64,1024]{1,0:T(8,128)(2,1)S(1)}, u32[]{:S(2)}, u32[]{:S(2)}) %collective-permute-start.32) | collective-permute-done | bytes 131104 | tf_op jit(solution)/shard_map/ppermute | solution.py:36
  124.1 1.4 %collective-permute-done.36.refs_14_ = bf16[64,1024]{1,0:T(8,128)(2,1)S(1)} collective-permute-done((bf16[64,1024]{1,0:T(8,128)(2,1)S(1)}, bf16[64,1024]{1,0:T(8,128)(2,1)S(1)}, u32[]{:S(2)}, u32[]{:S(2)}) %collective-permute-start.36) | collective-permute-done | bytes 131104 | tf_op jit(solution)/shard_map/ppermute | solution.py:36
  125.6 1.3 collective-permute-done.37.refs_15_
  127.6 1.5 %collective-permute-start.38 = (bf16[256,256]{1,0:T(8,128)(2,1)S(1)}, bf16[256,256]{1,0:T(8,128)(2,1)S(1)}, u32[]{:S(2)}, u32[]{:S(2)}) collective-permute-start(bf16[256,256]{1,0:T(8,128)(2,1)S(1)} %output.3), channel_id=1, source_target_pairs={{0,1},{1,0},{2,3},{3,2},{4,5},{5,4},{6,7},{7,6},{8,9},{9,8},{10,11... | collective-permute-start | bytes 393224 | tf_op jit(solution)/shard_map/ppermute | solution.py:367
  129.9 3.4 %collective-permute-done.38 = bf16[256,256]{1,0:T(8,128)(2,1)S(1)} collective-permute-done((bf16[256,256]{1,0:T(8,128)(2,1)S(1)}, bf16[256,256]{1,0:T(8,128)(2,1)S(1)}, u32[]{:S(2)}, u32[]{:S(2)}) %collective-permute-start.38) | collective-permute-done | bytes 131104 | tf_op jit(solution)/shard_map/ppermute | solution.py:367
  (103 shorter events, 12.9 us)
Async XLA Ops:
  8.5 12.8 %collective-permute-start.1 = (f32[4,64,1280]{2,1,0:T(8,128)}, f32[4,64,1280]{2,1,0:T(8,128)}, u32[]{:S(2)}, u32[]{:S(2)}) collective-permute-start(f32[4,64,1280]{2,1,0:T(8,128)} %get-tuple-element.28), channel_id=1, source_target_pairs={{0,2},{2,0},{4,6},{6,4},{8,10},{10,8},{12,14},{14,12},{16,18},{18,... | collective-permute-start | bytes 3932168 | tf_op jit(solution)/shard_map/ppermute | solution.py:36
  9.0 12.3 %collective-permute-start = (f32[4,64,1280]{2,1,0:T(8,128)}, f32[4,64,1280]{2,1,0:T(8,128)}, u32[]{:S(2)}, u32[]{:S(2)}) collective-permute-start(f32[4,64,1280]{2,1,0:T(8,128)} %get-tuple-element.27), channel_id=1, source_target_pairs={{0,2},{2,0},{4,6},{6,4},{8,10},{10,8},{12,14},{14,12},{16,18},{18,... | collective-permute-start | bytes 3932168 | tf_op jit(solution)/shard_map/ppermute | solution.py:36
  12.1 44.5 %collective-permute-start.7 = (bf16[2,512,128]{2,1,0:T(8,128)(2,1)}, bf16[2,512,128]{2,1,0:T(8,128)(2,1)S(1)}, u32[]{:S(2)}, u32[]{:S(2)}) collective-permute-start(bf16[2,512,128]{2,1,0:T(8,128)(2,1)} %get-tuple-element.34.refs_0_), channel_id=1, source_target_pairs={{0,2},{2,0},{4,6},{6,4},{8,10},{10,8},{12,14},{14,12},{16,18},{18,... | collective-permute-start | bytes 786440 | tf_op jit(solution)/shard_map/ppermute | solution.py:36
  12.7 57.7 %collective-permute-start.8 = (bf16[2,512,128]{2,1,0:T(8,128)(2,1)}, bf16[2,512,128]{2,1,0:T(8,128)(2,1)S(1)}, u32[]{:S(2)}, u32[]{:S(2)}) collective-permute-start(bf16[2,512,128]{2,1,0:T(8,128)(2,1)} %get-tuple-element.35), channel_id=1, source_target_pairs={{0,20},{2,22},{4,16},{6,18},{8,28},{10,30},{12,24},{14,26},{16,4},... | collective-permute-start | bytes 786440 | tf_op jit(solution)/shard_map/ppermute | solution.py:36
  17.3 54.7 %collective-permute-start.10 = (bf16[2,512,128]{2,1,0:T(8,128)(2,1)}, bf16[2,512,128]{2,1,0:T(8,128)(2,1)S(1)}, u32[]{:S(2)}, u32[]{:S(2)}) collective-permute-start(bf16[2,512,128]{2,1,0:T(8,128)(2,1)} %get-tuple-element.36), channel_id=1, source_target_pairs={{0,12},{2,14},{4,8},{6,10},{8,4},{10,6},{12,0},{14,2},{16,28},{18,... | collective-permute-start | bytes 786440 | tf_op jit(solution)/shard_map/ppermute | solution.py:36
  23.5 14.9 %collective-permute-start.2 = (f16[2,64,1280]{2,1,0:T(8,128)(2,1)S(1)}, f16[2,64,1280]{2,1,0:T(8,128)(2,1)S(1)}, u32[]{:S(2)}, u32[]{:S(2)}) collective-permute-start(f16[2,64,1280]{2,1,0:T(8,128)(2,1)S(1)} %get-tuple-element.52), channel_id=1, source_target_pairs={{0,4},{2,6},{4,0},{6,2},{8,12},{10,14},{12,8},{14,10},{16,20},{18,... | collective-permute-start | bytes 983048 | tf_op jit(solution)/shard_map/ppermute | solution.py:36
  25.2 20.1 %collective-permute-start.4 = (f16[2,64,1280]{2,1,0:T(8,128)(2,1)S(1)}, f16[2,64,1280]{2,1,0:T(8,128)(2,1)S(1)}, u32[]{:S(2)}, u32[]{:S(2)}) collective-permute-start(f16[2,64,1280]{2,1,0:T(8,128)(2,1)S(1)} %get-tuple-element.51), channel_id=1, source_target_pairs={{0,4},{2,6},{4,0},{6,2},{8,12},{10,14},{12,8},{14,10},{16,20},{18,... | collective-permute-start | bytes 983048 | tf_op jit(solution)/shard_map/ppermute | solution.py:36
  38.6 7.2 %collective-permute-start.3 = (f16[1,64,1280]{2,1,0:T(8,128)(2,1)S(1)}, f16[1,64,1280]{2,1,0:T(8,128)(2,1)S(1)}, u32[]{:S(2)}, u32[]{:S(2)}) collective-permute-start(f16[1,64,1280]{2,1,0:T(8,128)(2,1)S(1)} %get-tuple-element.56), channel_id=1, source_target_pairs={{0,8},{2,10},{4,12},{6,14},{8,0},{10,2},{12,4},{14,6},{16,24},{18,... | collective-permute-start | bytes 491528 | tf_op jit(solution)/shard_map/ppermute | solution.py:36
  45.3 9.3 %collective-permute-start.6 = (f16[1,64,1280]{2,1,0:T(8,128)(2,1)S(1)}, f16[1,64,1280]{2,1,0:T(8,128)(2,1)S(1)}, u32[]{:S(2)}, u32[]{:S(2)}) collective-permute-start(f16[1,64,1280]{2,1,0:T(8,128)(2,1)S(1)} %get-tuple-element.55), channel_id=1, source_target_pairs={{0,8},{2,10},{4,12},{6,14},{8,0},{10,2},{12,4},{14,6},{16,24},{18,... | collective-permute-start | bytes 491528 | tf_op jit(solution)/shard_map/ppermute | solution.py:36
  45.9 10.7 %collective-permute-start.5 = (f16[1,64,1280]{2,1,0:T(8,128)(2,1)S(1)}, f16[1,64,1280]{2,1,0:T(8,128)(2,1)S(1)}, u32[]{:S(2)}, u32[]{:S(2)}) collective-permute-start(f16[1,64,1280]{2,1,0:T(8,128)(2,1)S(1)} %fusion.7), channel_id=1, source_target_pairs={{0,16},{2,18},{4,20},{6,22},{8,24},{10,26},{12,28},{14,30},{16,0},... | collective-permute-start | bytes 491528 | tf_op jit(solution)/shard_map/ppermute | solution.py:36
  54.6 17.4 %collective-permute-start.12 = (bf16[2,512,128]{2,1,0:T(8,128)(2,1)S(1)}, bf16[2,512,128]{2,1,0:T(8,128)(2,1)S(1)}, u32[]{:S(2)}, u32[]{:S(2)}) collective-permute-start(bf16[2,512,128]{2,1,0:T(8,128)(2,1)S(1)} %copy-done.11), channel_id=1, source_target_pairs={{0,28},{2,30},{4,24},{6,26},{8,20},{10,22},{12,16},{14,18},{16,12}... | collective-permute-start | bytes 786440 | tf_op jit(solution)/shard_map/ppermute | solution.py:36
  56.6 28.7 %collective-permute-start.14 = (bf16[2,512,128]{2,1,0:T(8,128)(2,1)S(1)}, bf16[2,512,128]{2,1,0:T(8,128)(2,1)S(1)}, u32[]{:S(2)}, u32[]{:S(2)}) collective-permute-start(bf16[2,512,128]{2,1,0:T(8,128)(2,1)S(1)} %copy-done.10), channel_id=1, source_target_pairs={{0,16},{2,18},{4,20},{6,22},{8,24},{10,26},{12,28},{14,30},{16,0},... | collective-permute-start | bytes 786440 | tf_op jit(solution)/shard_map/ppermute | solution.py:36
  56.7 28.6 %collective-permute-start.16 = (bf16[2,512,128]{2,1,0:T(8,128)(2,1)S(1)}, bf16[2,512,128]{2,1,0:T(8,128)(2,1)S(1)}, u32[]{:S(2)}, u32[]{:S(2)}) collective-permute-start(bf16[2,512,128]{2,1,0:T(8,128)(2,1)S(1)} %copy-done.9), channel_id=1, source_target_pairs={{0,8},{2,10},{4,12},{6,14},{8,0},{10,2},{12,4},{14,6},{16,24},{18,... | collective-permute-start | bytes 786440 | tf_op jit(solution)/shard_map/ppermute | solution.py:36
  70.4 15.5 %collective-permute-start.18 = (bf16[2,512,128]{2,1,0:T(8,128)(2,1)S(1)}, bf16[2,512,128]{2,1,0:T(8,128)(2,1)S(1)}, u32[]{:S(2)}, u32[]{:S(2)}) collective-permute-start(bf16[2,512,128]{2,1,0:T(8,128)(2,1)S(1)} %copy-done.8), channel_id=1, source_target_pairs={{0,4},{2,6},{4,0},{6,2},{8,12},{10,14},{12,8},{14,10},{16,20},{18,... | collective-permute-start | bytes 786440 | tf_op jit(solution)/shard_map/ppermute | solution.py:36
  72.0 14.0 %collective-permute-start.20 = (bf16[2,512,128]{2,1,0:T(8,128)(2,1)S(1)}, bf16[2,512,128]{2,1,0:T(8,128)(2,1)S(1)}, u32[]{:S(2)}, u32[]{:S(2)}) collective-permute-start(bf16[2,512,128]{2,1,0:T(8,128)(2,1)S(1)} %copy-done.7), channel_id=1, source_target_pairs={{0,24},{2,26},{4,28},{6,30},{8,16},{10,18},{12,20},{14,22},{16,8},... | collective-permute-start | bytes 786440 | tf_op jit(solution)/shard_map/ppermute | solution.py:36
  72.0 14.5 %collective-permute-start.9 = (bf16[2,512,128]{2,1,0:T(8,128)(2,1)S(1)}, bf16[2,512,128]{2,1,0:T(8,128)(2,1)S(1)}, u32[]{:S(2)}, u32[]{:S(2)}) collective-permute-start(bf16[2,512,128]{2,1,0:T(8,128)(2,1)S(1)} %collective-permute-done.8.refs_2_), channel_id=1, source_target_pairs={{0,2},{2,0},{4,6},{6,4},{8,10},{10,8},{12,14},{14,12},{16,18},{18,... | collective-permute-start | bytes 786440 | tf_op jit(solution)/shard_map/ppermute | solution.py:36
  86.8 10.8 %collective-permute-start.21 = (bf16[2,512,128]{2,1,0:T(8,128)(2,1)S(1)}, bf16[2,512,128]{2,1,0:T(8,128)(2,1)S(1)}, u32[]{:S(2)}, u32[]{:S(2)}) collective-permute-start(bf16[2,512,128]{2,1,0:T(8,128)(2,1)S(1)} %collective-permute-done.20.refs_0_), channel_id=1, source_target_pairs={{0,2},{2,0},{4,6},{6,4},{8,10},{10,8},{12,14},{14,12},{16,18},{18,... | collective-permute-start | bytes 786440 | tf_op jit(solution)/shard_map/ppermute | solution.py:36
  87.1 10.4 %collective-permute-start.22 = (bf16[2,64,128]{2,1,0:T(8,128)(2,1)S(1)}, bf16[2,64,128]{2,1,0:T(8,128)(2,1)S(1)}, u32[]{:S(2)}, u32[]{:S(2)}) collective-permute-start(bf16[2,64,128]{2,1,0:T(8,128)(2,1)S(1)} %pad_maximum_fusion.2.refs_2_), channel_id=1, source_target_pairs={{0,2},{2,0},{4,6},{6,4},{8,10},{10,8},{12,14},{14,12},{16,18},{18,... | collective-permute-start | bytes 98312 | tf_op jit(solution)/shard_map/ppermute | solution.py:36
  99.5 8.3 %collective-permute-start.24 = (bf16[64,1024]{1,0:T(8,128)(2,1)S(1)}, bf16[64,1024]{1,0:T(8,128)(2,1)S(1)}, u32[]{:S(2)}, u32[]{:S(2)}) collective-permute-start(bf16[64,1024]{1,0:T(8,128)(2,1)S(1)} %last.1.refs_0_), channel_id=1, source_target_pairs={{0,4},{2,6},{4,0},{6,2},{8,12},{10,14},{12,8},{14,10},{16,20},{18,... | collective-permute-start | bytes 393224 | tf_op jit(solution)/shard_map/ppermute | solution.py:36
  101.1 8.1 %collective-permute-start.26 = (bf16[64,1024]{1,0:T(8,128)(2,1)S(1)}, bf16[64,1024]{1,0:T(8,128)(2,1)S(1)}, u32[]{:S(2)}, u32[]{:S(2)}) collective-permute-start(bf16[64,1024]{1,0:T(8,128)(2,1)S(1)} %last.1.refs_0_), channel_id=1, source_target_pairs={{0,8},{2,10},{4,12},{6,14},{8,0},{10,2},{12,4},{14,6},{16,24},{18,... | collective-permute-start | bytes 393224 | tf_op jit(solution)/shard_map/ppermute | solution.py:36
  105.2 3.9 %collective-permute-start.23 = (bf16[64,1024]{1,0:T(8,128)(2,1)S(1)}, bf16[64,1024]{1,0:T(8,128)(2,1)S(1)}, u32[]{:S(2)}, u32[]{:S(2)}) collective-permute-start(bf16[64,1024]{1,0:T(8,128)(2,1)S(1)} %last.1.refs_0_), channel_id=1, source_target_pairs={{0,2},{2,0},{4,6},{6,4},{8,10},{10,8},{12,14},{14,12},{16,18},{18,... | collective-permute-start | bytes 393224 | tf_op jit(solution)/shard_map/ppermute | solution.py:36
  105.2 12.9 %collective-permute-start.30 = (bf16[64,1024]{1,0:T(8,128)(2,1)S(1)}, bf16[64,1024]{1,0:T(8,128)(2,1)S(1)}, u32[]{:S(2)}, u32[]{:S(2)}) collective-permute-start(bf16[64,1024]{1,0:T(8,128)(2,1)S(1)} %last.1.refs_0_), channel_id=1, source_target_pairs={{0,16},{2,18},{4,20},{6,22},{8,24},{10,26},{12,28},{14,30},{16,0},... | collective-permute-start | bytes 393224 | tf_op jit(solution)/shard_map/ppermute | solution.py:36
  106.3 12.3 %collective-permute-start.34 = (bf16[64,1024]{1,0:T(8,128)(2,1)S(1)}, bf16[64,1024]{1,0:T(8,128)(2,1)S(1)}, u32[]{:S(2)}, u32[]{:S(2)}) collective-permute-start(bf16[64,1024]{1,0:T(8,128)(2,1)S(1)} %last.1.refs_0_), channel_id=1, source_target_pairs={{0,24},{2,26},{4,28},{6,30},{8,16},{10,18},{12,20},{14,22},{16,8},... | collective-permute-start | bytes 393224 | tf_op jit(solution)/shard_map/ppermute | solution.py:36
  107.8 12.4 %collective-permute-start.25 = (bf16[64,1024]{1,0:T(8,128)(2,1)S(1)}, bf16[64,1024]{1,0:T(8,128)(2,1)S(1)}, u32[]{:S(2)}, u32[]{:S(2)}) collective-permute-start(bf16[64,1024]{1,0:T(8,128)(2,1)S(1)} %collective-permute-done.24.refs_2_), channel_id=1, source_target_pairs={{0,2},{2,0},{4,6},{6,4},{8,10},{10,8},{12,14},{14,12},{16,18},{18,... | collective-permute-start | bytes 393224 | tf_op jit(solution)/shard_map/ppermute | solution.py:36
  109.1 11.0 %collective-permute-start.27 = (bf16[64,1024]{1,0:T(8,128)(2,1)S(1)}, bf16[64,1024]{1,0:T(8,128)(2,1)S(1)}, u32[]{:S(2)}, u32[]{:S(2)}) collective-permute-start(bf16[64,1024]{1,0:T(8,128)(2,1)S(1)} %collective-permute-done.26.refs_4_), channel_id=1, source_target_pairs={{0,2},{2,0},{4,6},{6,4},{8,10},{10,8},{12,14},{14,12},{16,18},{18,... | collective-permute-start | bytes 393224 | tf_op jit(solution)/shard_map/ppermute | solution.py:36
  109.1 11.6 %collective-permute-start.28 = (bf16[64,1024]{1,0:T(8,128)(2,1)S(1)}, bf16[64,1024]{1,0:T(8,128)(2,1)S(1)}, u32[]{:S(2)}, u32[]{:S(2)}) collective-permute-start(bf16[64,1024]{1,0:T(8,128)(2,1)S(1)} %collective-permute-done.26.refs_4_), channel_id=1, source_target_pairs={{0,4},{2,6},{4,0},{6,2},{8,12},{10,14},{12,8},{14,10},{16,20},{18,... | collective-permute-start | bytes 393224 | tf_op jit(solution)/shard_map/ppermute | solution.py:36
  118.1 6.0 %collective-permute-start.32 = (bf16[64,1024]{1,0:T(8,128)(2,1)S(1)}, bf16[64,1024]{1,0:T(8,128)(2,1)S(1)}, u32[]{:S(2)}, u32[]{:S(2)}) collective-permute-start(bf16[64,1024]{1,0:T(8,128)(2,1)S(1)} %collective-permute-done.30.refs_8_), channel_id=1, source_target_pairs={{0,4},{2,6},{4,0},{6,2},{8,12},{10,14},{12,8},{14,10},{16,20},{18,... | collective-permute-start | bytes 393224 | tf_op jit(solution)/shard_map/ppermute | solution.py:36
  118.6 6.9 %collective-permute-start.36 = (bf16[64,1024]{1,0:T(8,128)(2,1)S(1)}, bf16[64,1024]{1,0:T(8,128)(2,1)S(1)}, u32[]{:S(2)}, u32[]{:S(2)}) collective-permute-start(bf16[64,1024]{1,0:T(8,128)(2,1)S(1)} %collective-permute-done.34.refs_12_), channel_id=1, source_target_pairs={{0,4},{2,6},{4,0},{6,2},{8,12},{10,14},{12,8},{14,10},{16,20},{18,... | collective-permute-start | bytes 393224 | tf_op jit(solution)/shard_map/ppermute | solution.py:36
  120.2 5.4 %collective-permute-start.31 = (bf16[64,1024]{1,0:T(8,128)(2,1)S(1)}, bf16[64,1024]{1,0:T(8,128)(2,1)S(1)}, u32[]{:S(2)}, u32[]{:S(2)}) collective-permute-start(bf16[64,1024]{1,0:T(8,128)(2,1)S(1)} %collective-permute-done.30.refs_8_), channel_id=1, source_target_pairs={{0,2},{2,0},{4,6},{6,4},{8,10},{10,8},{12,14},{14,12},{16,18},{18,... | collective-permute-start | bytes 393224 | tf_op jit(solution)/shard_map/ppermute | solution.py:36
  120.2 5.4 %collective-permute-start.35 = (bf16[64,1024]{1,0:T(8,128)(2,1)S(1)}, bf16[64,1024]{1,0:T(8,128)(2,1)S(1)}, u32[]{:S(2)}, u32[]{:S(2)}) collective-permute-start(bf16[64,1024]{1,0:T(8,128)(2,1)S(1)} %collective-permute-done.34.refs_12_), channel_id=1, source_target_pairs={{0,2},{2,0},{4,6},{6,4},{8,10},{10,8},{12,14},{14,12},{16,18},{18,... | collective-permute-start | bytes 393224 | tf_op jit(solution)/shard_map/ppermute | solution.py:36
  120.7 4.9 %collective-permute-start.29 = (bf16[64,1024]{1,0:T(8,128)(2,1)S(1)}, bf16[64,1024]{1,0:T(8,128)(2,1)S(1)}, u32[]{:S(2)}, u32[]{:S(2)}) collective-permute-start(bf16[64,1024]{1,0:T(8,128)(2,1)S(1)} %collective-permute-done.28.refs_6_), channel_id=1, source_target_pairs={{0,2},{2,0},{4,6},{6,4},{8,10},{10,8},{12,14},{14,12},{16,18},{18,... | collective-permute-start | bytes 393224 | tf_op jit(solution)/shard_map/ppermute | solution.py:36
  127.6 5.6 %collective-permute-start.38 = (bf16[256,256]{1,0:T(8,128)(2,1)S(1)}, bf16[256,256]{1,0:T(8,128)(2,1)S(1)}, u32[]{:S(2)}, u32[]{:S(2)}) collective-permute-start(bf16[256,256]{1,0:T(8,128)(2,1)S(1)} %output.3), channel_id=1, source_target_pairs={{0,1},{1,0},{2,3},{3,2},{4,5},{5,4},{6,7},{7,6},{8,9},{9,8},{10,11... | collective-permute-start | bytes 393224 | tf_op jit(solution)/shard_map/ppermute | solution.py:367
  (20 other events, 226.2 us)

commit v3 on v2

--- a/solution.py
+++ b/solution.py
@@ -242,6 +242,7 @@
         send = (keep[half:] + high.astype(f32)).astype(jnp.float16)
         keep, rest = keep[:half], low
         if bit == 0:
+            low, _ = lax.optimization_barrier((low, send[0, :16, :HEAD_DIM]))
             keep, rest = keep + low, None
         low_send, high_send = send[: half // 2], send[half // 2 :]
     high = swap(send, 1 << (steps - 1), size)
@@ -252,18 +253,22 @@
     order += [h * trees for h in away[:-1]]
     order += list(range(1, trees))
     order += [h * trees for h in away[-1:]]
-    packed = pl.pallas_call(
-        functools.partial(pack_kernel, splits, trees, [0] + order),
-        out_shape=[shape((2, span, HEAD_DIM), bf16)] * units,
-        in_specs=[HBM, HBM],
-        out_specs=[VMEM] * units,
-        scratch_shapes=[pltpu.SemaphoreType.DMA((2 * units,))],
-        name="pack",
-        compiler_params=room(60),
-    )(key_cache, value_cache)
-    held = {0: packed[0]}
-    for spot, unit in enumerate(order):
-        held[unit] = swap(packed[1 + spot], unit * splits, size)
+    held = {}
+    first = len(order) // 2
+    for some in (order[:first], [0] + order[first:]):
+        packed = pl.pallas_call(
+            functools.partial(pack_kernel, splits, trees, some),
+            out_shape=[shape((2, span, HEAD_DIM), bf16)] * len(some),
+            in_specs=[HBM, HBM],
+            out_specs=[VMEM] * len(some),
+            scratch_shapes=[pltpu.SemaphoreType.DMA((2 * len(some),))],
+            name="pack",
+            compiler_params=room(60),
+        )(key_cache, value_cache)
+        for unit, item in zip(some, packed):
+            held[unit] = item
+            if unit:
+                held[unit] = swap(item, unit * splits, size)
 
     w_out, raw = lax.optimization_barrier((w_out, raw))
 

time: 134 us -> 136 us (1.015)
  Pallas kernels: 19 us -> 20.6 us
    pallas_call x1 -> x2, Pallas kernels: 3.11 us -> 4.71 us  [local(): pl.pallas_call(functools.partial(pack_kernel, splits, trees, some), out_s...]
  transfers between devices with their start and end apart: 39 -> 39, of which waited for: 14 -> 14; matrix products, arithmetic and copies ran while one was open for 4% -> 4% of each run, Pallas kernels for 10% -> 11%
where the time goes in v3:
time: 136 us
  waiting for transfers between devices  58.2 us (43%)
  starting transfers between devices  44.3 us (33%)
  Pallas kernels  20.6 us (15%)
  local copies, waits for them, and re-layouts  6.29 us (5%)
  other arithmetic  4.14 us (3%)
    ppermute x38, waiting for transfers between devices, swap(): return lax.ppermute(value, 'seq', [(i, i ^ mask) for i in range(size)])  54.8 us
    ppermute x38, starting transfers between devices, swap(): return lax.ppermute(value, 'seq', [(i, i ^ mask) for i in range(size)])  42.8 us
    pallas_call x1, Pallas kernels, local(): attend(filled[:near], raw, cosine, sine, *chunks[:near])  9.25 us
    unnamed x26, local copies, waits for them, and re-layouts  5.27 us
    pallas_call x2, Pallas kernels, local(): pl.pallas_call(functools.partial(pack_kernel, splits, trees, some), out_s...  4.71 us
    ppermute x1, waiting for transfers between devices, local(): lax.ppermute(product(step, bf16), 'head', [(i, i ^ step) for i in range(s...  3.36 us
    pallas_call x1, Pallas kernels, local(): keep, low_send, high_send = project(states, w_query, w_key, w_value)  3.26 us
  transfers between devices with their start and end apart: 39, of which 14 were waited for; matrix products, arithmetic and copies ran while one was open for 4% of the time, Pallas kernels for 11%

profile of v3, /device:TPU:0, one launch (start us, length us, event | category | flops | bytes accessed | tf_op | source)
XLA Modules:
  0.0 135.6 jit_solution(17687828924550743884)
XLA Ops:
  0.0 2.2 %copy-done.2 = bf16[512,4096]{1,0:T(8,128)(2,1)S(1)} copy-done((bf16[512,4096]{1,0:T(8,128)(2,1)S(1)}, bf16[512,4096]{1,0:T(8,128)(2,1)}, u32[]{:S(2)}) %copy-start.2) | copy-done | bytes 4194328
  2.2 1.0 copy-done.3
  3.2 1.0 copy-done.4
  5.2 3.3 %project.1 = (f32[8,64,1280]{2,1,0:T(8,128)S(1)}, f32[4,64,1280]{2,1,0:T(8,128)}, f32[4,64,1280]{2,1,0:T(8,128)}) custom-call(bf16[256,512]{1,0:T(8,128)(2,1)S(1)} %copy-done.6, bf16[512,4096]{1,0:T(8,128)(2,1)S(1)} %copy-done.2, bf16[512,512]{1,0:T(8,128)(2,1)S(1)} %copy-done.3, bf16[512,512]{1,0:T(8,128)(2,1)S(1)} %copy-done.4), custom_call_target="tpu_custom_call" | custom-call | tf_op jit(solution)/shard_map/project/pallas_call | solution.py:233
  9.0 2.5 %pack.2 = (bf16[2,512,128]{2,1,0:T(8,128)(2,1)}, bf16[2,512,128]{2,1,0:T(8,128)(2,1)}, bf16[2,512,128]{2,1,0:T(8,128)(2,1)}, bf16[2,512,128]{2,1,0:T(8,128)(2,1)}, bf16[2,512,128]{2,1,0:T(8,128)(2,1)}) custom-call(bf16[2,512,512]{2,1,0:T(8,128)(2,1)} %key_ref.3, bf16[2,512,512]{2,1,0:T(8,128)(2,1)} %value_ref.3), custom_call_target="tpu_custom_call" | custom-call | tf_op jit(solution)/shard_map/pack/pallas_call | solution.py:259
  12.1 2.2 %pack.3 = (bf16[2,512,128]{2,1,0:T(8,128)(2,1)}, bf16[2,512,128]{2,1,0:T(8,128)(2,1)}, bf16[2,512,128]{2,1,0:T(8,128)(2,1)}) custom-call(bf16[2,512,512]{2,1,0:T(8,128)(2,1)} %key_ref.3, bf16[2,512,512]{2,1,0:T(8,128)(2,1)} %value_ref.3), custom_call_target="tpu_custom_call" | custom-call | tf_op jit(solution)/shard_map/pack/pallas_call | solution.py:259
  14.3 4.6 %collective-permute-start.8 = (bf16[2,512,128]{2,1,0:T(8,128)(2,1)}, bf16[2,512,128]{2,1,0:T(8,128)(2,1)S(1)}, u32[]{:S(2)}, u32[]{:S(2)}) collective-permute-start(bf16[2,512,128]{2,1,0:T(8,128)(2,1)} %get-tuple-element.35), channel_id=1, source_target_pairs={{0,20},{2,22},{4,16},{6,18},{8,28},{10,30},{12,24},{14,26},{16,4},... | collective-permute-start | bytes 786440 | tf_op jit(solution)/shard_map/ppermute | solution.py:36
  18.9 1.5 %collective-permute-start.10 = (bf16[2,512,128]{2,1,0:T(8,128)(2,1)}, bf16[2,512,128]{2,1,0:T(8,128)(2,1)S(1)}, u32[]{:S(2)}, u32[]{:S(2)}) collective-permute-start(bf16[2,512,128]{2,1,0:T(8,128)(2,1)} %get-tuple-element.36), channel_id=1, source_target_pairs={{0,12},{2,14},{4,8},{6,10},{8,4},{10,6},{12,0},{14,2},{16,28},{18,... | collective-permute-start | bytes 786440 | tf_op jit(solution)/shard_map/ppermute | solution.py:36
  23.0 2.1 %add_convert_fusion = (f16[4,64,1280]{2,1,0:T(8,128)(2,1)S(1)}, f32[4,64,1280]{2,1,0:T(8,128)S(1)}) fusion(f32[4,64,1280]{2,1,0:T(8,128)} %collective-permute-done.1, f32[8,64,1280]{2,1,0:T(8,128)S(1)} %get-tuple-element.26, f32[4,64,1280]{2,1,0:T(8,128)} %collective-permute-done), kind=kLoop, calls=%fused_computation | loop fusion | flops 983040 | bytes 7208960 | tf_op jit(solution)/shard_map/convert_element_type | solution.py:242
  25.2 1.6 %collective-permute-start.2 = (f16[2,64,1280]{2,1,0:T(8,128)(2,1)S(1)}, f16[2,64,1280]{2,1,0:T(8,128)(2,1)S(1)}, u32[]{:S(2)}, u32[]{:S(2)}) collective-permute-start(f16[2,64,1280]{2,1,0:T(8,128)(2,1)S(1)} %get-tuple-element.52), channel_id=1, source_target_pairs={{0,4},{2,6},{4,0},{6,2},{8,12},{10,14},{12,8},{14,10},{16,20},{18,... | collective-permute-start | bytes 983048 | tf_op jit(solution)/shard_map/ppermute | solution.py:36
  27.5 12.6 %collective-permute-done.2 = f16[2,64,1280]{2,1,0:T(8,128)(2,1)S(1)} collective-permute-done((f16[2,64,1280]{2,1,0:T(8,128)(2,1)S(1)}, f16[2,64,1280]{2,1,0:T(8,128)(2,1)S(1)}, u32[]{:S(2)}, u32[]{:S(2)}) %collective-permute-start.2) | collective-permute-done | bytes 327712 | tf_op jit(solution)/shard_map/ppermute | solution.py:36
  41.0 6.0 %collective-permute-done.4 = f16[2,64,1280]{2,1,0:T(8,128)(2,1)S(1)} collective-permute-done((f16[2,64,1280]{2,1,0:T(8,128)(2,1)S(1)}, f16[2,64,1280]{2,1,0:T(8,128)(2,1)S(1)}, u32[]{:S(2)}, u32[]{:S(2)}) %collective-permute-start.4) | collective-permute-done | bytes 327712 | tf_op jit(solution)/shard_map/ppermute | solution.py:36
  47.6 2.7 %collective-permute-start.5 = (f16[1,64,1280]{2,1,0:T(8,128)(2,1)S(1)}, f16[1,64,1280]{2,1,0:T(8,128)(2,1)S(1)}, u32[]{:S(2)}, u32[]{:S(2)}) collective-permute-start(f16[1,64,1280]{2,1,0:T(8,128)(2,1)S(1)} %fusion.7), channel_id=1, source_target_pairs={{0,16},{2,18},{4,20},{6,22},{8,24},{10,26},{12,28},{14,30},{16,0},... | collective-permute-start | bytes 491528 | tf_op jit(solution)/shard_map/ppermute | solution.py:36
  50.2 6.1 %collective-permute-done.6 = f16[1,64,1280]{2,1,0:T(8,128)(2,1)S(1)} collective-permute-done((f16[1,64,1280]{2,1,0:T(8,128)(2,1)S(1)}, f16[1,64,1280]{2,1,0:T(8,128)(2,1)S(1)}, u32[]{:S(2)}, u32[]{:S(2)}) %collective-permute-start.6) | collective-permute-done | bytes 163872 | tf_op jit(solution)/shard_map/ppermute | solution.py:36
  56.3 1.2 collective-permute-start.12
  58.3 13.7 %collective-permute-start.16 = (bf16[2,512,128]{2,1,0:T(8,128)(2,1)S(1)}, bf16[2,512,128]{2,1,0:T(8,128)(2,1)S(1)}, u32[]{:S(2)}, u32[]{:S(2)}) collective-permute-start(bf16[2,512,128]{2,1,0:T(8,128)(2,1)S(1)} %copy-done.9), channel_id=1, source_target_pairs={{0,8},{2,10},{4,12},{6,14},{8,0},{10,2},{12,4},{14,6},{16,24},{18,... | collective-permute-start | bytes 786440 | tf_op jit(solution)/shard_map/ppermute | solution.py:36
  72.1 1.5 %collective-permute-start.18 = (bf16[2,512,128]{2,1,0:T(8,128)(2,1)S(1)}, bf16[2,512,128]{2,1,0:T(8,128)(2,1)S(1)}, u32[]{:S(2)}, u32[]{:S(2)}) collective-permute-start(bf16[2,512,128]{2,1,0:T(8,128)(2,1)S(1)} %copy-done.8), channel_id=1, source_target_pairs={{0,4},{2,6},{4,0},{6,2},{8,12},{10,14},{12,8},{14,10},{16,20},{18,... | collective-permute-start | bytes 786440 | tf_op jit(solution)/shard_map/ppermute | solution.py:36
  73.7 13.2 %collective-permute-done.14.refs_8_ = bf16[2,512,128]{2,1,0:T(8,128)(2,1)S(1)} collective-permute-done((bf16[2,512,128]{2,1,0:T(8,128)(2,1)S(1)}, bf16[2,512,128]{2,1,0:T(8,128)(2,1)S(1)}, u32[]{:S(2)}, u32[]{:S(2)}) %collective-permute-start.14) | collective-permute-done | bytes 262176 | tf_op jit(solution)/shard_map/ppermute | solution.py:36
  90.0 9.2 %cache.1 = (bf16[512,128]{1,0:T(8,128)(2,1)S(1)}, f32[512,128]{1,0:T(8,128)S(1)}, f32[512,128]{1,0:T(8,128)S(1)}, f32[512,128]{1,0:T(8,128)S(1)}) custom-call(f32[14,512]{1,0:T(8,128)S(1)} %bitcast.32, f32[64,1280]{1,0:T(8,128)S(1)} %fusion.9.raw, f32[64,128]{1,0:T(8,128)S(1)} %get-tuple-element.59.cosine, f32[64,128]{1,0:T(8,128)S(1)} %get-tuple-element.48.sine, ...), custom_call_target="tpu_custom_call" | custom-call | tf_op jit(solution)/shard_map/cache/pallas_call | solution.py:319
  99.3 1.9 %last.1.refs_0_ = bf16[64,1024]{1,0:T(8,128)(2,1)S(1)} custom-call(f32[2,512]{1,0:T(2,128)S(1)} %slice.70.filled, bf16[512,128]{1,0:T(8,128)(2,1)S(1)} %get-tuple-element.41.query, bf16[2,512,128]{2,1,0:T(8,128)(2,1)S(1)} %collective-permute-done.20.refs_0_, bf16[2,512,128]{2,1,0:T(8,128)(2,1)S(1)} %collective-permute-done.21.refs_1_, ...), custom_call_target="tpu_custom_call" | custom-call | tf_op jit(solution)/shard_map/last/pallas_call | solution.py:322
  101.2 1.5 %collective-permute-start.24 = (bf16[64,1024]{1,0:T(8,128)(2,1)S(1)}, bf16[64,1024]{1,0:T(8,128)(2,1)S(1)}, u32[]{:S(2)}, u32[]{:S(2)}) collective-permute-start(bf16[64,1024]{1,0:T(8,128)(2,1)S(1)} %last.1.refs_0_), channel_id=1, source_target_pairs={{0,4},{2,6},{4,0},{6,2},{8,12},{10,14},{12,8},{14,10},{16,20},{18,... | collective-permute-start | bytes 393224 | tf_op jit(solution)/shard_map/ppermute | solution.py:36
  102.8 4.1 %collective-permute-start.26 = (bf16[64,1024]{1,0:T(8,128)(2,1)S(1)}, bf16[64,1024]{1,0:T(8,128)(2,1)S(1)}, u32[]{:S(2)}, u32[]{:S(2)}) collective-permute-start(bf16[64,1024]{1,0:T(8,128)(2,1)S(1)} %last.1.refs_0_), channel_id=1, source_target_pairs={{0,8},{2,10},{4,12},{6,14},{8,0},{10,2},{12,4},{14,6},{16,24},{18,... | collective-permute-start | bytes 393224 | tf_op jit(solution)/shard_map/ppermute | solution.py:36
  106.9 1.1 collective-permute-start.30
  108.0 1.5 %collective-permute-start.34 = (bf16[64,1024]{1,0:T(8,128)(2,1)S(1)}, bf16[64,1024]{1,0:T(8,128)(2,1)S(1)}, u32[]{:S(2)}, u32[]{:S(2)}) collective-permute-start(bf16[64,1024]{1,0:T(8,128)(2,1)S(1)} %last.1.refs_0_), channel_id=1, source_target_pairs={{0,24},{2,26},{4,28},{6,30},{8,16},{10,18},{12,20},{14,22},{16,8},... | collective-permute-start | bytes 393224 | tf_op jit(solution)/shard_map/ppermute | solution.py:36
  109.7 1.1 collective-permute-done.26.refs_4_
  111.3 8.5 %collective-permute-done.30.refs_8_ = bf16[64,1024]{1,0:T(8,128)(2,1)S(1)} collective-permute-done((bf16[64,1024]{1,0:T(8,128)(2,1)S(1)}, bf16[64,1024]{1,0:T(8,128)(2,1)S(1)}, u32[]{:S(2)}, u32[]{:S(2)}) %collective-permute-start.30) | collective-permute-done | bytes 131104 | tf_op jit(solution)/shard_map/ppermute | solution.py:36
  120.3 1.5 %collective-permute-start.36 = (bf16[64,1024]{1,0:T(8,128)(2,1)S(1)}, bf16[64,1024]{1,0:T(8,128)(2,1)S(1)}, u32[]{:S(2)}, u32[]{:S(2)}) collective-permute-start(bf16[64,1024]{1,0:T(8,128)(2,1)S(1)} %collective-permute-done.34.refs_12_), channel_id=1, source_target_pairs={{0,4},{2,6},{4,0},{6,2},{8,12},{10,14},{12,8},{14,10},{16,20},{18,... | collective-permute-start | bytes 393224 | tf_op jit(solution)/shard_map/ppermute | solution.py:36
  122.4 3.4 %collective-permute-done.32.refs_10_ = bf16[64,1024]{1,0:T(8,128)(2,1)S(1)} collective-permute-done((bf16[64,1024]{1,0:T(8,128)(2,1)S(1)}, bf16[64,1024]{1,0:T(8,128)(2,1)S(1)}, u32[]{:S(2)}, u32[]{:S(2)}) %collective-permute-start.32) | collective-permute-done | bytes 131104 | tf_op jit(solution)/shard_map/ppermute | solution.py:36
  125.8 1.4 %collective-permute-done.36.refs_14_ = bf16[64,1024]{1,0:T(8,128)(2,1)S(1)} collective-permute-done((bf16[64,1024]{1,0:T(8,128)(2,1)S(1)}, bf16[64,1024]{1,0:T(8,128)(2,1)S(1)}, u32[]{:S(2)}, u32[]{:S(2)}) %collective-permute-start.36) | collective-permute-done | bytes 131104 | tf_op jit(solution)/shard_map/ppermute | solution.py:36
  127.2 1.3 collective-permute-done.37.refs_15_
  129.3 1.5 %collective-permute-start.38 = (bf16[256,256]{1,0:T(8,128)(2,1)S(1)}, bf16[256,256]{1,0:T(8,128)(2,1)S(1)}, u32[]{:S(2)}, u32[]{:S(2)}) collective-permute-start(bf16[256,256]{1,0:T(8,128)(2,1)S(1)} %output.3), channel_id=1, source_target_pairs={{0,1},{1,0},{2,3},{3,2},{4,5},{5,4},{6,7},{7,6},{8,9},{9,8},{10,11... | collective-permute-start | bytes 393224 | tf_op jit(solution)/shard_map/ppermute | solution.py:372
  131.5 3.4 %collective-permute-done.38 = bf16[256,256]{1,0:T(8,128)(2,1)S(1)} collective-permute-done((bf16[256,256]{1,0:T(8,128)(2,1)S(1)}, bf16[256,256]{1,0:T(8,128)(2,1)S(1)}, u32[]{:S(2)}, u32[]{:S(2)}) %collective-permute-start.38) | collective-permute-done | bytes 131104 | tf_op jit(solution)/shard_map/ppermute | solution.py:372
  (104 shorter events, 14.1 us)
Async XLA Ops:
  8.5 14.5 %collective-permute-start = (f32[4,64,1280]{2,1,0:T(8,128)}, f32[4,64,1280]{2,1,0:T(8,128)}, u32[]{:S(2)}, u32[]{:S(2)}) collective-permute-start(f32[4,64,1280]{2,1,0:T(8,128)} %get-tuple-element.27), channel_id=1, source_target_pairs={{0,2},{2,0},{4,6},{6,4},{8,10},{10,8},{12,14},{14,12},{16,18},{18,... | collective-permute-start | bytes 3932168 | tf_op jit(solution)/shard_map/ppermute | solution.py:36
  9.0 14.0 %collective-permute-start.1 = (f32[4,64,1280]{2,1,0:T(8,128)}, f32[4,64,1280]{2,1,0:T(8,128)}, u32[]{:S(2)}, u32[]{:S(2)}) collective-permute-start(f32[4,64,1280]{2,1,0:T(8,128)} %get-tuple-element.28), channel_id=1, source_target_pairs={{0,2},{2,0},{4,6},{6,4},{8,10},{10,8},{12,14},{14,12},{16,18},{18,... | collective-permute-start | bytes 3932168 | tf_op jit(solution)/shard_map/ppermute | solution.py:36
  11.6 46.7 %collective-permute-start.7 = (bf16[2,512,128]{2,1,0:T(8,128)(2,1)}, bf16[2,512,128]{2,1,0:T(8,128)(2,1)S(1)}, u32[]{:S(2)}, u32[]{:S(2)}) collective-permute-start(bf16[2,512,128]{2,1,0:T(8,128)(2,1)} %get-tuple-element.34.refs_0_), channel_id=1, source_target_pairs={{0,2},{2,0},{4,6},{6,4},{8,10},{10,8},{12,14},{14,12},{16,18},{18,... | collective-permute-start | bytes 786440 | tf_op jit(solution)/shard_map/ppermute | solution.py:36
  14.3 57.8 %collective-permute-start.8 = (bf16[2,512,128]{2,1,0:T(8,128)(2,1)}, bf16[2,512,128]{2,1,0:T(8,128)(2,1)S(1)}, u32[]{:S(2)}, u32[]{:S(2)}) collective-permute-start(bf16[2,512,128]{2,1,0:T(8,128)(2,1)} %get-tuple-element.35), channel_id=1, source_target_pairs={{0,20},{2,22},{4,16},{6,18},{8,28},{10,30},{12,24},{14,26},{16,4},... | collective-permute-start | bytes 786440 | tf_op jit(solution)/shard_map/ppermute | solution.py:36
  18.9 54.7 %collective-permute-start.10 = (bf16[2,512,128]{2,1,0:T(8,128)(2,1)}, bf16[2,512,128]{2,1,0:T(8,128)(2,1)S(1)}, u32[]{:S(2)}, u32[]{:S(2)}) collective-permute-start(bf16[2,512,128]{2,1,0:T(8,128)(2,1)} %get-tuple-element.36), channel_id=1, source_target_pairs={{0,12},{2,14},{4,8},{6,10},{8,4},{10,6},{12,0},{14,2},{16,28},{18,... | collective-permute-start | bytes 786440 | tf_op jit(solution)/shard_map/ppermute | solution.py:36
  25.2 14.9 %collective-permute-start.2 = (f16[2,64,1280]{2,1,0:T(8,128)(2,1)S(1)}, f16[2,64,1280]{2,1,0:T(8,128)(2,1)S(1)}, u32[]{:S(2)}, u32[]{:S(2)}) collective-permute-start(f16[2,64,1280]{2,1,0:T(8,128)(2,1)S(1)} %get-tuple-element.52), channel_id=1, source_target_pairs={{0,4},{2,6},{4,0},{6,2},{8,12},{10,14},{12,8},{14,10},{16,20},{18,... | collective-permute-start | bytes 983048 | tf_op jit(solution)/shard_map/ppermute | solution.py:36
  26.9 20.1 %collective-permute-start.4 = (f16[2,64,1280]{2,1,0:T(8,128)(2,1)S(1)}, f16[2,64,1280]{2,1,0:T(8,128)(2,1)S(1)}, u32[]{:S(2)}, u32[]{:S(2)}) collective-permute-start(f16[2,64,1280]{2,1,0:T(8,128)(2,1)S(1)} %get-tuple-element.51), channel_id=1, source_target_pairs={{0,4},{2,6},{4,0},{6,2},{8,12},{10,14},{12,8},{14,10},{16,20},{18,... | collective-permute-start | bytes 983048 | tf_op jit(solution)/shard_map/ppermute | solution.py:36
  40.2 7.2 %collective-permute-start.3 = (f16[1,64,1280]{2,1,0:T(8,128)(2,1)S(1)}, f16[1,64,1280]{2,1,0:T(8,128)(2,1)S(1)}, u32[]{:S(2)}, u32[]{:S(2)}) collective-permute-start(f16[1,64,1280]{2,1,0:T(8,128)(2,1)S(1)} %get-tuple-element.56), channel_id=1, source_target_pairs={{0,8},{2,10},{4,12},{6,14},{8,0},{10,2},{12,4},{14,6},{16,24},{18,... | collective-permute-start | bytes 491528 | tf_op jit(solution)/shard_map/ppermute | solution.py:36
  47.0 9.3 %collective-permute-start.6 = (f16[1,64,1280]{2,1,0:T(8,128)(2,1)S(1)}, f16[1,64,1280]{2,1,0:T(8,128)(2,1)S(1)}, u32[]{:S(2)}, u32[]{:S(2)}) collective-permute-start(f16[1,64,1280]{2,1,0:T(8,128)(2,1)S(1)} %get-tuple-element.55), channel_id=1, source_target_pairs={{0,8},{2,10},{4,12},{6,14},{8,0},{10,2},{12,4},{14,6},{16,24},{18,... | collective-permute-start | bytes 491528 | tf_op jit(solution)/shard_map/ppermute | solution.py:36
  47.6 10.6 %collective-permute-start.5 = (f16[1,64,1280]{2,1,0:T(8,128)(2,1)S(1)}, f16[1,64,1280]{2,1,0:T(8,128)(2,1)S(1)}, u32[]{:S(2)}, u32[]{:S(2)}) collective-permute-start(f16[1,64,1280]{2,1,0:T(8,128)(2,1)S(1)} %fusion.7), channel_id=1, source_target_pairs={{0,16},{2,18},{4,20},{6,22},{8,24},{10,26},{12,28},{14,30},{16,0},... | collective-permute-start | bytes 491528 | tf_op jit(solution)/shard_map/ppermute | solution.py:36
  56.3 17.3 %collective-permute-start.12 = (bf16[2,512,128]{2,1,0:T(8,128)(2,1)S(1)}, bf16[2,512,128]{2,1,0:T(8,128)(2,1)S(1)}, u32[]{:S(2)}, u32[]{:S(2)}) collective-permute-start(bf16[2,512,128]{2,1,0:T(8,128)(2,1)S(1)} %copy-done.11), channel_id=1, source_target_pairs={{0,28},{2,30},{4,24},{6,26},{8,20},{10,22},{12,16},{14,18},{16,12}... | collective-permute-start | bytes 786440 | tf_op jit(solution)/shard_map/ppermute | solution.py:36
  58.2 28.7 %collective-permute-start.14 = (bf16[2,512,128]{2,1,0:T(8,128)(2,1)S(1)}, bf16[2,512,128]{2,1,0:T(8,128)(2,1)S(1)}, u32[]{:S(2)}, u32[]{:S(2)}) collective-permute-start(bf16[2,512,128]{2,1,0:T(8,128)(2,1)S(1)} %copy-done.10), channel_id=1, source_target_pairs={{0,16},{2,18},{4,20},{6,22},{8,24},{10,26},{12,28},{14,30},{16,0},... | collective-permute-start | bytes 786440 | tf_op jit(solution)/shard_map/ppermute | solution.py:36
  58.3 28.7 %collective-permute-start.16 = (bf16[2,512,128]{2,1,0:T(8,128)(2,1)S(1)}, bf16[2,512,128]{2,1,0:T(8,128)(2,1)S(1)}, u32[]{:S(2)}, u32[]{:S(2)}) collective-permute-start(bf16[2,512,128]{2,1,0:T(8,128)(2,1)S(1)} %copy-done.9), channel_id=1, source_target_pairs={{0,8},{2,10},{4,12},{6,14},{8,0},{10,2},{12,4},{14,6},{16,24},{18,... | collective-permute-start | bytes 786440 | tf_op jit(solution)/shard_map/ppermute | solution.py:36
  72.1 15.5 %collective-permute-start.18 = (bf16[2,512,128]{2,1,0:T(8,128)(2,1)S(1)}, bf16[2,512,128]{2,1,0:T(8,128)(2,1)S(1)}, u32[]{:S(2)}, u32[]{:S(2)}) collective-permute-start(bf16[2,512,128]{2,1,0:T(8,128)(2,1)S(1)} %copy-done.8), channel_id=1, source_target_pairs={{0,4},{2,6},{4,0},{6,2},{8,12},{10,14},{12,8},{14,10},{16,20},{18,... | collective-permute-start | bytes 786440 | tf_op jit(solution)/shard_map/ppermute | solution.py:36
  73.6 14.1 %collective-permute-start.20 = (bf16[2,512,128]{2,1,0:T(8,128)(2,1)S(1)}, bf16[2,512,128]{2,1,0:T(8,128)(2,1)S(1)}, u32[]{:S(2)}, u32[]{:S(2)}) collective-permute-start(bf16[2,512,128]{2,1,0:T(8,128)(2,1)S(1)} %copy-done.7), channel_id=1, source_target_pairs={{0,24},{2,26},{4,28},{6,30},{8,16},{10,18},{12,20},{14,22},{16,8},... | collective-permute-start | bytes 786440 | tf_op jit(solution)/shard_map/ppermute | solution.py:36
  73.7 14.6 %collective-permute-start.9 = (bf16[2,512,128]{2,1,0:T(8,128)(2,1)S(1)}, bf16[2,512,128]{2,1,0:T(8,128)(2,1)S(1)}, u32[]{:S(2)}, u32[]{:S(2)}) collective-permute-start(bf16[2,512,128]{2,1,0:T(8,128)(2,1)S(1)} %collective-permute-done.8.refs_2_), channel_id=1, source_target_pairs={{0,2},{2,0},{4,6},{6,4},{8,10},{10,8},{12,14},{14,12},{16,18},{18,... | collective-permute-start | bytes 786440 | tf_op jit(solution)/shard_map/ppermute | solution.py:36
  88.5 10.8 %collective-permute-start.21 = (bf16[2,512,128]{2,1,0:T(8,128)(2,1)S(1)}, bf16[2,512,128]{2,1,0:T(8,128)(2,1)S(1)}, u32[]{:S(2)}, u32[]{:S(2)}) collective-permute-start(bf16[2,512,128]{2,1,0:T(8,128)(2,1)S(1)} %collective-permute-done.20.refs_0_), channel_id=1, source_target_pairs={{0,2},{2,0},{4,6},{6,4},{8,10},{10,8},{12,14},{14,12},{16,18},{18,... | collective-permute-start | bytes 786440 | tf_op jit(solution)/shard_map/ppermute | solution.py:36
  88.9 10.4 %collective-permute-start.22 = (bf16[2,64,128]{2,1,0:T(8,128)(2,1)S(1)}, bf16[2,64,128]{2,1,0:T(8,128)(2,1)S(1)}, u32[]{:S(2)}, u32[]{:S(2)}) collective-permute-start(bf16[2,64,128]{2,1,0:T(8,128)(2,1)S(1)} %pad_maximum_fusion.2.refs_2_), channel_id=1, source_target_pairs={{0,2},{2,0},{4,6},{6,4},{8,10},{10,8},{12,14},{14,12},{16,18},{18,... | collective-permute-start | bytes 98312 | tf_op jit(solution)/shard_map/ppermute | solution.py:36
  101.2 8.2 %collective-permute-start.24 = (bf16[64,1024]{1,0:T(8,128)(2,1)S(1)}, bf16[64,1024]{1,0:T(8,128)(2,1)S(1)}, u32[]{:S(2)}, u32[]{:S(2)}) collective-permute-start(bf16[64,1024]{1,0:T(8,128)(2,1)S(1)} %last.1.refs_0_), channel_id=1, source_target_pairs={{0,4},{2,6},{4,0},{6,2},{8,12},{10,14},{12,8},{14,10},{16,20},{18,... | collective-permute-start | bytes 393224 | tf_op jit(solution)/shard_map/ppermute | solution.py:36
  102.8 8.0 %collective-permute-start.26 = (bf16[64,1024]{1,0:T(8,128)(2,1)S(1)}, bf16[64,1024]{1,0:T(8,128)(2,1)S(1)}, u32[]{:S(2)}, u32[]{:S(2)}) collective-permute-start(bf16[64,1024]{1,0:T(8,128)(2,1)S(1)} %last.1.refs_0_), channel_id=1, source_target_pairs={{0,8},{2,10},{4,12},{6,14},{8,0},{10,2},{12,4},{14,6},{16,24},{18,... | collective-permute-start | bytes 393224 | tf_op jit(solution)/shard_map/ppermute | solution.py:36
  106.9 3.8 %collective-permute-start.23 = (bf16[64,1024]{1,0:T(8,128)(2,1)S(1)}, bf16[64,1024]{1,0:T(8,128)(2,1)S(1)}, u32[]{:S(2)}, u32[]{:S(2)}) collective-permute-start(bf16[64,1024]{1,0:T(8,128)(2,1)S(1)} %last.1.refs_0_), channel_id=1, source_target_pairs={{0,2},{2,0},{4,6},{6,4},{8,10},{10,8},{12,14},{14,12},{16,18},{18,... | collective-permute-start | bytes 393224 | tf_op jit(solution)/shard_map/ppermute | solution.py:36
  106.9 12.9 %collective-permute-start.30 = (bf16[64,1024]{1,0:T(8,128)(2,1)S(1)}, bf16[64,1024]{1,0:T(8,128)(2,1)S(1)}, u32[]{:S(2)}, u32[]{:S(2)}) collective-permute-start(bf16[64,1024]{1,0:T(8,128)(2,1)S(1)} %last.1.refs_0_), channel_id=1, source_target_pairs={{0,16},{2,18},{4,20},{6,22},{8,24},{10,26},{12,28},{14,30},{16,0},... | collective-permute-start | bytes 393224 | tf_op jit(solution)/shard_map/ppermute | solution.py:36
  108.0 12.4 %collective-permute-start.34 = (bf16[64,1024]{1,0:T(8,128)(2,1)S(1)}, bf16[64,1024]{1,0:T(8,128)(2,1)S(1)}, u32[]{:S(2)}, u32[]{:S(2)}) collective-permute-start(bf16[64,1024]{1,0:T(8,128)(2,1)S(1)} %last.1.refs_0_), channel_id=1, source_target_pairs={{0,24},{2,26},{4,28},{6,30},{8,16},{10,18},{12,20},{14,22},{16,8},... | collective-permute-start | bytes 393224 | tf_op jit(solution)/shard_map/ppermute | solution.py:36
  109.4 12.4 %collective-permute-start.25 = (bf16[64,1024]{1,0:T(8,128)(2,1)S(1)}, bf16[64,1024]{1,0:T(8,128)(2,1)S(1)}, u32[]{:S(2)}, u32[]{:S(2)}) collective-permute-start(bf16[64,1024]{1,0:T(8,128)(2,1)S(1)} %collective-permute-done.24.refs_2_), channel_id=1, source_target_pairs={{0,2},{2,0},{4,6},{6,4},{8,10},{10,8},{12,14},{14,12},{16,18},{18,... | collective-permute-start | bytes 393224 | tf_op jit(solution)/shard_map/ppermute | solution.py:36
  110.7 11.1 %collective-permute-start.27 = (bf16[64,1024]{1,0:T(8,128)(2,1)S(1)}, bf16[64,1024]{1,0:T(8,128)(2,1)S(1)}, u32[]{:S(2)}, u32[]{:S(2)}) collective-permute-start(bf16[64,1024]{1,0:T(8,128)(2,1)S(1)} %collective-permute-done.26.refs_4_), channel_id=1, source_target_pairs={{0,2},{2,0},{4,6},{6,4},{8,10},{10,8},{12,14},{14,12},{16,18},{18,... | collective-permute-start | bytes 393224 | tf_op jit(solution)/shard_map/ppermute | solution.py:36
  110.7 11.6 %collective-permute-start.28 = (bf16[64,1024]{1,0:T(8,128)(2,1)S(1)}, bf16[64,1024]{1,0:T(8,128)(2,1)S(1)}, u32[]{:S(2)}, u32[]{:S(2)}) collective-permute-start(bf16[64,1024]{1,0:T(8,128)(2,1)S(1)} %collective-permute-done.26.refs_4_), channel_id=1, source_target_pairs={{0,4},{2,6},{4,0},{6,2},{8,12},{10,14},{12,8},{14,10},{16,20},{18,... | collective-permute-start | bytes 393224 | tf_op jit(solution)/shard_map/ppermute | solution.py:36
  119.8 6.0 %collective-permute-start.32 = (bf16[64,1024]{1,0:T(8,128)(2,1)S(1)}, bf16[64,1024]{1,0:T(8,128)(2,1)S(1)}, u32[]{:S(2)}, u32[]{:S(2)}) collective-permute-start(bf16[64,1024]{1,0:T(8,128)(2,1)S(1)} %collective-permute-done.30.refs_8_), channel_id=1, source_target_pairs={{0,4},{2,6},{4,0},{6,2},{8,12},{10,14},{12,8},{14,10},{16,20},{18,... | collective-permute-start | bytes 393224 | tf_op jit(solution)/shard_map/ppermute | solution.py:36
  120.3 6.9 %collective-permute-start.36 = (bf16[64,1024]{1,0:T(8,128)(2,1)S(1)}, bf16[64,1024]{1,0:T(8,128)(2,1)S(1)}, u32[]{:S(2)}, u32[]{:S(2)}) collective-permute-start(bf16[64,1024]{1,0:T(8,128)(2,1)S(1)} %collective-permute-done.34.refs_12_), channel_id=1, source_target_pairs={{0,4},{2,6},{4,0},{6,2},{8,12},{10,14},{12,8},{14,10},{16,20},{18,... | collective-permute-start | bytes 393224 | tf_op jit(solution)/shard_map/ppermute | solution.py:36
  121.8 5.4 %collective-permute-start.31 = (bf16[64,1024]{1,0:T(8,128)(2,1)S(1)}, bf16[64,1024]{1,0:T(8,128)(2,1)S(1)}, u32[]{:S(2)}, u32[]{:S(2)}) collective-permute-start(bf16[64,1024]{1,0:T(8,128)(2,1)S(1)} %collective-permute-done.30.refs_8_), channel_id=1, source_target_pairs={{0,2},{2,0},{4,6},{6,4},{8,10},{10,8},{12,14},{14,12},{16,18},{18,... | collective-permute-start | bytes 393224 | tf_op jit(solution)/shard_map/ppermute | solution.py:36
  121.8 5.4 %collective-permute-start.35 = (bf16[64,1024]{1,0:T(8,128)(2,1)S(1)}, bf16[64,1024]{1,0:T(8,128)(2,1)S(1)}, u32[]{:S(2)}, u32[]{:S(2)}) collective-permute-start(bf16[64,1024]{1,0:T(8,128)(2,1)S(1)} %collective-permute-done.34.refs_12_), channel_id=1, source_target_pairs={{0,2},{2,0},{4,6},{6,4},{8,10},{10,8},{12,14},{14,12},{16,18},{18,... | collective-permute-start | bytes 393224 | tf_op jit(solution)/shard_map/ppermute | solution.py:36
  122.3 4.9 %collective-permute-start.29 = (bf16[64,1024]{1,0:T(8,128)(2,1)S(1)}, bf16[64,1024]{1,0:T(8,128)(2,1)S(1)}, u32[]{:S(2)}, u32[]{:S(2)}) collective-permute-start(bf16[64,1024]{1,0:T(8,128)(2,1)S(1)} %collective-permute-done.28.refs_6_), channel_id=1, source_target_pairs={{0,2},{2,0},{4,6},{6,4},{8,10},{10,8},{12,14},{14,12},{16,18},{18,... | collective-permute-start | bytes 393224 | tf_op jit(solution)/shard_map/ppermute | solution.py:36
  129.3 5.6 %collective-permute-start.38 = (bf16[256,256]{1,0:T(8,128)(2,1)S(1)}, bf16[256,256]{1,0:T(8,128)(2,1)S(1)}, u32[]{:S(2)}, u32[]{:S(2)}) collective-permute-start(bf16[256,256]{1,0:T(8,128)(2,1)S(1)} %output.3), channel_id=1, source_target_pairs={{0,1},{1,0},{2,3},{3,2},{4,5},{5,4},{6,7},{7,6},{8,9},{9,8},{10,11... | collective-permute-start | bytes 393224 | tf_op jit(solution)/shard_map/ppermute | solution.py:372
  (20 other events, 226.4 us)

commit v4 on v3

--- a/solution.py
+++ b/solution.py
@@ -99,7 +99,7 @@
         scores[i] = piece
         return functools.reduce(jnp.maximum, lane_blocks(piece), top)
 
-    return lax.fori_loop(0, keys.shape[0], body, top)
+    return lax.fori_loop(0, keys.shape[0], body, top, unroll=2)
 
 
 def weigh(scores, values, top, mass, acc):
@@ -111,7 +111,7 @@
         acc[...] += jnp.dot(weight.astype(jnp.bfloat16), values[i], preferred_element_type=jnp.float32)
         return 0
 
-    lax.fori_loop(0, values.shape[0], body, 0)
+    lax.fori_loop(0, values.shape[0], body, 0, unroll=2)
 
 
 def cache_kernel(count, group, filled, raw, cosine, sine, *refs):
@@ -249,10 +249,10 @@
     high, rest = lax.optimization_barrier((high, rest))
     raw = (keep + rest.astype(f32) + high.astype(f32))[0]
     away = sorted(range(1, heads), key=lambda h: (h.bit_count() > 1, -h))
-    order = [h * trees + t for h in away for t in range(1, trees)]
-    order += [h * trees for h in away[:-1]]
+    order = [h * trees + t for h in away[:-1] for t in range(1, trees)]
+    order += [h * trees for h in away[-1:] + away[:-1]]
     order += list(range(1, trees))
-    order += [h * trees for h in away[-1:]]
+    order += [h * trees + t for h in away[-1:] for t in range(1, trees)]
     held = {}
     first = len(order) // 2
     for some in (order[:first], [0] + order[first:]):

time: 136 us -> 133 us (0.978)
  Pallas kernels: 20.6 us -> 17.8 us
    pallas_call x1, Pallas kernels: 9.25 us -> 7.01 us  [local(): attend(filled[:near], raw, cosine, sine, *chunks[:near])]
  transfers between devices with their start and end apart: 39 -> 39, of which waited for: 14 -> 14; matrix products, arithmetic and copies ran while one was open for 4% -> 4% of each run, Pallas kernels for 11% -> 9%
where the time goes in v4:
time: 133 us
  waiting for transfers between devices  57.8 us (43%)
  starting transfers between devices  44.7 us (34%)
  Pallas kernels  17.8 us (13%)
  local copies, waits for them, and re-layouts  6.29 us (5%)
  other arithmetic  4.14 us (3%)
    ppermute x38, waiting for transfers between devices, swap(): return lax.ppermute(value, 'seq', [(i, i ^ mask) for i in range(size)])  54.4 us
    ppermute x38, starting transfers between devices, swap(): return lax.ppermute(value, 'seq', [(i, i ^ mask) for i in range(size)])  43.2 us
    pallas_call x1, Pallas kernels, local(): attend(filled[:near], raw, cosine, sine, *chunks[:near])  7.01 us
    unnamed x26, local copies, waits for them, and re-layouts  5.27 us
    pallas_call x2, Pallas kernels, local(): pl.pallas_call(functools.partial(pack_kernel, splits, trees, some), out_s...  4.71 us
    ppermute x1, waiting for transfers between devices, local(): lax.ppermute(product(step, bf16), 'head', [(i, i ^ step) for i in range(s...  3.39 us
    pallas_call x1, Pallas kernels, local(): keep, low_send, high_send = project(states, w_query, w_key, w_value)  3.26 us
  transfers between devices with their start and end apart: 39, of which 14 were waited for; matrix products, arithmetic and copies ran while one was open for 4% of the time, Pallas kernels for 9%

profile of v4, /device:TPU:0, one launch (start us, length us, event | category | flops | bytes accessed | tf_op | source)
XLA Modules:
  0.0 132.8 jit_solution(6980430266048785909)
XLA Ops:
  0.0 2.2 %copy-done.2 = bf16[512,4096]{1,0:T(8,128)(2,1)S(1)} copy-done((bf16[512,4096]{1,0:T(8,128)(2,1)S(1)}, bf16[512,4096]{1,0:T(8,128)(2,1)}, u32[]{:S(2)}) %copy-start.2) | copy-done | bytes 4194328
  2.2 1.0 copy-done.3
  3.2 1.0 copy-done.4
  5.2 3.3 %project.1 = (f32[8,64,1280]{2,1,0:T(8,128)S(1)}, f32[4,64,1280]{2,1,0:T(8,128)}, f32[4,64,1280]{2,1,0:T(8,128)}) custom-call(bf16[256,512]{1,0:T(8,128)(2,1)S(1)} %copy-done.6, bf16[512,4096]{1,0:T(8,128)(2,1)S(1)} %copy-done.2, bf16[512,512]{1,0:T(8,128)(2,1)S(1)} %copy-done.3, bf16[512,512]{1,0:T(8,128)(2,1)S(1)} %copy-done.4), custom_call_target="tpu_custom_call" | custom-call | tf_op jit(solution)/shard_map/project/pallas_call | solution.py:233
  9.0 2.5 %pack.2 = (bf16[2,512,128]{2,1,0:T(8,128)(2,1)}, bf16[2,512,128]{2,1,0:T(8,128)(2,1)}, bf16[2,512,128]{2,1,0:T(8,128)(2,1)}, bf16[2,512,128]{2,1,0:T(8,128)(2,1)}, bf16[2,512,128]{2,1,0:T(8,128)(2,1)}) custom-call(bf16[2,512,512]{2,1,0:T(8,128)(2,1)} %key_ref.3, bf16[2,512,512]{2,1,0:T(8,128)(2,1)} %value_ref.3), custom_call_target="tpu_custom_call" | custom-call | tf_op jit(solution)/shard_map/pack/pallas_call | solution.py:259
  12.1 2.2 %pack.3 = (bf16[2,512,128]{2,1,0:T(8,128)(2,1)}, bf16[2,512,128]{2,1,0:T(8,128)(2,1)}, bf16[2,512,128]{2,1,0:T(8,128)(2,1)}) custom-call(bf16[2,512,512]{2,1,0:T(8,128)(2,1)} %key_ref.3, bf16[2,512,512]{2,1,0:T(8,128)(2,1)} %value_ref.3), custom_call_target="tpu_custom_call" | custom-call | tf_op jit(solution)/shard_map/pack/pallas_call | solution.py:259
  14.3 4.6 %collective-permute-start.8 = (bf16[2,512,128]{2,1,0:T(8,128)(2,1)}, bf16[2,512,128]{2,1,0:T(8,128)(2,1)S(1)}, u32[]{:S(2)}, u32[]{:S(2)}) collective-permute-start(bf16[2,512,128]{2,1,0:T(8,128)(2,1)} %get-tuple-element.35), channel_id=1, source_target_pairs={{0,20},{2,22},{4,16},{6,18},{8,28},{10,30},{12,24},{14,26},{16,4},... | collective-permute-start | bytes 786440 | tf_op jit(solution)/shard_map/ppermute | solution.py:36
  18.9 1.5 %collective-permute-start.10 = (bf16[2,512,128]{2,1,0:T(8,128)(2,1)}, bf16[2,512,128]{2,1,0:T(8,128)(2,1)S(1)}, u32[]{:S(2)}, u32[]{:S(2)}) collective-permute-start(bf16[2,512,128]{2,1,0:T(8,128)(2,1)} %get-tuple-element.36), channel_id=1, source_target_pairs={{0,12},{2,14},{4,8},{6,10},{8,4},{10,6},{12,0},{14,2},{16,28},{18,... | collective-permute-start | bytes 786440 | tf_op jit(solution)/shard_map/ppermute | solution.py:36
  23.0 2.1 %add_convert_fusion = (f16[4,64,1280]{2,1,0:T(8,128)(2,1)S(1)}, f32[4,64,1280]{2,1,0:T(8,128)S(1)}) fusion(f32[4,64,1280]{2,1,0:T(8,128)} %collective-permute-done.1, f32[8,64,1280]{2,1,0:T(8,128)S(1)} %get-tuple-element.26, f32[4,64,1280]{2,1,0:T(8,128)} %collective-permute-done), kind=kLoop, calls=%fused_computation | loop fusion | flops 983040 | bytes 7208960 | tf_op jit(solution)/shard_map/convert_element_type | solution.py:242
  25.2 1.6 %collective-permute-start.2 = (f16[2,64,1280]{2,1,0:T(8,128)(2,1)S(1)}, f16[2,64,1280]{2,1,0:T(8,128)(2,1)S(1)}, u32[]{:S(2)}, u32[]{:S(2)}) collective-permute-start(f16[2,64,1280]{2,1,0:T(8,128)(2,1)S(1)} %get-tuple-element.52), channel_id=1, source_target_pairs={{0,4},{2,6},{4,0},{6,2},{8,12},{10,14},{12,8},{14,10},{16,20},{18,... | collective-permute-start | bytes 983048 | tf_op jit(solution)/shard_map/ppermute | solution.py:36
  27.5 12.6 %collective-permute-done.2 = f16[2,64,1280]{2,1,0:T(8,128)(2,1)S(1)} collective-permute-done((f16[2,64,1280]{2,1,0:T(8,128)(2,1)S(1)}, f16[2,64,1280]{2,1,0:T(8,128)(2,1)S(1)}, u32[]{:S(2)}, u32[]{:S(2)}) %collective-permute-start.2) | collective-permute-done | bytes 327712 | tf_op jit(solution)/shard_map/ppermute | solution.py:36
  41.0 6.0 %collective-permute-done.4 = f16[2,64,1280]{2,1,0:T(8,128)(2,1)S(1)} collective-permute-done((f16[2,64,1280]{2,1,0:T(8,128)(2,1)S(1)}, f16[2,64,1280]{2,1,0:T(8,128)(2,1)S(1)}, u32[]{:S(2)}, u32[]{:S(2)}) %collective-permute-start.4) | collective-permute-done | bytes 327712 | tf_op jit(solution)/shard_map/ppermute | solution.py:36
  47.6 2.7 %collective-permute-start.5 = (f16[1,64,1280]{2,1,0:T(8,128)(2,1)S(1)}, f16[1,64,1280]{2,1,0:T(8,128)(2,1)S(1)}, u32[]{:S(2)}, u32[]{:S(2)}) collective-permute-start(f16[1,64,1280]{2,1,0:T(8,128)(2,1)S(1)} %fusion.7), channel_id=1, source_target_pairs={{0,16},{2,18},{4,20},{6,22},{8,24},{10,26},{12,28},{14,30},{16,0},... | collective-permute-start | bytes 491528 | tf_op jit(solution)/shard_map/ppermute | solution.py:36
  50.2 6.1 %collective-permute-done.6 = f16[1,64,1280]{2,1,0:T(8,128)(2,1)S(1)} collective-permute-done((f16[1,64,1280]{2,1,0:T(8,128)(2,1)S(1)}, f16[1,64,1280]{2,1,0:T(8,128)(2,1)S(1)}, u32[]{:S(2)}, u32[]{:S(2)}) %collective-permute-start.6) | collective-permute-done | bytes 163872 | tf_op jit(solution)/shard_map/ppermute | solution.py:36
  56.3 1.3 collective-permute-start.12
  58.3 13.7 %collective-permute-start.16 = (bf16[2,512,128]{2,1,0:T(8,128)(2,1)S(1)}, bf16[2,512,128]{2,1,0:T(8,128)(2,1)S(1)}, u32[]{:S(2)}, u32[]{:S(2)}) collective-permute-start(bf16[2,512,128]{2,1,0:T(8,128)(2,1)S(1)} %copy-done.9), channel_id=1, source_target_pairs={{0,8},{2,10},{4,12},{6,14},{8,0},{10,2},{12,4},{14,6},{16,24},{18,... | collective-permute-start | bytes 786440 | tf_op jit(solution)/shard_map/ppermute | solution.py:36
  73.1 13.9 %collective-permute-done.14.refs_8_ = bf16[2,512,128]{2,1,0:T(8,128)(2,1)S(1)} collective-permute-done((bf16[2,512,128]{2,1,0:T(8,128)(2,1)S(1)}, bf16[2,512,128]{2,1,0:T(8,128)(2,1)S(1)}, u32[]{:S(2)}, u32[]{:S(2)}) %collective-permute-start.14) | collective-permute-done | bytes 262176 | tf_op jit(solution)/shard_map/ppermute | solution.py:36
  90.0 7.0 %cache.1 = (bf16[512,128]{1,0:T(8,128)(2,1)S(1)}, f32[512,128]{1,0:T(8,128)S(1)}, f32[512,128]{1,0:T(8,128)S(1)}, f32[512,128]{1,0:T(8,128)S(1)}) custom-call(f32[14,512]{1,0:T(8,128)S(1)} %bitcast.32, f32[64,1280]{1,0:T(8,128)S(1)} %fusion.9.raw, f32[64,128]{1,0:T(8,128)S(1)} %get-tuple-element.59.cosine, f32[64,128]{1,0:T(8,128)S(1)} %get-tuple-element.48.sine, ...), custom_call_target="tpu_custom_call" | custom-call | tf_op jit(solution)/shard_map/cache/pallas_call | solution.py:319
  97.1 1.4 %last.1.refs_0_ = bf16[64,1024]{1,0:T(8,128)(2,1)S(1)} custom-call(f32[2,512]{1,0:T(2,128)S(1)} %slice.70.filled, bf16[512,128]{1,0:T(8,128)(2,1)S(1)} %get-tuple-element.41.query, bf16[2,512,128]{2,1,0:T(8,128)(2,1)S(1)} %collective-permute-done.20.refs_0_, bf16[2,512,128]{2,1,0:T(8,128)(2,1)S(1)} %collective-permute-done.21.refs_1_, ...), custom_call_target="tpu_custom_call" | custom-call | tf_op jit(solution)/shard_map/last/pallas_call | solution.py:322
  98.4 1.1 collective-permute-start.24
  99.6 4.5 %collective-permute-start.26 = (bf16[64,1024]{1,0:T(8,128)(2,1)S(1)}, bf16[64,1024]{1,0:T(8,128)(2,1)S(1)}, u32[]{:S(2)}, u32[]{:S(2)}) collective-permute-start(bf16[64,1024]{1,0:T(8,128)(2,1)S(1)} %last.1.refs_0_), channel_id=1, source_target_pairs={{0,8},{2,10},{4,12},{6,14},{8,0},{10,2},{12,4},{14,6},{16,24},{18,... | collective-permute-start | bytes 393224 | tf_op jit(solution)/shard_map/ppermute | solution.py:36
  104.1 1.1 collective-permute-start.30
  105.1 1.5 %collective-permute-start.34 = (bf16[64,1024]{1,0:T(8,128)(2,1)S(1)}, bf16[64,1024]{1,0:T(8,128)(2,1)S(1)}, u32[]{:S(2)}, u32[]{:S(2)}) collective-permute-start(bf16[64,1024]{1,0:T(8,128)(2,1)S(1)} %last.1.refs_0_), channel_id=1, source_target_pairs={{0,24},{2,26},{4,28},{6,30},{8,16},{10,18},{12,20},{14,22},{16,8},... | collective-permute-start | bytes 393224 | tf_op jit(solution)/shard_map/ppermute | solution.py:36
  106.8 1.1 collective-permute-done.26.refs_4_
  107.9 1.5 %collective-permute-start.28 = (bf16[64,1024]{1,0:T(8,128)(2,1)S(1)}, bf16[64,1024]{1,0:T(8,128)(2,1)S(1)}, u32[]{:S(2)}, u32[]{:S(2)}) collective-permute-start(bf16[64,1024]{1,0:T(8,128)(2,1)S(1)} %collective-permute-done.26.refs_4_), channel_id=1, source_target_pairs={{0,4},{2,6},{4,0},{6,2},{8,12},{10,14},{12,8},{14,10},{16,20},{18,... | collective-permute-start | bytes 393224 | tf_op jit(solution)/shard_map/ppermute | solution.py:36
  109.4 7.5 %collective-permute-done.30.refs_8_ = bf16[64,1024]{1,0:T(8,128)(2,1)S(1)} collective-permute-done((bf16[64,1024]{1,0:T(8,128)(2,1)S(1)}, bf16[64,1024]{1,0:T(8,128)(2,1)S(1)}, u32[]{:S(2)}, u32[]{:S(2)}) %collective-permute-start.30) | collective-permute-done | bytes 131104 | tf_op jit(solution)/shard_map/ppermute | solution.py:36
  117.0 1.5 %collective-permute-start.32 = (bf16[64,1024]{1,0:T(8,128)(2,1)S(1)}, bf16[64,1024]{1,0:T(8,128)(2,1)S(1)}, u32[]{:S(2)}, u32[]{:S(2)}) collective-permute-start(bf16[64,1024]{1,0:T(8,128)(2,1)S(1)} %collective-permute-done.30.refs_8_), channel_id=1, source_target_pairs={{0,4},{2,6},{4,0},{6,2},{8,12},{10,14},{12,8},{14,10},{16,20},{18,... | collective-permute-start | bytes 393224 | tf_op jit(solution)/shard_map/ppermute | solution.py:36
  119.6 3.4 %collective-permute-done.32.refs_10_ = bf16[64,1024]{1,0:T(8,128)(2,1)S(1)} collective-permute-done((bf16[64,1024]{1,0:T(8,128)(2,1)S(1)}, bf16[64,1024]{1,0:T(8,128)(2,1)S(1)}, u32[]{:S(2)}, u32[]{:S(2)}) %collective-permute-start.32) | collective-permute-done | bytes 131104 | tf_op jit(solution)/shard_map/ppermute | solution.py:36
  123.0 1.4 %collective-permute-done.36.refs_14_ = bf16[64,1024]{1,0:T(8,128)(2,1)S(1)} collective-permute-done((bf16[64,1024]{1,0:T(8,128)(2,1)S(1)}, bf16[64,1024]{1,0:T(8,128)(2,1)S(1)}, u32[]{:S(2)}, u32[]{:S(2)}) %collective-permute-start.36) | collective-permute-done | bytes 131104 | tf_op jit(solution)/shard_map/ppermute | solution.py:36
  124.4 1.3 collective-permute-done.37.refs_15_
  126.5 1.5 %collective-permute-start.38 = (bf16[256,256]{1,0:T(8,128)(2,1)S(1)}, bf16[256,256]{1,0:T(8,128)(2,1)S(1)}, u32[]{:S(2)}, u32[]{:S(2)}) collective-permute-start(bf16[256,256]{1,0:T(8,128)(2,1)S(1)} %output.3), channel_id=1, source_target_pairs={{0,1},{1,0},{2,3},{3,2},{4,5},{5,4},{6,7},{7,6},{8,9},{9,8},{10,11... | collective-permute-start | bytes 393224 | tf_op jit(solution)/shard_map/ppermute | solution.py:372
  128.7 3.4 %collective-permute-done.38 = bf16[256,256]{1,0:T(8,128)(2,1)S(1)} collective-permute-done((bf16[256,256]{1,0:T(8,128)(2,1)S(1)}, bf16[256,256]{1,0:T(8,128)(2,1)S(1)}, u32[]{:S(2)}, u32[]{:S(2)}) %collective-permute-start.38) | collective-permute-done | bytes 131104 | tf_op jit(solution)/shard_map/ppermute | solution.py:372
  (104 shorter events, 14.4 us)
Async XLA Ops:
  8.5 14.5 %collective-permute-start = (f32[4,64,1280]{2,1,0:T(8,128)}, f32[4,64,1280]{2,1,0:T(8,128)}, u32[]{:S(2)}, u32[]{:S(2)}) collective-permute-start(f32[4,64,1280]{2,1,0:T(8,128)} %get-tuple-element.27), channel_id=1, source_target_pairs={{0,2},{2,0},{4,6},{6,4},{8,10},{10,8},{12,14},{14,12},{16,18},{18,... | collective-permute-start | bytes 3932168 | tf_op jit(solution)/shard_map/ppermute | solution.py:36
  9.0 14.0 %collective-permute-start.1 = (f32[4,64,1280]{2,1,0:T(8,128)}, f32[4,64,1280]{2,1,0:T(8,128)}, u32[]{:S(2)}, u32[]{:S(2)}) collective-permute-start(f32[4,64,1280]{2,1,0:T(8,128)} %get-tuple-element.28), channel_id=1, source_target_pairs={{0,2},{2,0},{4,6},{6,4},{8,10},{10,8},{12,14},{14,12},{16,18},{18,... | collective-permute-start | bytes 3932168 | tf_op jit(solution)/shard_map/ppermute | solution.py:36
  11.6 46.7 %collective-permute-start.7 = (bf16[2,512,128]{2,1,0:T(8,128)(2,1)}, bf16[2,512,128]{2,1,0:T(8,128)(2,1)S(1)}, u32[]{:S(2)}, u32[]{:S(2)}) collective-permute-start(bf16[2,512,128]{2,1,0:T(8,128)(2,1)} %get-tuple-element.34.refs_0_), channel_id=1, source_target_pairs={{0,2},{2,0},{4,6},{6,4},{8,10},{10,8},{12,14},{14,12},{16,18},{18,... | collective-permute-start | bytes 786440 | tf_op jit(solution)/shard_map/ppermute | solution.py:36
  14.3 57.8 %collective-permute-start.8 = (bf16[2,512,128]{2,1,0:T(8,128)(2,1)}, bf16[2,512,128]{2,1,0:T(8,128)(2,1)S(1)}, u32[]{:S(2)}, u32[]{:S(2)}) collective-permute-start(bf16[2,512,128]{2,1,0:T(8,128)(2,1)} %get-tuple-element.35), channel_id=1, source_target_pairs={{0,20},{2,22},{4,16},{6,18},{8,28},{10,30},{12,24},{14,26},{16,4},... | collective-permute-start | bytes 786440 | tf_op jit(solution)/shard_map/ppermute | solution.py:36
  18.9 53.3 %collective-permute-start.10 = (bf16[2,512,128]{2,1,0:T(8,128)(2,1)}, bf16[2,512,128]{2,1,0:T(8,128)(2,1)S(1)}, u32[]{:S(2)}, u32[]{:S(2)}) collective-permute-start(bf16[2,512,128]{2,1,0:T(8,128)(2,1)} %get-tuple-element.36), channel_id=1, source_target_pairs={{0,12},{2,14},{4,8},{6,10},{8,4},{10,6},{12,0},{14,2},{16,28},{18,... | collective-permute-start | bytes 786440 | tf_op jit(solution)/shard_map/ppermute | solution.py:36
  25.2 14.9 %collective-permute-start.2 = (f16[2,64,1280]{2,1,0:T(8,128)(2,1)S(1)}, f16[2,64,1280]{2,1,0:T(8,128)(2,1)S(1)}, u32[]{:S(2)}, u32[]{:S(2)}) collective-permute-start(f16[2,64,1280]{2,1,0:T(8,128)(2,1)S(1)} %get-tuple-element.52), channel_id=1, source_target_pairs={{0,4},{2,6},{4,0},{6,2},{8,12},{10,14},{12,8},{14,10},{16,20},{18,... | collective-permute-start | bytes 983048 | tf_op jit(solution)/shard_map/ppermute | solution.py:36
  26.9 20.1 %collective-permute-start.4 = (f16[2,64,1280]{2,1,0:T(8,128)(2,1)S(1)}, f16[2,64,1280]{2,1,0:T(8,128)(2,1)S(1)}, u32[]{:S(2)}, u32[]{:S(2)}) collective-permute-start(f16[2,64,1280]{2,1,0:T(8,128)(2,1)S(1)} %get-tuple-element.51), channel_id=1, source_target_pairs={{0,4},{2,6},{4,0},{6,2},{8,12},{10,14},{12,8},{14,10},{16,20},{18,... | collective-permute-start | bytes 983048 | tf_op jit(solution)/shard_map/ppermute | solution.py:36
  40.2 7.2 %collective-permute-start.3 = (f16[1,64,1280]{2,1,0:T(8,128)(2,1)S(1)}, f16[1,64,1280]{2,1,0:T(8,128)(2,1)S(1)}, u32[]{:S(2)}, u32[]{:S(2)}) collective-permute-start(f16[1,64,1280]{2,1,0:T(8,128)(2,1)S(1)} %get-tuple-element.56), channel_id=1, source_target_pairs={{0,8},{2,10},{4,12},{6,14},{8,0},{10,2},{12,4},{14,6},{16,24},{18,... | collective-permute-start | bytes 491528 | tf_op jit(solution)/shard_map/ppermute | solution.py:36
  47.0 9.3 %collective-permute-start.6 = (f16[1,64,1280]{2,1,0:T(8,128)(2,1)S(1)}, f16[1,64,1280]{2,1,0:T(8,128)(2,1)S(1)}, u32[]{:S(2)}, u32[]{:S(2)}) collective-permute-start(f16[1,64,1280]{2,1,0:T(8,128)(2,1)S(1)} %get-tuple-element.55), channel_id=1, source_target_pairs={{0,8},{2,10},{4,12},{6,14},{8,0},{10,2},{12,4},{14,6},{16,24},{18,... | collective-permute-start | bytes 491528 | tf_op jit(solution)/shard_map/ppermute | solution.py:36
  47.6 10.6 %collective-permute-start.5 = (f16[1,64,1280]{2,1,0:T(8,128)(2,1)S(1)}, f16[1,64,1280]{2,1,0:T(8,128)(2,1)S(1)}, u32[]{:S(2)}, u32[]{:S(2)}) collective-permute-start(f16[1,64,1280]{2,1,0:T(8,128)(2,1)S(1)} %fusion.7), channel_id=1, source_target_pairs={{0,16},{2,18},{4,20},{6,22},{8,24},{10,26},{12,28},{14,30},{16,0},... | collective-permute-start | bytes 491528 | tf_op jit(solution)/shard_map/ppermute | solution.py:36
  56.3 16.7 %collective-permute-start.12 = (bf16[2,512,128]{2,1,0:T(8,128)(2,1)S(1)}, bf16[2,512,128]{2,1,0:T(8,128)(2,1)S(1)}, u32[]{:S(2)}, u32[]{:S(2)}) collective-permute-start(bf16[2,512,128]{2,1,0:T(8,128)(2,1)S(1)} %copy-done.11), channel_id=1, source_target_pairs={{0,24},{2,26},{4,28},{6,30},{8,16},{10,18},{12,20},{14,22},{16,8},... | collective-permute-start | bytes 786440 | tf_op jit(solution)/shard_map/ppermute | solution.py:36
  58.2 28.7 %collective-permute-start.14 = (bf16[2,512,128]{2,1,0:T(8,128)(2,1)S(1)}, bf16[2,512,128]{2,1,0:T(8,128)(2,1)S(1)}, u32[]{:S(2)}, u32[]{:S(2)}) collective-permute-start(bf16[2,512,128]{2,1,0:T(8,128)(2,1)S(1)} %copy-done.10), channel_id=1, source_target_pairs={{0,16},{2,18},{4,20},{6,22},{8,24},{10,26},{12,28},{14,30},{16,0},... | collective-permute-start | bytes 786440 | tf_op jit(solution)/shard_map/ppermute | solution.py:36
  58.3 28.7 %collective-permute-start.16 = (bf16[2,512,128]{2,1,0:T(8,128)(2,1)S(1)}, bf16[2,512,128]{2,1,0:T(8,128)(2,1)S(1)}, u32[]{:S(2)}, u32[]{:S(2)}) collective-permute-start(bf16[2,512,128]{2,1,0:T(8,128)(2,1)S(1)} %copy-done.9), channel_id=1, source_target_pairs={{0,8},{2,10},{4,12},{6,14},{8,0},{10,2},{12,4},{14,6},{16,24},{18,... | collective-permute-start | bytes 786440 | tf_op jit(solution)/shard_map/ppermute | solution.py:36
  72.1 15.6 %collective-permute-start.18 = (bf16[2,512,128]{2,1,0:T(8,128)(2,1)S(1)}, bf16[2,512,128]{2,1,0:T(8,128)(2,1)S(1)}, u32[]{:S(2)}, u32[]{:S(2)}) collective-permute-start(bf16[2,512,128]{2,1,0:T(8,128)(2,1)S(1)} %copy-done.8), channel_id=1, source_target_pairs={{0,4},{2,6},{4,0},{6,2},{8,12},{10,14},{12,8},{14,10},{16,20},{18,... | collective-permute-start | bytes 786440 | tf_op jit(solution)/shard_map/ppermute | solution.py:36
  72.3 15.5 %collective-permute-start.20 = (bf16[2,512,128]{2,1,0:T(8,128)(2,1)S(1)}, bf16[2,512,128]{2,1,0:T(8,128)(2,1)S(1)}, u32[]{:S(2)}, u32[]{:S(2)}) collective-permute-start(bf16[2,512,128]{2,1,0:T(8,128)(2,1)S(1)} %copy-done.7), channel_id=1, source_target_pairs={{0,28},{2,30},{4,24},{6,26},{8,20},{10,22},{12,16},{14,18},{16,12}... | collective-permute-start | bytes 786440 | tf_op jit(solution)/shard_map/ppermute | solution.py:36
  73.1 15.2 %collective-permute-start.9 = (bf16[2,512,128]{2,1,0:T(8,128)(2,1)S(1)}, bf16[2,512,128]{2,1,0:T(8,128)(2,1)S(1)}, u32[]{:S(2)}, u32[]{:S(2)}) collective-permute-start(bf16[2,512,128]{2,1,0:T(8,128)(2,1)S(1)} %collective-permute-done.8.refs_2_), channel_id=1, source_target_pairs={{0,2},{2,0},{4,6},{6,4},{8,10},{10,8},{12,14},{14,12},{16,18},{18,... | collective-permute-start | bytes 786440 | tf_op jit(solution)/shard_map/ppermute | solution.py:36
  88.5 8.5 %collective-permute-start.21 = (bf16[2,512,128]{2,1,0:T(8,128)(2,1)S(1)}, bf16[2,512,128]{2,1,0:T(8,128)(2,1)S(1)}, u32[]{:S(2)}, u32[]{:S(2)}) collective-permute-start(bf16[2,512,128]{2,1,0:T(8,128)(2,1)S(1)} %collective-permute-done.20.refs_0_), channel_id=1, source_target_pairs={{0,2},{2,0},{4,6},{6,4},{8,10},{10,8},{12,14},{14,12},{16,18},{18,... | collective-permute-start | bytes 786440 | tf_op jit(solution)/shard_map/ppermute | solution.py:36
  88.9 8.2 %collective-permute-start.22 = (bf16[2,64,128]{2,1,0:T(8,128)(2,1)S(1)}, bf16[2,64,128]{2,1,0:T(8,128)(2,1)S(1)}, u32[]{:S(2)}, u32[]{:S(2)}) collective-permute-start(bf16[2,64,128]{2,1,0:T(8,128)(2,1)S(1)} %pad_maximum_fusion.2.refs_2_), channel_id=1, source_target_pairs={{0,2},{2,0},{4,6},{6,4},{8,10},{10,8},{12,14},{14,12},{16,18},{18,... | collective-permute-start | bytes 98312 | tf_op jit(solution)/shard_map/ppermute | solution.py:36
  98.4 8.2 %collective-permute-start.24 = (bf16[64,1024]{1,0:T(8,128)(2,1)S(1)}, bf16[64,1024]{1,0:T(8,128)(2,1)S(1)}, u32[]{:S(2)}, u32[]{:S(2)}) collective-permute-start(bf16[64,1024]{1,0:T(8,128)(2,1)S(1)} %last.1.refs_0_), channel_id=1, source_target_pairs={{0,4},{2,6},{4,0},{6,2},{8,12},{10,14},{12,8},{14,10},{16,20},{18,... | collective-permute-start | bytes 393224 | tf_op jit(solution)/shard_map/ppermute | solution.py:36
  99.6 8.4 %collective-permute-start.26 = (bf16[64,1024]{1,0:T(8,128)(2,1)S(1)}, bf16[64,1024]{1,0:T(8,128)(2,1)S(1)}, u32[]{:S(2)}, u32[]{:S(2)}) collective-permute-start(bf16[64,1024]{1,0:T(8,128)(2,1)S(1)} %last.1.refs_0_), channel_id=1, source_target_pairs={{0,8},{2,10},{4,12},{6,14},{8,0},{10,2},{12,4},{14,6},{16,24},{18,... | collective-permute-start | bytes 393224 | tf_op jit(solution)/shard_map/ppermute | solution.py:36
  104.1 3.8 %collective-permute-start.23 = (bf16[64,1024]{1,0:T(8,128)(2,1)S(1)}, bf16[64,1024]{1,0:T(8,128)(2,1)S(1)}, u32[]{:S(2)}, u32[]{:S(2)}) collective-permute-start(bf16[64,1024]{1,0:T(8,128)(2,1)S(1)} %last.1.refs_0_), channel_id=1, source_target_pairs={{0,2},{2,0},{4,6},{6,4},{8,10},{10,8},{12,14},{14,12},{16,18},{18,... | collective-permute-start | bytes 393224 | tf_op jit(solution)/shard_map/ppermute | solution.py:36
  104.1 12.9 %collective-permute-start.30 = (bf16[64,1024]{1,0:T(8,128)(2,1)S(1)}, bf16[64,1024]{1,0:T(8,128)(2,1)S(1)}, u32[]{:S(2)}, u32[]{:S(2)}) collective-permute-start(bf16[64,1024]{1,0:T(8,128)(2,1)S(1)} %last.1.refs_0_), channel_id=1, source_target_pairs={{0,16},{2,18},{4,20},{6,22},{8,24},{10,26},{12,28},{14,30},{16,0},... | collective-permute-start | bytes 393224 | tf_op jit(solution)/shard_map/ppermute | solution.py:36
  105.1 13.3 %collective-permute-start.34 = (bf16[64,1024]{1,0:T(8,128)(2,1)S(1)}, bf16[64,1024]{1,0:T(8,128)(2,1)S(1)}, u32[]{:S(2)}, u32[]{:S(2)}) collective-permute-start(bf16[64,1024]{1,0:T(8,128)(2,1)S(1)} %last.1.refs_0_), channel_id=1, source_target_pairs={{0,24},{2,26},{4,28},{6,30},{8,16},{10,18},{12,20},{14,22},{16,8},... | collective-permute-start | bytes 393224 | tf_op jit(solution)/shard_map/ppermute | solution.py:36
  106.6 12.4 %collective-permute-start.25 = (bf16[64,1024]{1,0:T(8,128)(2,1)S(1)}, bf16[64,1024]{1,0:T(8,128)(2,1)S(1)}, u32[]{:S(2)}, u32[]{:S(2)}) collective-permute-start(bf16[64,1024]{1,0:T(8,128)(2,1)S(1)} %collective-permute-done.24.refs_2_), channel_id=1, source_target_pairs={{0,2},{2,0},{4,6},{6,4},{8,10},{10,8},{12,14},{14,12},{16,18},{18,... | collective-permute-start | bytes 393224 | tf_op jit(solution)/shard_map/ppermute | solution.py:36
  107.9 11.1 %collective-permute-start.27 = (bf16[64,1024]{1,0:T(8,128)(2,1)S(1)}, bf16[64,1024]{1,0:T(8,128)(2,1)S(1)}, u32[]{:S(2)}, u32[]{:S(2)}) collective-permute-start(bf16[64,1024]{1,0:T(8,128)(2,1)S(1)} %collective-permute-done.26.refs_4_), channel_id=1, source_target_pairs={{0,2},{2,0},{4,6},{6,4},{8,10},{10,8},{12,14},{14,12},{16,18},{18,... | collective-permute-start | bytes 393224 | tf_op jit(solution)/shard_map/ppermute | solution.py:36
  107.9 11.6 %collective-permute-start.28 = (bf16[64,1024]{1,0:T(8,128)(2,1)S(1)}, bf16[64,1024]{1,0:T(8,128)(2,1)S(1)}, u32[]{:S(2)}, u32[]{:S(2)}) collective-permute-start(bf16[64,1024]{1,0:T(8,128)(2,1)S(1)} %collective-permute-done.26.refs_4_), channel_id=1, source_target_pairs={{0,4},{2,6},{4,0},{6,2},{8,12},{10,14},{12,8},{14,10},{16,20},{18,... | collective-permute-start | bytes 393224 | tf_op jit(solution)/shard_map/ppermute | solution.py:36
  117.0 6.0 %collective-permute-start.32 = (bf16[64,1024]{1,0:T(8,128)(2,1)S(1)}, bf16[64,1024]{1,0:T(8,128)(2,1)S(1)}, u32[]{:S(2)}, u32[]{:S(2)}) collective-permute-start(bf16[64,1024]{1,0:T(8,128)(2,1)S(1)} %collective-permute-done.30.refs_8_), channel_id=1, source_target_pairs={{0,4},{2,6},{4,0},{6,2},{8,12},{10,14},{12,8},{14,10},{16,20},{18,... | collective-permute-start | bytes 393224 | tf_op jit(solution)/shard_map/ppermute | solution.py:36
  118.4 5.9 %collective-permute-start.36 = (bf16[64,1024]{1,0:T(8,128)(2,1)S(1)}, bf16[64,1024]{1,0:T(8,128)(2,1)S(1)}, u32[]{:S(2)}, u32[]{:S(2)}) collective-permute-start(bf16[64,1024]{1,0:T(8,128)(2,1)S(1)} %collective-permute-done.34.refs_12_), channel_id=1, source_target_pairs={{0,4},{2,6},{4,0},{6,2},{8,12},{10,14},{12,8},{14,10},{16,20},{18,... | collective-permute-start | bytes 393224 | tf_op jit(solution)/shard_map/ppermute | solution.py:36
  119.0 5.4 %collective-permute-start.31 = (bf16[64,1024]{1,0:T(8,128)(2,1)S(1)}, bf16[64,1024]{1,0:T(8,128)(2,1)S(1)}, u32[]{:S(2)}, u32[]{:S(2)}) collective-permute-start(bf16[64,1024]{1,0:T(8,128)(2,1)S(1)} %collective-permute-done.30.refs_8_), channel_id=1, source_target_pairs={{0,2},{2,0},{4,6},{6,4},{8,10},{10,8},{12,14},{14,12},{16,18},{18,... | collective-permute-start | bytes 393224 | tf_op jit(solution)/shard_map/ppermute | solution.py:36
  119.0 5.4 %collective-permute-start.35 = (bf16[64,1024]{1,0:T(8,128)(2,1)S(1)}, bf16[64,1024]{1,0:T(8,128)(2,1)S(1)}, u32[]{:S(2)}, u32[]{:S(2)}) collective-permute-start(bf16[64,1024]{1,0:T(8,128)(2,1)S(1)} %collective-permute-done.34.refs_12_), channel_id=1, source_target_pairs={{0,2},{2,0},{4,6},{6,4},{8,10},{10,8},{12,14},{14,12},{16,18},{18,... | collective-permute-start | bytes 393224 | tf_op jit(solution)/shard_map/ppermute | solution.py:36
  119.5 4.9 %collective-permute-start.29 = (bf16[64,1024]{1,0:T(8,128)(2,1)S(1)}, bf16[64,1024]{1,0:T(8,128)(2,1)S(1)}, u32[]{:S(2)}, u32[]{:S(2)}) collective-permute-start(bf16[64,1024]{1,0:T(8,128)(2,1)S(1)} %collective-permute-done.28.refs_6_), channel_id=1, source_target_pairs={{0,2},{2,0},{4,6},{6,4},{8,10},{10,8},{12,14},{14,12},{16,18},{18,... | collective-permute-start | bytes 393224 | tf_op jit(solution)/shard_map/ppermute | solution.py:36
  126.5 5.6 %collective-permute-start.38 = (bf16[256,256]{1,0:T(8,128)(2,1)S(1)}, bf16[256,256]{1,0:T(8,128)(2,1)S(1)}, u32[]{:S(2)}, u32[]{:S(2)}) collective-permute-start(bf16[256,256]{1,0:T(8,128)(2,1)S(1)} %output.3), channel_id=1, source_target_pairs={{0,1},{1,0},{2,3},{3,2},{4,5},{5,4},{6,7},{7,6},{8,9},{9,8},{10,11... | collective-permute-start | bytes 393224 | tf_op jit(solution)/shard_map/ppermute | solution.py:372
  (20 other events, 222.2 us)
